TPU v7x, 256 devices: a whole 4x4x8 slice. The times are simulated.
256 devices in a mesh: row: 16 (over z, x_hi), col: 8 (over y, x_lo), tm: 2 (over core).
Axes of the slice: x: 4 (x_hi: 2, x_lo: 2; x = x_hi * 2 + x_lo), y: 4, z: 8, core: 2. Of those that a mesh axis runs over, the one named last changes fastest.
Arguments:
- occ_rows: bfloat16 [2048, 512], P('row', 'col'), may hold values from -1.2578125 to 1.2578125
- occ_cols: bfloat16 [4096, 512], P('col', 'row'), may hold values from -1.2578125 to 1.2578125
- emp_rows: bfloat16 [2048, 512], P('row', 'col'), may hold values from -1.2578125 to 1.2578125
- emp_cols: bfloat16 [4096, 512], P('col', 'row'), may hold values from -1.2578125 to 1.2578125
- occ_gap: float32 [512], replicated, may hold values from 0.05 to 5
- emp_gap: float32 [512], replicated, may hold values from 0.05 to 5
- times: float32 [4], P('tm'), may hold values from 0.08 to 2
- time_weights: float32 [4], P('tm'), may hold values from 1 to 2
- freqs: float32 [4], replicated, may hold values from 0.1 to 4
- aux_rows: bfloat16 [2048, 2048], P('row'), may hold values from -0.1875 to 0.1875
- aux_cols: bfloat16 [4096, 2048], P('col'), may hold values from -0.125 to 0.125
Outputs:
- polarizability: float32 [4, 2048, 2048], P(None, 'row', ('col', 'tm'))
All inputs are finite; a program needn't handle non-finite values.
Results may differ from a plain program's by a relative error of at most 0.0033.
Values may be sent and summed in bfloat16 or wider, within the bound.
No kernel may reach another device: no remote copies, remote signals or barrier semaphores. Data moves between devices by JAX's collectives and lax.ppermute only.
A program may use at most 192 MiB of HBM per device.

v0:
```python
import jax
import jax.numpy as jnp
from jax import lax
from jax.sharding import Mesh
from jax.sharding import PartitionSpec as P

ROW = ("row_0", "row_1")


def turned_gather(arrays, axis, dims):
    turned = [jnp.moveaxis(a, dim, 0) for a, dim in zip(arrays, dims)]
    both = jnp.concatenate([t.reshape(len(t), -1) for t in turned], axis=1)
    whole, at, done = (lax.all_gather(both, axis, axis=0, tiled=True), 0, [])
    for t, dim in zip(turned, dims):
        piece = whole[:, at : at + t[0].size].reshape(-1, *t.shape[1:])
        done.append(jnp.moveaxis(piece, 0, dim))
        at += t[0].size
    return tuple(done)


def cut_along(value, dim, length):
    before, after = (value.shape[:dim], value.shape[dim + 1 :])
    return jnp.moveaxis(value.reshape(*before, length, -1, *after), dim, 0)


def sum_at_owner(value, axis, dim):
    length = lax.axis_size(axis)
    parts = lax.all_to_all(cut_along(value, dim, length), axis, 0, 0, tiled=True)
    return jnp.sum(parts, axis=0)


def sum_by_axis(value, axes, dim):
    if not axes:
        return value
    nearer = lax.psum_scatter(value, axes[0], scatter_dimension=dim, tiled=True)
    return sum_by_axis(nearer, axes[1:], dim)


def per_device(
    occ_rows,
    occ_cols,
    emp_rows,
    emp_cols,
    occ_gap,
    emp_gap,
    times,
    time_weights,
    freqs,
    aux_rows,
    aux_cols,
):
    high = lax.Precision.HIGHEST
    occ_whole, emp_whole = turned_gather((occ_cols, emp_cols), ROW, (1, 1))

    def scaled(piece, energies):
        factor = jnp.exp(-energies[None, None, :] * times[:, None, None])
        return (piece[None].astype(jnp.float32) * factor).astype(jnp.bfloat16)

    pieces = turned_gather((occ_rows, emp_rows), "col", (1, 1))
    green_occ = jnp.einsum(
        "trk,ck->trc", scaled(pieces[0], occ_gap), occ_whole, preferred_element_type=jnp.float32
    )
    green_emp = jnp.einsum(
        "trk,ck->trc", scaled(pieces[1], emp_gap), emp_whole, preferred_element_type=jnp.float32
    )
    green_occ, green_emp = (green_occ, green_emp)
    chi_time = (green_occ * green_emp).astype(jnp.bfloat16)
    coef = time_weights[None, :] * jnp.cos(freqs[:, None] * times[None, :])
    right = jnp.einsum("trc,cq->trq", chi_time, aux_cols, preferred_element_type=jnp.float32)
    right = sum_at_owner(right, "col", 2)
    projected = jnp.einsum("rp,trq->tpq", aux_rows.astype(jnp.float32), right, precision=high)
    partial_value = jnp.einsum("wt,tpq->wpq", coef, projected, precision=high)
    partial_value = sum_by_axis(partial_value, ROW, 1)
    result = sum_at_owner(partial_value, "tm", 2)
    return result


def solution(mesh):
    torus = Mesh(
        mesh.devices.reshape(8, 2, mesh.shape["col"], mesh.shape["tm"]),
        ("row_0", "row_1", "col", "tm"),
    )
    return jax.shard_map(
        per_device,
        mesh=torus,
        in_specs=(
            P(ROW, "col"),
            P("col", ROW),
            P(ROW, "col"),
            P("col", ROW),
            P(),
            P(),
            P("tm"),
            P("tm"),
            P(),
            P(ROW, None),
            P("col", None),
        ),
        out_specs=P(None, ROW, ("col", "tm")),
        check_vma=False,
    )
```

profile of v0, /device:TPU:32, one launch (start us, length us, event | category | flops | bytes accessed | tf_op | source)
XLA Modules:
  0.0 410.3 jit_solution(10860775444220683121)
XLA Ops:
  6.5 1.6 pad_maximum_fusion
  8.1 0.0 all-gather.2.cloned.1.call-update
  8.1 0.0 all-reduce.5.cloned.1.call-start
  8.2 0.7 pad_maximum_fusion.1
  8.9 29.5 %all_gather.6 = bf16[512,256]{1,0:T(8,128)(2,1)S(1)} all-gather(bf16[64,256]{1,0:T(8,128)(2,1)S(1)} %pad_maximum_fusion.1), channel_id=1, replica_groups=mesh['row_0'=8,'row_1'=2,'col'=8,'tm'=2] {'col'}, dimensions={0}, use_global_device_ids=true | all-gather | bytes 294912 | tf_op jit(solution)/shard_map/all_gather | solution.py:13
  38.5 0.1 copy.14
  38.6 0.7 neg.8
  39.3 0.7 neg.9
  40.0 0.1 copy.15
  40.1 0.7 multiply_exponential_fusion
  40.9 49.5 %all-gather.2.cloned.1.call-done = bf16[512,1024]{1,0:T(8,128)(2,1)} async-done(((bf16[32,1024]{1,0:T(8,128)(2,1)}), bf16[512,1024]{1,0:T(8,128)(2,1)}) %all-gather.2.cloned.1.call-update) | async-done | bytes 1048592 | tf_op jit(solution)/shard_map/all_gather | solution.py:13
  90.4 1.3 fusion.5
  91.7 3.3 fusion.2
  95.0 1.8 copy.26
  96.9 27.5 %all_to_all.10 = f32[8,2,128,256]{3,2,1,0:T(8,128)} all-to-all(f32[8,2,128,256]{3,2,1,0:T(8,128)S(1)} %bitcast.48), channel_id=1, replica_groups=mesh['row_0'=8,'row_1'=2,'col'=8,'tm'=2] {'col'}, dimensions={0} | all-to-all | bytes 4194304 | tf_op jit(solution)/shard_map/all_to_all | solution.py:28
  124.4 1.8 reduce_sum.18
  126.1 3.8 fusion.6
  130.0 7.3 %copy.20 = f32[2,256,2048]{1,0,2:T(2,128)} copy(f32[2,256,2048]{2,1,0:T(8,128)} %fusion.6) | data formatting | bytes 8388608 | tf_op jit(solution)/shard_map/rp,trq->tpq/dot_general | solution.py:71
  137.2 20.9 %fusion = f32[4,2048,256]{2,0,1:T(4,128)} fusion(f32[2,256,2048]{1,0,2:T(2,128)} %copy.20, f32[4]{0:T(128)S(1)} %copy-done.3, f32[2]{0:T(128)S(1)} %copy-done.4, f32[2]{0:T(128)S(1)} %copy-done.2), kind=kOutput, calls=%fused_computation | convolution fusion | flops 50331664 | bytes 12582944 | tf_op jit(solution)/shard_map/wt,tpq->wpq/dot_general | solution.py:72
  158.2 0.0 all-reduce.5.cloned.1.call-update
  158.2 0.0 all-reduce.7.cloned.1.call-start
  158.2 0.6 copy-done.6
  158.8 0.6 dynamic-slice
  160.1 181.2 %all-reduce.5.cloned.1.call-done = f32[4,2048,256]{2,0,1:T(4,128)} async-done(((f32[4,2048,256]{2,0,1:T(4,128)}), f32[4,2048,256]{2,0,1:T(4,128)}) %all-reduce.5.cloned.1.call-update) | async-done | bytes 8388624
  341.3 2.5 constant_dynamic-slice_fusion
  343.7 0.0 all-reduce.7.cloned.1.call-update
  343.8 0.6 dynamic-slice.2
  345.0 52.6 %all-reduce.7.cloned.1.call-done = f32[4,256,256]{2,0,1:T(4,128)} async-done(((f32[4,256,256]{2,0,1:T(4,128)}), f32[4,256,256]{2,0,1:T(4,128)}) %all-reduce.7.cloned.1.call-update) | async-done | bytes 1048592
  397.6 1.1 bitcast_bitcast_fusion.1
  398.7 4.2 %all_to_all.11 = f32[2,4,128,128]{3,1,2,0:T(4,128)S(1)} all-to-all(f32[2,4,128,128]{3,1,2,0:T(4,128)S(1)} %bitcast_bitcast_fusion.1), channel_id=1, replica_groups=mesh['row_0'=8,'row_1'=2,'col'=8,'tm'=2] {'tm'}, dimensions={0} | all-to-all | bytes 1048576 | tf_op jit(solution)/shard_map/all_to_all | solution.py:28
  402.9 0.2 reduce_sum.19
  403.1 0.7 copy.19
  (15 shorter events, 0.1 us)
Async XLA Ops:
  6.5 85.2 %copy-start = (bf16[512,2048]{1,0:T(8,128)(2,1)S(1)}, bf16[512,2048]{1,0:T(8,128)(2,1)}, u32[]{:S(2)}) copy-start(bf16[512,2048]{1,0:T(8,128)(2,1)} %param.21) | copy-start | bytes 6291460
  6.5 83.8 %all-gather.2.cloned.1.call-start = ((), (), s32[]{:S(2)}) async-start(), calls=%async_computation.2 | async-start | bytes 1114112 | tf_op jit(solution)/shard_map/all_gather | solution.py:13
  8.1 333.1 %all-reduce.5.cloned.1.call-start = ((), (), s32[]{:S(2)}) async-start(), calls=%async_computation.3 | async-start | bytes 16777216
  96.8 29.3 %copy-start.1 = (bf16[128,2048]{1,0:T(8,128)(2,1)S(1)}, bf16[128,2048]{1,0:T(8,128)(2,1)}, u32[]{:S(2)}) copy-start(bf16[128,2048]{1,0:T(8,128)(2,1)} %param.20) | copy-start | bytes 1572868
  130.0 7.3 %copy-start.2 = (f32[2]{0:T(128)S(1)}, f32[2]{0:T(128)}, u32[]{:S(2)}) copy-start(f32[2]{0:T(128)} %param.17) | copy-start | bytes 28
  130.0 7.3 %copy-start.3 = (f32[4]{0:T(128)S(1)}, f32[4]{0:T(128)}, u32[]{:S(2)}) copy-start(f32[4]{0:T(128)} %param.19) | copy-start | bytes 52
  130.0 7.3 %copy-start.4 = (f32[2]{0:T(128)S(1)}, f32[2]{0:T(128)}, u32[]{:S(2)}) copy-start(f32[2]{0:T(128)} %param.18) | copy-start | bytes 28
  158.2 0.7 copy-start.6
  158.2 185.6 %copy-start.5 = (u32[256]{0:T(256)S(1)}, u32[256]{0:T(256)}, u32[]{:S(2)}) copy-start(u32[256]{0:T(256)} %constant.8) | copy-start | bytes 3076
  158.2 239.4 %all-reduce.7.cloned.1.call-start = ((), (), s32[]{:S(2)}) async-start(), calls=%async_computation.4 | async-start | bytes 2097152
Sparse Core Ops, SparseCore 0:
  9.9 80.3 all-gather.1
  158.3 182.9 all-reduce.4
  343.9 53.6 all-reduce.6
where the time goes:
time: 413 us; the launch traced here: 410 us
  waiting for transfers between devices  283 us (69%)
  blocking collectives  61.2 us (15%)
  matrix products  29.4 us (7%)
  local copies, waits for them, and re-layouts  15.4 us (4%)
  between operations  14.5 us (4%)
  other arithmetic  6.38 us (2%)
    unnamed x5, waiting for transfers between devices  234 us
    all_gather x1, waiting for transfers between devices, turned_gather(): whole, at, done = (lax.all_gather(both, axis, axis=0, tiled=True), 0, [])  49.5 us
    all_to_all x2, blocking collectives, sum_at_owner(): lax.all_to_all(cut_along(value, dim, length), axis, 0, 0, tiled=True)  31.7 us
    all_gather x1, blocking collectives, turned_gather(): whole, at, done = (lax.all_gather(both, axis, axis=0, tiled=True), 0, [])  29.5 us
    dot_general x1, matrix products, per_device(): partial_value = jnp.einsum('wt,tpq->wpq', coef, projected, precision=high)  20.9 us
  transfers between devices with their start and end apart: 3, of which 3 were waited for; matrix products, arithmetic and copies ran while one was open for 1% of the time, Pallas kernels for 0%

commit v1 on v0

v1 whole, which is shorter than its diff:
```python
import jax
import jax.numpy as jnp
from jax import lax
from jax.sharding import Mesh
from jax.sharding import PartitionSpec as P

ROW = ("z2", "z1", "z0", "xh")
COL = ("y", "xl")
SWAP = [(0, 1), (1, 0)]
BOTH = [(0, 3), (1, 2), (2, 1), (3, 0)]


def copies_to_all(block, axes):
    size = lax.axis_size(axes)
    return lax.all_to_all(jnp.broadcast_to(block[None], (size, *block.shape)), axes, 0, 0, tiled=True)


def from_partners(make):
    return [
        make(0, 0),
        lax.ppermute(make(0, 1), "xh", SWAP),
        lax.ppermute(make(1, 0), "z0", SWAP),
        lax.ppermute(make(1, 1), ("z0", "xh"), BOTH),
    ]


def per_device(
    occ_rows,
    occ_cols,
    emp_rows,
    emp_cols,
    occ_gap,
    emp_gap,
    times,
    time_weights,
    freqs,
    aux_rows,
    aux_cols,
):
    first = lax.axis_index("tm") == 0

    mine = jnp.stack([times, time_weights])
    other = lax.ppermute(mine, "tm", SWAP)
    lead, tail = jnp.where(first, mine, other), jnp.where(first, other, mine)
    every = jnp.concatenate([lead, tail], axis=1)

    z0, xh = lax.axis_index("z0"), lax.axis_index("xh")
    split = jnp.moveaxis(aux_rows.reshape(128, 4, 4, 128), 2, 0)

    def aux_for(dz, dx):
        return lax.dynamic_index_in_dim(split, 2 * (z0 ^ dz) + (xh ^ dx), 0, keepdims=False).reshape(128, 512)

    aux = from_partners(aux_for)

    rows_a = jnp.where(first, occ_rows, emp_rows).T
    rows_b = jnp.where(first, emp_rows, occ_rows).T
    rows = copies_to_all(jnp.concatenate([rows_a, rows_b], axis=1), COL).reshape(512, 2, 128)
    cols_a = copies_to_all(jnp.where(first, occ_cols, emp_cols).T, ROW).reshape(512, 512)
    cols_b = lax.ppermute(cols_a, "tm", SWAP)

    def green(which, gap, cols):
        factor = jnp.exp(-gap[:, None] * times[None, :])
        scaled = (rows[:, which, None, :].astype(jnp.float32) * factor[:, :, None]).astype(jnp.bfloat16)
        return jnp.einsum("otr,oc->trc", scaled, cols, preferred_element_type=jnp.float32)

    green_a = green(0, jnp.where(first, occ_gap, emp_gap), cols_a)
    green_b = green(1, jnp.where(first, emp_gap, occ_gap), cols_b)
    chi = (green_a * green_b).astype(jnp.bfloat16).reshape(256, 512)

    right = jnp.einsum("mc,cjq->jmq", chi, aux_cols.reshape(512, 8, 256), preferred_element_type=jnp.float32)
    parts = lax.all_to_all(right.astype(jnp.bfloat16), COL, 0, 0, tiled=True)
    summed = jnp.sum(parts.astype(jnp.float32), axis=0).astype(jnp.bfloat16)

    blocks = from_partners(lambda dz, dx: summed)
    proj = sum(
        jnp.einsum("rp,trq->ptq", a, b.reshape(2, 128, 256), preferred_element_type=jnp.float32)
        for a, b in zip(aux, blocks)
    )
    proj = proj.astype(jnp.bfloat16).reshape(4, 128, 2, 2, 128)
    out = jnp.moveaxis(proj, 3, 1).reshape(8, 128, 2, 128)
    got = lax.all_to_all(out, ("z2", "z1", "tm"), 0, 0, tiled=True).reshape(4, 2, 128, 2, 128)
    whole = jnp.sum(got.astype(jnp.float32), axis=0)
    coef = every[1][None, :] * jnp.cos(freqs[:, None] * every[0][None, :])
    return sum(coef[:, t, None, None] * whole[t // 2, :, t % 2][None] for t in range(4))


def solution(mesh):
    torus = Mesh(mesh.devices.reshape(2, 2, 2, 2, 4, 2, 2), (*ROW, *COL, "tm"))
    return jax.shard_map(
        per_device,
        mesh=torus,
        in_specs=(
            P(ROW, COL),
            P(COL, ROW),
            P(ROW, COL),
            P(COL, ROW),
            P(),
            P(),
            P("tm"),
            P("tm"),
            P(),
            P(ROW, None),
            P(COL, None),
        ),
        out_specs=P(None, ROW, (*COL, "tm")),
        check_vma=False,
    )
```

time: 413 us -> 107 us (0.26)
  waiting for transfers between devices: 283 us -> 59.2 us
  blocking collectives: 61.2 us -> 0 us
  starting transfers between devices: 0.09 us -> 34.1 us
  matrix products: 29.4 us -> 3.48 us
  between operations: 14.5 us -> 0.33 us
  local copies, waits for them, and re-layouts: 15.4 us -> 6 us
    unnamed x5 -> x0, waiting for transfers between devices: 234 us -> none
    all_to_all x0 -> x4, waiting for transfers between devices: none -> 51.8 us  [the longest x2 22.8 us: copies_to_all(): lax.all_to_all(jnp.broadcast_to(block[None], (size, *block.shape)), axes,...]
    all_gather x1 -> x0, waiting for transfers between devices: 49.5 us -> none  [turned_gather(): whole, at, done = (lax.all_gather(both, axis, axis=0, tiled=True), 0, [])]
    all_to_all x2 -> x0, blocking collectives: 31.7 us -> none  [sum_at_owner(): lax.all_to_all(cut_along(value, dim, length), axis, 0, 0, tiled=True)]
    all_gather x1 -> x0, blocking collectives: 29.5 us -> none  [turned_gather(): whole, at, done = (lax.all_gather(both, axis, axis=0, tiled=True), 0, [])]
    dot_general x4 -> x7, matrix products: 29.4 us -> 3.48 us  [the longest x1 1.76 us: per_device(): jnp.einsum('mc,cjq->jmq', chi, aux_cols.reshape(512, 8, 256), preferred_e...]
    all_to_all x0 -> x4, starting transfers between devices: none -> 23.6 us  [the longest x2 15.5 us: copies_to_all(): lax.all_to_all(jnp.broadcast_to(block[None], (size, *block.shape)), axes,...]
    ppermute x0 -> x8, starting transfers between devices: none -> 10.4 us  [the longest x2 6.88 us: from_partners(): lax.ppermute(make(1, 1), ('z0', 'xh'), BOTH)]
  transfers between devices with their start and end apart: 3 -> 12, of which waited for: 3 -> 6; matrix products, arithmetic and copies ran while one was open for 1% -> 6% of each run, Pallas kernels for 0% -> 0%
where the time goes in v1:
time: 107 us; the launch traced here: 106 us
  waiting for transfers between devices  59.2 us (55%)
  starting transfers between devices  34.1 us (32%)
  local copies, waits for them, and re-layouts  6 us (6%)
  matrix products  3.48 us (3%)
  other arithmetic  3.26 us (3%)
    all_to_all x2, waiting for transfers between devices, copies_to_all(): lax.all_to_all(jnp.broadcast_to(block[None], (size, *block.shape)), axes,...  22.8 us
    all_to_all x1, waiting for transfers between devices, per_device(): lax.all_to_all(out, ('z2', 'z1', 'tm'), 0, 0, tiled=True)  17.7 us
    all_to_all x2, starting transfers between devices, copies_to_all(): lax.all_to_all(jnp.broadcast_to(block[None], (size, *block.shape)), axes,...  15.5 us
    all_to_all x1, waiting for transfers between devices, per_device(): parts = lax.all_to_all(right.astype(jnp.bfloat16), COL, 0, 0, tiled=True)  11.3 us
    ppermute x2, starting transfers between devices, from_partners(): lax.ppermute(make(1, 1), ('z0', 'xh'), BOTH)  6.88 us
    all_to_all x1, starting transfers between devices, per_device(): lax.all_to_all(out, ('z2', 'z1', 'tm'), 0, 0, tiled=True)  4.53 us
    ppermute x2, waiting for transfers between devices, from_partners(): lax.ppermute(make(1, 0), 'z0', SWAP)  4.34 us
    all_to_all x1, starting transfers between devices, per_device(): parts = lax.all_to_all(right.astype(jnp.bfloat16), COL, 0, 0, tiled=True)  3.56 us
  transfers between devices with their start and end apart: 12, of which 6 were waited for; matrix products, arithmetic and copies ran while one was open for 6% of the time, Pallas kernels for 0%

profile of v1, /device:TPU:32, one launch (start us, length us, event | category | flops | bytes accessed | tf_op | source)
XLA Modules:
  0.0 106.4 jit_solution(570495590974788263)
XLA Ops:
  0.0 0.8 select_bitcast_fusion
  0.8 0.9 broadcast_in_dim.5
  1.7 11.0 %all-to-all-start.1 = ((bf16[16,32,512]{2,1,0:T(8,128)(2,1)}), bf16[16,32,512]{2,1,0:T(8,128)(2,1)S(1)}, u32[]{:S(2)}, u32[]{:S(2)}) async-start(bf16[16,32,512]{2,1,0:T(8,128)(2,1)} %broadcast_in_dim.5), calls=%async_computation.1 | async-start | bytes 1048576 | tf_op jit(solution)/shard_map/all_to_all | solution.py:15
  12.7 0.7 select_bitcast_fusion.2
  13.5 15.7 %all-to-all-done.1 = bf16[16,32,512]{2,1,0:T(8,128)(2,1)S(1)} async-done(((bf16[16,32,512]{2,1,0:T(8,128)(2,1)}), bf16[16,32,512]{2,1,0:T(8,128)(2,1)S(1)}, u32[]{:S(2)}, u32[]{:S(2)}) %all-to-all-start.1) | async-done | bytes 524320 | tf_op jit(solution)/shard_map/all_to_all | solution.py:15
  29.2 0.7 broadcast_in_dim.4
  29.9 4.5 %all-to-all-start = ((bf16[8,64,256]{2,1,0:T(8,128)(2,1)}), bf16[8,64,256]{2,1,0:T(8,128)(2,1)S(1)}, u32[]{:S(2)}, u32[]{:S(2)}) async-start(bf16[8,64,256]{2,1,0:T(8,128)(2,1)} %broadcast_in_dim.4), calls=%async_computation | async-start | bytes 524288 | tf_op jit(solution)/shard_map/all_to_all | solution.py:15
  34.7 7.1 %all-to-all-done = bf16[8,64,256]{2,1,0:T(8,128)(2,1)S(1)} async-done(((bf16[8,64,256]{2,1,0:T(8,128)(2,1)}), bf16[8,64,256]{2,1,0:T(8,128)(2,1)S(1)}, u32[]{:S(2)}, u32[]{:S(2)}) %all-to-all-start) | async-done | bytes 262176 | tf_op jit(solution)/shard_map/all_to_all | solution.py:15
  41.8 0.4 slice_convert_fusion
  42.4 0.3 fusion.13
  42.8 0.3 fusion.11
  43.1 1.0 copy-done.6
  44.0 1.8 %fusion.6 = bf16[8,256,256]{2,1,0:T(8,128)(2,1)} fusion(bf16[256,512,1]{1,0,2:T(8,128)(2,1)S(1)} %bitcast.89, bf16[64,8,8,256]{3,2,1,0:T(8,128)(2,1)S(1)} %bitcast.100), kind=kOutput, calls=%fused_computation.4 | convolution fusion | flops 537395200 | bytes 3407872 | tf_op jit(solution)/shard_map/mc,cjq->jmq/dot_general | solution.py:70
  45.8 3.6 %all-to-all-start.2 = ((bf16[8,256,256]{2,1,0:T(8,128)(2,1)}), bf16[8,256,256]{2,1,0:T(8,128)(2,1)S(1)}, u32[]{:S(2)}, u32[]{:S(2)}) async-start(bf16[8,256,256]{2,1,0:T(8,128)(2,1)} %fusion.6), calls=%async_computation.2 | async-start | bytes 2097152 | tf_op jit(solution)/shard_map/all_to_all | solution.py:71
  49.5 0.4 reshape.127
  49.9 1.1 %constant_dynamic-slice_fusion.1 = (bf16[128,4,1,128]{3,2,1,0:T(2,128)(2,1)S(1)}, bf16[128,4,1,128]{3,2,1,0:T(2,128)(2,1)S(1)}, bf16[128,4,1,128]{3,2,1,0:T(2,128)(2,1)S(1)}, bf16[128,4,1,128]{3,2,1,0:T(2,128)(2,1)S(1)}) fusion(bf16[128,4,4,128]{3,2,1,0:T(4,128)(2,1)S(1)} %reshape.127, s32[]{:T(128)S(6)} %select_n.70, s32[]{:T(128)S(6)} %select_n.69, ...), kind=kLoop, calls=%fused_computation.43 | loop fusion | bytes 1048592 | tf_op jit(solution)/shard_map/dynamic-slice.2
  51.0 0.2 copy.29
  51.1 2.4 %collective-permute-start.6 = (bf16[128,512]{0,1:T(8,128)(2,1)S(1)}, bf16[128,512]{0,1:T(8,128)(2,1)S(1)}, u32[]{:S(2)}, u32[]{:S(2)}) collective-permute-start(bf16[128,512]{0,1:T(8,128)(2,1)S(1)} %bitcast.90), channel_id=1, source_target_pairs={{0,48},{16,32},{32,16},{48,0},{1,49},{17,33},{33,17},{49,1},{2,50}... | collective-permute-start | bytes 393224 | tf_op jit(solution)/shard_map/ppermute | solution.py:23
  53.7 3.2 %collective-permute-start.2 = (bf16[128,512]{0,1:T(8,128)(2,1)S(1)}, bf16[128,512]{0,1:T(8,128)(2,1)S(1)}, u32[]{:S(2)}, u32[]{:S(2)}) collective-permute-start(bf16[128,512]{0,1:T(8,128)(2,1)S(1)} %bitcast.92), channel_id=1, source_target_pairs={{0,16},{16,0},{1,17},{17,1},{2,18},{18,2},{3,19},{19,3},{4,20},{20... | collective-permute-start | bytes 393224 | tf_op jit(solution)/shard_map/ppermute | solution.py:21
  57.1 0.2 copy.26
  57.3 11.3 %all-to-all-done.2 = bf16[8,256,256]{2,1,0:T(8,128)(2,1)S(1)} async-done(((bf16[8,256,256]{2,1,0:T(8,128)(2,1)}), bf16[8,256,256]{2,1,0:T(8,128)(2,1)S(1)}, u32[]{:S(2)}, u32[]{:S(2)}) %all-to-all-start.2) | async-done | bytes 1048608 | tf_op jit(solution)/shard_map/all_to_all | solution.py:71
  68.8 0.3 fusion.22
  69.1 4.5 %collective-permute-start.7 = (bf16[256,256]{1,0:T(8,128)(2,1)S(1)}, bf16[256,256]{1,0:T(8,128)(2,1)S(1)}, u32[]{:S(2)}, u32[]{:S(2)}) collective-permute-start(bf16[256,256]{1,0:T(8,128)(2,1)S(1)} %reduce_sum.21), channel_id=1, source_target_pairs={{0,48},{16,32},{32,16},{48,0},{1,49},{17,33},{33,17},{49,1},{2,50}... | collective-permute-start | bytes 393224 | tf_op jit(solution)/shard_map/ppermute | solution.py:23
  73.6 3.1 %collective-permute-done.3 = bf16[256,256]{1,0:T(8,128)(2,1)S(1)} collective-permute-done((bf16[256,256]{1,0:T(8,128)(2,1)S(1)}, bf16[256,256]{1,0:T(8,128)(2,1)S(1)}, u32[]{:S(2)}, u32[]{:S(2)}) %collective-permute-start.3) | collective-permute-done | bytes 131104 | tf_op jit(solution)/shard_map/ppermute | solution.py:21
  76.7 0.3 convolution_add_fusion.1
  77.1 0.3 fusion.18
  77.3 4.3 %collective-permute-done.5 = bf16[256,256]{1,0:T(8,128)(2,1)S(1)} collective-permute-done((bf16[256,256]{1,0:T(8,128)(2,1)S(1)}, bf16[256,256]{1,0:T(8,128)(2,1)S(1)}, u32[]{:S(2)}, u32[]{:S(2)}) %collective-permute-start.5) | collective-permute-done | bytes 131104 | tf_op jit(solution)/shard_map/ppermute | solution.py:22
  81.7 0.3 fusion.10
  82.1 0.9 copy.25
  83.0 4.5 %all-to-all-start.3 = ((bf16[8,128,2,128]{3,1,2,0:T(8,128)(2,1)}), bf16[8,128,2,128]{3,1,2,0:T(8,128)(2,1)S(1)}, u32[]{:S(2)}, u32[]{:S(2)}) async-start(bf16[8,128,2,128]{3,1,2,0:T(8,128)(2,1)} %bitcast.29), calls=%async_computation.3 | async-start | bytes 1048576 | tf_op jit(solution)/shard_map/all_to_all | solution.py:81
  87.8 17.7 %all-to-all-done.3 = bf16[8,128,2,128]{3,1,2,0:T(8,128)(2,1)S(1)} async-done(((bf16[8,128,2,128]{3,1,2,0:T(8,128)(2,1)}), bf16[8,128,2,128]{3,1,2,0:T(8,128)(2,1)S(1)}, u32[]{:S(2)}, u32[]{:S(2)}) %all-to-all-start.3) | async-done | bytes 524320 | tf_op jit(solution)/shard_map/all_to_all | solution.py:81
  105.5 0.8 multiply_add_fusion
  (42 shorter events, 1.8 us)
Async XLA Ops:
  0.0 34.4 %copy-start.2 = (f32[512]{0:T(512)S(1)}, f32[512]{0:T(512)}, u32[]{:S(2)}) copy-start(f32[512]{0:T(512)} %param.16) | copy-start | bytes 6148
  0.0 34.4 %copy-start.3 = (f32[512]{0:T(512)S(1)}, f32[512]{0:T(512)}, u32[]{:S(2)}) copy-start(f32[512]{0:T(512)} %param.15) | copy-start | bytes 6148
  0.0 34.6 %copy-start.1 = (f32[2]{0:T(128)S(1)}, f32[2]{0:T(128)}, u32[]{:S(2)}) copy-start(f32[2]{0:T(128)} %param.17) | copy-start | bytes 28
  1.7 27.5 %all-to-all-start.1 = ((bf16[16,32,512]{2,1,0:T(8,128)(2,1)}), bf16[16,32,512]{2,1,0:T(8,128)(2,1)S(1)}, u32[]{:S(2)}, u32[]{:S(2)}) async-start(bf16[16,32,512]{2,1,0:T(8,128)(2,1)} %broadcast_in_dim.5), calls=%async_computation.1 | async-start | bytes 1048576 | tf_op jit(solution)/shard_map/all_to_all | solution.py:15
  29.9 11.8 %all-to-all-start = ((bf16[8,64,256]{2,1,0:T(8,128)(2,1)}), bf16[8,64,256]{2,1,0:T(8,128)(2,1)S(1)}, u32[]{:S(2)}, u32[]{:S(2)}) async-start(bf16[8,64,256]{2,1,0:T(8,128)(2,1)} %broadcast_in_dim.4), calls=%async_computation | async-start | bytes 524288 | tf_op jit(solution)/shard_map/all_to_all | solution.py:15
  34.5 8.3 %collective-permute-start.1 = (bf16[512,512]{1,0:T(8,128)(2,1)S(1)}, bf16[512,512]{1,0:T(8,128)(2,1)S(1)}, u32[]{:S(2)}, u32[]{:S(2)}) collective-permute-start(bf16[512,512]{1,0:T(8,128)(2,1)S(1)} %bitcast.82), channel_id=1, source_target_pairs={{0,1},{1,0},{2,3},{3,2},{4,5},{5,4},{6,7},{7,6},{8,9},{9,8},{10,11... | collective-permute-start | bytes 1572872 | tf_op jit(solution)/shard_map/ppermute | solution.py:59
  42.4 1.6 %copy-start.6 = (bf16[512,2048]{1,0:T(8,128)(2,1)S(1)}, bf16[512,2048]{1,0:T(8,128)(2,1)}, u32[]{:S(2)}) copy-start(bf16[512,2048]{1,0:T(8,128)(2,1)} %param.21) | copy-start | bytes 6291460
  44.0 5.3 %copy-start.4 = (f32[2]{0:T(128)S(1)}, f32[2]{0:T(128)}, u32[]{:S(2)}) copy-start(f32[2]{0:T(128)} %param.18) | copy-start | bytes 28
  44.0 5.5 %copy-start = (bf16[128,2048]{1,0:T(8,128)(2,1)S(1)}, bf16[128,2048]{1,0:T(8,128)(2,1)}, u32[]{:S(2)}) copy-start(bf16[128,2048]{1,0:T(8,128)(2,1)} %param.20) | copy-start | bytes 1572868
  45.8 22.8 %all-to-all-start.2 = ((bf16[8,256,256]{2,1,0:T(8,128)(2,1)}), bf16[8,256,256]{2,1,0:T(8,128)(2,1)S(1)}, u32[]{:S(2)}, u32[]{:S(2)}) async-start(bf16[8,256,256]{2,1,0:T(8,128)(2,1)} %fusion.6), calls=%async_computation.2 | async-start | bytes 2097152 | tf_op jit(solution)/shard_map/all_to_all | solution.py:71
  49.4 38.2 %collective-permute-start = (f32[2,2]{1,0:T(2,128)S(1)}, f32[2,2]{1,0:T(2,128)S(1)}, u32[]{:S(2)}, u32[]{:S(2)}) collective-permute-start(f32[2,2]{1,0:T(2,128)S(1)} %pad_maximum_fusion.1), channel_id=1, source_target_pairs={{0,1},{1,0},{2,3},{3,2},{4,5},{5,4},{6,7},{7,6},{8,9},{9,8},{10,11... | collective-permute-start | bytes 56 | tf_op jit(solution)/shard_map/ppermute | solution.py:43
  51.1 25.9 %collective-permute-start.6 = (bf16[128,512]{0,1:T(8,128)(2,1)S(1)}, bf16[128,512]{0,1:T(8,128)(2,1)S(1)}, u32[]{:S(2)}, u32[]{:S(2)}) collective-permute-start(bf16[128,512]{0,1:T(8,128)(2,1)S(1)} %bitcast.90), channel_id=1, source_target_pairs={{0,48},{16,32},{32,16},{48,0},{1,49},{17,33},{33,17},{49,1},{2,50}... | collective-permute-start | bytes 393224 | tf_op jit(solution)/shard_map/ppermute | solution.py:23
  53.7 15.4 %collective-permute-start.2 = (bf16[128,512]{0,1:T(8,128)(2,1)S(1)}, bf16[128,512]{0,1:T(8,128)(2,1)S(1)}, u32[]{:S(2)}, u32[]{:S(2)}) collective-permute-start(bf16[128,512]{0,1:T(8,128)(2,1)S(1)} %bitcast.92), channel_id=1, source_target_pairs={{0,16},{16,0},{1,17},{17,1},{2,18},{18,2},{3,19},{19,3},{4,20},{20... | collective-permute-start | bytes 393224 | tf_op jit(solution)/shard_map/ppermute | solution.py:21
  57.0 20.3 %collective-permute-start.4 = (bf16[128,512]{0,1:T(8,128)(2,1)S(1)}, bf16[128,512]{0,1:T(8,128)(2,1)S(1)}, u32[]{:S(2)}, u32[]{:S(2)}) collective-permute-start(bf16[128,512]{0,1:T(8,128)(2,1)S(1)} %bitcast.91), channel_id=1, source_target_pairs={{0,32},{32,0},{1,33},{33,1},{2,34},{34,2},{3,35},{35,3},{4,36},{36... | collective-permute-start | bytes 393224 | tf_op jit(solution)/shard_map/ppermute | solution.py:22
  68.7 8.0 %collective-permute-start.3 = (bf16[256,256]{1,0:T(8,128)(2,1)S(1)}, bf16[256,256]{1,0:T(8,128)(2,1)S(1)}, u32[]{:S(2)}, u32[]{:S(2)}) collective-permute-start(bf16[256,256]{1,0:T(8,128)(2,1)S(1)} %reduce_sum.21), channel_id=1, source_target_pairs={{0,16},{16,0},{1,17},{17,1},{2,18},{18,2},{3,19},{19,3},{4,20},{20... | collective-permute-start | bytes 393224 | tf_op jit(solution)/shard_map/ppermute | solution.py:21
  69.1 7.9 %collective-permute-start.7 = (bf16[256,256]{1,0:T(8,128)(2,1)S(1)}, bf16[256,256]{1,0:T(8,128)(2,1)S(1)}, u32[]{:S(2)}, u32[]{:S(2)}) collective-permute-start(bf16[256,256]{1,0:T(8,128)(2,1)S(1)} %reduce_sum.21), channel_id=1, source_target_pairs={{0,48},{16,32},{32,16},{48,0},{1,49},{17,33},{33,17},{49,1},{2,50}... | collective-permute-start | bytes 393224 | tf_op jit(solution)/shard_map/ppermute | solution.py:23
  76.7 5.0 %collective-permute-start.5 = (bf16[256,256]{1,0:T(8,128)(2,1)S(1)}, bf16[256,256]{1,0:T(8,128)(2,1)S(1)}, u32[]{:S(2)}, u32[]{:S(2)}) collective-permute-start(bf16[256,256]{1,0:T(8,128)(2,1)S(1)} %reduce_sum.21), channel_id=1, source_target_pairs={{0,32},{32,0},{1,33},{33,1},{2,34},{34,2},{3,35},{35,3},{4,36},{36... | collective-permute-start | bytes 393224 | tf_op jit(solution)/shard_map/ppermute | solution.py:22
  82.0 5.7 %copy-start.5 = (f32[4]{0:T(128)S(1)}, f32[4]{0:T(128)}, u32[]{:S(2)}) copy-start(f32[4]{0:T(128)} %param.19) | copy-start | bytes 52
  83.0 22.4 %all-to-all-start.3 = ((bf16[8,128,2,128]{3,1,2,0:T(8,128)(2,1)}), bf16[8,128,2,128]{3,1,2,0:T(8,128)(2,1)S(1)}, u32[]{:S(2)}, u32[]{:S(2)}) async-start(bf16[8,128,2,128]{3,1,2,0:T(8,128)(2,1)} %bitcast.29), calls=%async_computation.3 | async-start | bytes 1048576 | tf_op jit(solution)/shard_map/all_to_all | solution.py:81

commit v2 on v1

v2 whole, which is shorter than its diff:
```python
import jax
import jax.numpy as jnp
from jax import lax
from jax.experimental import pallas as pl
from jax.experimental.pallas import tpu as pltpu
from jax.sharding import Mesh
from jax.sharding import PartitionSpec as P


ROW = ("z2", "z1", "z0", "xh")
COL = ("y2", "y1", "xl")
SWAP = [(0, 1), (1, 0)]
SMALL = pltpu.CompilerParams(vmem_limit_bytes=6 * 2**20)


def exchange(block, axes, mask):
    return lax.ppermute(block, axes, [(i, i ^ mask) for i in range(lax.axis_size(axes))])


def doubled(block, axis):
    other = lax.ppermute(block, axis, SWAP)
    low = lax.axis_index(axis) == 0
    return jnp.concatenate([jnp.where(low, block, other), jnp.where(low, other, block)], axis=0)


def sum_kernel(*refs):
    parts, out = refs[:-1], refs[-1]
    for t in range(4):
        here = slice(t * 128, t * 128 + 128)
        out[:, here] = sum(part[here, :].astype(jnp.float32) for part in parts).astype(jnp.bfloat16)


def summed(parts):
    return pl.pallas_call(
        sum_kernel,
        name="summed",
        out_shape=jax.ShapeDtypeStruct((128, 512), jnp.bfloat16),
        compiler_params=SMALL,
        cost_estimate=pl.CostEstimate(flops=500_000, bytes_accessed=1_300_000, transcendentals=0),
    )(*parts)


def left_kernel(place, *refs):
    aux, right, outs = refs[:4], refs[4:8], refs[8:]
    for e in range(4):
        at = pl.ds(pl.multiple_of((place[0] ^ e) * 128, 128), 128)
        made = sum(jnp.dot(a[at, :], r[...], preferred_element_type=jnp.float32) for a, r in zip(aux, right))
        outs[e][...] = made.astype(outs[e].dtype)


def left_parts(place, aux, right):
    vmem = pl.BlockSpec(memory_space=pltpu.VMEM)
    return pl.pallas_call(
        left_kernel,
        name="left_parts",
        out_shape=[jax.ShapeDtypeStruct((128, 512), jnp.bfloat16 if e else jnp.float32) for e in range(4)],
        in_specs=[pl.BlockSpec(memory_space=pltpu.SMEM)] + [vmem] * 8,
        out_specs=[vmem] * 4,
        compiler_params=SMALL,
        cost_estimate=pl.CostEstimate(flops=270_000_000, bytes_accessed=1_700_000, transcendentals=0),
    )(place, *aux, *right)


def mix_kernel(coef, *refs):
    parts, out = refs[:4], refs[4]
    whole = [sum(part[:, t * 128 : t * 128 + 128].astype(jnp.float32) for part in parts) for t in range(4)]
    for w in range(4):
        out[w] = sum(coef[w, t] * whole[t] for t in range(4))


def mix(coef, parts):
    vmem = pl.BlockSpec(memory_space=pltpu.VMEM)
    return pl.pallas_call(
        mix_kernel,
        name="mix",
        out_shape=jax.ShapeDtypeStruct((4, 128, 128), jnp.float32),
        in_specs=[pl.BlockSpec(memory_space=pltpu.SMEM)] + [vmem] * 4,
        out_specs=vmem,
        compiler_params=SMALL,
    )(coef, *parts)


def per_device(
    occ_rows,
    occ_cols,
    emp_rows,
    emp_cols,
    occ_gap,
    emp_gap,
    times,
    time_weights,
    freqs,
    aux_rows,
    aux_cols,
):
    core = lax.axis_index("tm")
    first = core == 0
    z2, z1, z0, xh = (lax.axis_index(a) for a in ROW)

    cols = jnp.where(first, occ_cols, emp_cols).T
    cols_a = lax.all_to_all(jnp.broadcast_to(cols[None], (16, 32, 512)), ROW, 0, 0, tiled=True).reshape(512, 512)

    rows = jnp.concatenate([jnp.where(first, occ_rows, emp_rows).T, jnp.where(first, emp_rows, occ_rows).T], axis=1)
    mine = jnp.stack([times, time_weights])
    for axis in reversed(COL):
        rows = doubled(rows, axis)
    other = lax.ppermute(mine, "tm", SWAP)

    every = jnp.concatenate([jnp.where(first, mine, other), jnp.where(first, other, mine)], axis=1)
    coef = every[1][None, :] * jnp.cos(freqs[:, None] * every[0][None, :])

    def scaled(piece, gap):
        factor = jnp.exp(-gap[:, None] * every[0][None, :])
        return (piece[:, None, :].astype(jnp.float32) * factor[:, :, None]).astype(jnp.bfloat16)

    scaled_a = scaled(rows[:, :128], jnp.where(first, occ_gap, emp_gap))
    scaled_b = scaled(rows[:, 128:], jnp.where(first, emp_gap, occ_gap))

    turned = aux_rows.T.reshape(2, 2, 2, 2, 128, 128)
    aux = []
    for mask in range(4):
        start = (0, 0, z0 ^ (mask // 2), xh ^ (mask % 2), 0, 0)
        block = lax.dynamic_slice(turned, start, (2, 2, 1, 1, 128, 128)).reshape(512, 128)
        aux.append(exchange(block, ("z0", "xh"), mask) if mask else block)

    here = lax.axis_index(COL)
    near = (0, 1, 2, 6, 3, 7, 4, 5)
    aux_to = [lax.dynamic_slice(aux_cols, (0, (2 * (here ^ s) + core) * 128), (512, 128)) for s in near]

    held = (scaled_a, scaled_b, cols_a, aux, aux_to)
    scaled_a, scaled_b, cols_a, aux, aux_to = lax.optimization_barrier(held)
    cols_b = lax.ppermute(cols_a, "tm", SWAP)
    green_a = jnp.einsum("otr,oc->trc", scaled_a, cols_a, preferred_element_type=jnp.float32)
    green_b = jnp.einsum("otr,oc->trc", scaled_b, cols_b, preferred_element_type=jnp.float32)
    chi = (green_a * green_b).astype(jnp.bfloat16).reshape(512, 512)

    parts = []
    for s, block in zip(near, aux_to):
        part = jnp.dot(chi, block, preferred_element_type=jnp.float32)
        parts.append(exchange(part.astype(jnp.bfloat16), COL, s) if s else part)
    right = summed(parts)
    right = [right] + [exchange(right, ("z0", "xh"), mask) for mask in (1, 2, 3)]
    place = (2 * z2 + z1).astype(jnp.int32).reshape(1)
    parts = left_parts(place, aux, right)
    parts = [parts[0]] + [exchange(parts[e], ("z2", "z1"), e) for e in (1, 2, 3)]
    return mix(coef, parts)


def solution(mesh):
    torus = Mesh(mesh.devices.reshape((2,) * 8), (*ROW, *COL, "tm"))
    return jax.shard_map(
        per_device,
        mesh=torus,
        in_specs=(
            P(ROW, COL),
            P(COL, ROW),
            P(ROW, COL),
            P(COL, ROW),
            P(),
            P(),
            P("tm"),
            P("tm"),
            P(),
            P(ROW, None),
            P(COL, None),
        ),
        out_specs=P(None, ROW, (*COL, "tm")),
        check_vma=False,
    )
```

time: 107 us -> 96.1 us (0.90)
  the two profiles are of different devices: /device:TPU:32 before, /device:TPU:40 now
where the time goes in v2:
time: 96.1 us; the launch traced here: 95.7 us
  starting transfers between devices  41.4 us (43%)
  waiting for transfers between devices  35.9 us (37%)
  local copies, waits for them, and re-layouts  7.31 us (8%)
  other arithmetic  5.25 us (5%)
  matrix products  3.21 us (3%)
  Pallas kernels  2.22 us (2%)
    ppermute x16, starting transfers between devices, exchange(): lax.ppermute(block, axes, [(i, i ^ mask) for i in range(lax.axis_size(axe...  26.3 us
    ppermute x16, waiting for transfers between devices, exchange(): lax.ppermute(block, axes, [(i, i ^ mask) for i in range(lax.axis_size(axe...  24.8 us
    all_to_all x1, starting transfers between devices, per_device(): lax.all_to_all(jnp.broadcast_to(cols[None], (16, 32, 512)), ROW, 0, 0, ti...  10.8 us
    ppermute x3, waiting for transfers between devices, doubled(): other = lax.ppermute(block, axis, SWAP)  7.9 us
    ppermute x3, starting transfers between devices, doubled(): other = lax.ppermute(block, axis, SWAP)  4.41 us
    unnamed x34, local copies, waits for them, and re-layouts  2.59 us
    dot_general x8, matrix products, per_device(): part = jnp.dot(chi, block, preferred_element_type=jnp.float32)  2.34 us
  transfers between devices with their start and end apart: 22, of which 14 were waited for; matrix products, arithmetic and copies ran while one was open for 14% of the time, Pallas kernels for 0%

profile of v2, /device:TPU:40, one launch (start us, length us, event | category | flops | bytes accessed | tf_op | source)
XLA Modules:
  0.0 95.7 jit_solution(1698697532732689887)
XLA Ops:
  1.4 1.5 %collective-permute-start.1 = (bf16[64,256]{1,0:T(8,128)(2,1)}, bf16[64,256]{1,0:T(8,128)(2,1)}, u32[]{:S(2)}, u32[]{:S(2)}) collective-permute-start(bf16[64,256]{1,0:T(8,128)(2,1)} %pad_maximum_fusion.3), channel_id=1, source_target_pairs={{0,2},{2,0},{1,3},{3,1},{4,6},{6,4},{5,7},{7,5},{8,10},{10,8},{9,1... | collective-permute-start | bytes 98312 | tf_op jit(solution)/shard_map/ppermute | solution.py:21
  2.9 1.2 %pad_maximum_fusion.4 = f32[2,2]{1,0:T(2,128)} fusion(f32[1,2]{1,0:T(1,128)} %bitcast.58, f32[1,2]{1,0:T(1,128)} %bitcast.60), kind=kLoop, calls=%fused_computation.49 | loop fusion | flops 4 | bytes 32 | tf_op jit(solution)/shard_map/stack | solution.py:104
  4.1 1.4 %reshape.94 = bf16[2,2,2,2,128,128]{4,3,2,1,0,5:T(2,128)(2,1)S(1)} reshape(bf16[2048,128]{0,1:T(8,128)(2,1)} %bitcast.57) | data formatting | bytes 1048576 | tf_op jit(solution)/shard_map/reshape | solution.py:119
  5.5 1.1 %constant_dynamic-slice_fusion.8 = (bf16[2,2,1,1,128,128]{4,3,2,1,0,5:T(2,128)(2,1)S(1)}, bf16[2,2,1,1,128,128]{4,3,2,1,0,5:T(2,128)(2,1)S(1)}, bf16[2,2,1,1,128...) fusion(bf16[2,2,2,2,128,128]{4,3,2,1,0,5:T(2,128)(2,1)S(1)} %reshape.94, s32[]{:T(128)S(6)} %select_n.143, ...), kind=kLoop, calls=%fused_computation.42 | loop fusion | bytes 1048592 | tf_op jit(solution)/shard_map/dynamic_slice | solution.py:123
  7.4 2.7 %collective-permute-start.4 = (bf16[512,128]{1,0:T(8,128)(2,1)}, bf16[512,128]{1,0:T(8,128)(2,1)S(1)}, u32[]{:S(2)}, u32[]{:S(2)}) collective-permute-start(bf16[512,128]{1,0:T(8,128)(2,1)} %bitcast.11), channel_id=1, source_target_pairs={{0,16},{16,0},{32,48},{48,32},{1,17},{17,1},{33,49},{49,33},{2,18}... | collective-permute-start | bytes 393224 | tf_op jit(solution)/shard_map/ppermute | solution.py:17
  11.9 2.2 %collective-permute-start.6 = (bf16[512,128]{1,0:T(8,128)(2,1)}, bf16[512,128]{1,0:T(8,128)(2,1)S(1)}, u32[]{:S(2)}, u32[]{:S(2)}) collective-permute-start(bf16[512,128]{1,0:T(8,128)(2,1)} %bitcast.13), channel_id=1, source_target_pairs={{0,48},{16,32},{32,16},{48,0},{1,49},{17,33},{33,17},{49,1},{2,50}... | collective-permute-start | bytes 393224 | tf_op jit(solution)/shard_map/ppermute | solution.py:17
  14.9 10.8 %all-to-all-start = ((bf16[16,32,512]{2,1,0:T(8,128)(2,1)}), bf16[16,32,512]{2,1,0:T(8,128)(2,1)S(1)}, u32[]{:S(2)}, u32[]{:S(2)}) async-start(bf16[16,32,512]{2,1,0:T(8,128)(2,1)} %broadcast_in_dim.2), calls=%async_computation | async-start | bytes 1048576 | tf_op jit(solution)/shard_map/all_to_all | solution.py:101
  26.4 1.1 %constant_dynamic-slice_fusion = (bf16[512,128]{1,0:T(8,128)(2,1)}, bf16[512,128]{1,0:T(8,128)(2,1)}, bf16[512,128]{1,0:T(8,128)(2,1)}, bf16[512,128]{1,0:T(8,12...) fusion(bf16[512,2048]{1,0:T(8,128)(2,1)S(1)} %copy-done, ...), kind=kLoop, calls=%fused_computation.34 | loop fusion | bytes 2097184 | tf_op jit(solution)/shard_map/dynamic_slice | solution.py:128
  29.6 3.8 %collective-permute-done.2 = bf16[128,256]{1,0:T(8,128)(2,1)S(1)} collective-permute-done((bf16[128,256]{1,0:T(8,128)(2,1)S(1)}, bf16[128,256]{1,0:T(8,128)(2,1)S(1)}, u32[]{:S(2)}, u32[]{:S(2)}) %collective-permute-start.2) | collective-permute-done | bytes 65568 | tf_op jit(solution)/shard_map/ppermute | solution.py:21
  33.5 2.4 %collective-permute-start.3 = (bf16[256,256]{1,0:T(8,128)(2,1)S(1)}, bf16[256,256]{1,0:T(8,128)(2,1)S(1)}, u32[]{:S(2)}, u32[]{:S(2)}) collective-permute-start(bf16[256,256]{1,0:T(8,128)(2,1)S(1)} %pad_maximum_fusion.1), channel_id=1, source_target_pairs={{0,8},{8,0},{1,9},{9,1},{2,10},{10,2},{3,11},{11,3},{4,12},{12,4},... | collective-permute-start | bytes 393224 | tf_op jit(solution)/shard_map/ppermute | solution.py:21
  35.9 4.1 %collective-permute-done.3 = bf16[256,256]{1,0:T(8,128)(2,1)S(1)} collective-permute-done((bf16[256,256]{1,0:T(8,128)(2,1)S(1)}, bf16[256,256]{1,0:T(8,128)(2,1)S(1)}, u32[]{:S(2)}, u32[]{:S(2)}) %collective-permute-start.3) | collective-permute-done | bytes 131104 | tf_op jit(solution)/shard_map/ppermute | solution.py:21
  40.7 1.3 %all-to-all-done = bf16[16,32,512]{2,1,0:T(8,128)(2,1)S(1)} async-done(((bf16[16,32,512]{2,1,0:T(8,128)(2,1)}), bf16[16,32,512]{2,1,0:T(8,128)(2,1)S(1)}, u32[]{:S(2)}, u32[]{:S(2)}) %all-to-all-start) | async-done | bytes 524320 | tf_op jit(solution)/shard_map/all_to_all | solution.py:101
  41.9 1.9 %collective-permute-done.7 = bf16[512,512]{1,0:T(8,128)(2,1)S(1)} collective-permute-done((bf16[512,512]{1,0:T(8,128)(2,1)S(1)}, bf16[512,512]{1,0:T(8,128)(2,1)S(1)}, u32[]{:S(2)}, u32[]{:S(2)}) %collective-permute-start.7) | collective-permute-done | bytes 524320 | tf_op jit(solution)/shard_map/ppermute | solution.py:132
  45.1 2.0 %collective-permute-start.14 = (bf16[512,128]{1,0:T(8,128)(2,1)S(1)}, bf16[512,128]{1,0:T(8,128)(2,1)S(1)}, u32[]{:S(2)}, u32[]{:S(2)}) collective-permute-start(bf16[512,128]{1,0:T(8,128)(2,1)S(1)} %convolution_convert_fusion), channel_id=1, source_target_pairs={{0,10},{2,8},{4,14},{6,12},{8,2},{10,0},{12,6},{14,4},{1,11},{3,9}... | collective-permute-start | bytes 393224 | tf_op jit(solution)/shard_map/ppermute | solution.py:17
  47.4 1.3 %collective-permute-start.13 = (bf16[512,128]{1,0:T(8,128)(2,1)S(1)}, bf16[512,128]{1,0:T(8,128)(2,1)S(1)}, u32[]{:S(2)}, u32[]{:S(2)}) collective-permute-start(bf16[512,128]{1,0:T(8,128)(2,1)S(1)} %convolution_convert_fusion.1), channel_id=1, source_target_pairs={{0,8},{2,10},{4,12},{6,14},{8,0},{10,2},{12,4},{14,6},{1,9},{3,11}... | collective-permute-start | bytes 393224 | tf_op jit(solution)/shard_map/ppermute | solution.py:17
  49.0 2.9 %collective-permute-start.12 = (bf16[512,128]{1,0:T(8,128)(2,1)S(1)}, bf16[512,128]{1,0:T(8,128)(2,1)S(1)}, u32[]{:S(2)}, u32[]{:S(2)}) collective-permute-start(bf16[512,128]{1,0:T(8,128)(2,1)S(1)} %convolution_convert_fusion.2), channel_id=1, source_target_pairs={{0,14},{2,12},{4,10},{6,8},{8,6},{10,4},{12,2},{14,0},{1,15},{3,13... | collective-permute-start | bytes 393224 | tf_op jit(solution)/shard_map/ppermute | solution.py:17
  52.3 1.6 %collective-permute-start.11 = (bf16[512,128]{1,0:T(8,128)(2,1)S(1)}, bf16[512,128]{1,0:T(8,128)(2,1)S(1)}, u32[]{:S(2)}, u32[]{:S(2)}) collective-permute-start(bf16[512,128]{1,0:T(8,128)(2,1)S(1)} %convolution_convert_fusion.3), channel_id=1, source_target_pairs={{0,6},{2,4},{4,2},{6,0},{8,14},{10,12},{12,10},{14,8},{1,7},{3,5},... | collective-permute-start | bytes 393224 | tf_op jit(solution)/shard_map/ppermute | solution.py:17
  55.1 1.2 %collective-permute-start.9 = (bf16[512,128]{1,0:T(8,128)(2,1)S(1)}, bf16[512,128]{1,0:T(8,128)(2,1)S(1)}, u32[]{:S(2)}, u32[]{:S(2)}) collective-permute-start(bf16[512,128]{1,0:T(8,128)(2,1)S(1)} %convolution_convert_fusion.5), channel_id=1, source_target_pairs={{0,4},{2,6},{4,0},{6,2},{8,12},{10,14},{12,8},{14,10},{1,5},{3,7},... | collective-permute-start | bytes 393224 | tf_op jit(solution)/shard_map/ppermute | solution.py:17
  56.4 3.6 %collective-permute-done.13.refs_6_ = bf16[512,128]{1,0:T(8,128)(2,1)S(1)} collective-permute-done((bf16[512,128]{1,0:T(8,128)(2,1)S(1)}, bf16[512,128]{1,0:T(8,128)(2,1)S(1)}, u32[]{:S(2)}, u32[]{:S(2)}) %collective-permute-start.13) | collective-permute-done | bytes 131104 | tf_op jit(solution)/shard_map/ppermute | solution.py:17
  60.3 1.2 %collective-permute-done.10.refs_3_ = bf16[512,128]{1,0:T(8,128)(2,1)S(1)} collective-permute-done((bf16[512,128]{1,0:T(8,128)(2,1)S(1)}, bf16[512,128]{1,0:T(8,128)(2,1)S(1)}, u32[]{:S(2)}, u32[]{:S(2)}) %collective-permute-start.10) | collective-permute-done | bytes 131104 | tf_op jit(solution)/shard_map/ppermute | solution.py:17
  62.4 2.9 %collective-permute-done.8.refs_1_ = bf16[512,128]{1,0:T(8,128)(2,1)S(1)} collective-permute-done((bf16[512,128]{1,0:T(8,128)(2,1)S(1)}, bf16[512,128]{1,0:T(8,128)(2,1)S(1)}, u32[]{:S(2)}, u32[]{:S(2)}) %collective-permute-start.8) | collective-permute-done | bytes 131104 | tf_op jit(solution)/shard_map/ppermute | solution.py:17
  66.0 1.9 %collective-permute-start.16 = (bf16[128,512]{1,0:T(8,128)(2,1)S(1)}, bf16[128,512]{1,0:T(8,128)(2,1)S(1)}, u32[]{:S(2)}, u32[]{:S(2)}) collective-permute-start(bf16[128,512]{1,0:T(8,128)(2,1)S(1)} %summed.1.refs_4_), channel_id=1, source_target_pairs={{0,32},{16,48},{32,0},{48,16},{1,33},{17,49},{33,1},{49,17},{2,34}... | collective-permute-start | bytes 393224 | tf_op jit(solution)/shard_map/ppermute | solution.py:17
  67.8 2.9 %collective-permute-start.17 = (bf16[128,512]{1,0:T(8,128)(2,1)S(1)}, bf16[128,512]{1,0:T(8,128)(2,1)S(1)}, u32[]{:S(2)}, u32[]{:S(2)}) collective-permute-start(bf16[128,512]{1,0:T(8,128)(2,1)S(1)} %summed.1.refs_4_), channel_id=1, source_target_pairs={{0,48},{16,32},{32,16},{48,0},{1,49},{17,33},{33,17},{49,1},{2,50}... | collective-permute-start | bytes 393224 | tf_op jit(solution)/shard_map/ppermute | solution.py:17
  70.7 2.0 %collective-permute-done.15.refs_5_ = bf16[128,512]{1,0:T(8,128)(2,1)S(1)} collective-permute-done((bf16[128,512]{1,0:T(8,128)(2,1)S(1)}, bf16[128,512]{1,0:T(8,128)(2,1)S(1)}, u32[]{:S(2)}, u32[]{:S(2)}) %collective-permute-start.15) | collective-permute-done | bytes 131104 | tf_op jit(solution)/shard_map/ppermute | solution.py:17
  72.8 3.2 %collective-permute-done.17.refs_7_ = bf16[128,512]{1,0:T(8,128)(2,1)S(1)} collective-permute-done((bf16[128,512]{1,0:T(8,128)(2,1)S(1)}, bf16[128,512]{1,0:T(8,128)(2,1)S(1)}, u32[]{:S(2)}, u32[]{:S(2)}) %collective-permute-start.17) | collective-permute-done | bytes 131104 | tf_op jit(solution)/shard_map/ppermute | solution.py:17
  76.6 2.1 %collective-permute-start.18 = (bf16[128,512]{1,0:T(8,128)(2,1)S(1)}, bf16[128,512]{1,0:T(8,128)(2,1)S(1)}, u32[]{:S(2)}, u32[]{:S(2)}) collective-permute-start(bf16[128,512]{1,0:T(8,128)(2,1)S(1)} %get-tuple-element.40), channel_id=1, source_target_pairs={{0,64},{64,0},{128,192},{192,128},{1,65},{65,1},{129,193},{193,129... | collective-permute-start | bytes 393224 | tf_op jit(solution)/shard_map/ppermute | solution.py:17
  78.8 2.0 %collective-permute-start.19 = (bf16[128,512]{1,0:T(8,128)(2,1)S(1)}, bf16[128,512]{1,0:T(8,128)(2,1)S(1)}, u32[]{:S(2)}, u32[]{:S(2)}) collective-permute-start(bf16[128,512]{1,0:T(8,128)(2,1)S(1)} %get-tuple-element.41), channel_id=1, source_target_pairs={{0,128},{64,192},{128,0},{192,64},{1,129},{65,193},{129,1},{193,65... | collective-permute-start | bytes 393224 | tf_op jit(solution)/shard_map/ppermute | solution.py:17
  80.8 2.4 %collective-permute-start.20 = (bf16[128,512]{1,0:T(8,128)(2,1)S(1)}, bf16[128,512]{1,0:T(8,128)(2,1)S(1)}, u32[]{:S(2)}, u32[]{:S(2)}) collective-permute-start(bf16[128,512]{1,0:T(8,128)(2,1)S(1)} %get-tuple-element.42), channel_id=1, source_target_pairs={{0,192},{64,128},{128,64},{192,0},{1,193},{65,129},{129,65},{193,1... | collective-permute-start | bytes 393224 | tf_op jit(solution)/shard_map/ppermute | solution.py:17
  83.3 3.8 %collective-permute-done.18.refs_1_ = bf16[128,512]{1,0:T(8,128)(2,1)S(1)} collective-permute-done((bf16[128,512]{1,0:T(8,128)(2,1)S(1)}, bf16[128,512]{1,0:T(8,128)(2,1)S(1)}, u32[]{:S(2)}, u32[]{:S(2)}) %collective-permute-start.18) | collective-permute-done | bytes 131104 | tf_op jit(solution)/shard_map/ppermute | solution.py:17
  87.1 3.3 %collective-permute-done.19.refs_2_ = bf16[128,512]{1,0:T(8,128)(2,1)S(1)} collective-permute-done((bf16[128,512]{1,0:T(8,128)(2,1)S(1)}, bf16[128,512]{1,0:T(8,128)(2,1)S(1)}, u32[]{:S(2)}, u32[]{:S(2)}) %collective-permute-start.19) | collective-permute-done | bytes 131104 | tf_op jit(solution)/shard_map/ppermute | solution.py:17
  90.4 3.9 %collective-permute-done.20.refs_3_ = bf16[128,512]{1,0:T(8,128)(2,1)S(1)} collective-permute-done((bf16[128,512]{1,0:T(8,128)(2,1)S(1)}, bf16[128,512]{1,0:T(8,128)(2,1)S(1)}, u32[]{:S(2)}, u32[]{:S(2)}) %collective-permute-start.20) | collective-permute-done | bytes 131104 | tf_op jit(solution)/shard_map/ppermute | solution.py:17
  94.3 1.4 %mix.1 = f32[4,128,128]{2,1,0:T(8,128)} custom-call(f32[4,4]{1,0:T(4,128)S(1)} %cosine_multiply_fusion.coef, f32[128,512]{1,0:T(8,128)S(1)} %get-tuple-element.39.refs_0_, bf16[128,512]{1,0:T(8,128)(2,1)S(1)} %collective-permute-done.18.refs_1_, bf16[128,512]{1,0:T(8,128)(2,1)S(1)} %collective-permute-done.19.refs_2_, ...), custom_call_target="tpu_custom_call" | custom-call | tf_op jit(solution)/shard_map/mix/pallas_call | solution.py:73
  (82 shorter events, 14.2 us)
Async XLA Ops:
  1.4 26.9 %collective-permute-start.1 = (bf16[64,256]{1,0:T(8,128)(2,1)}, bf16[64,256]{1,0:T(8,128)(2,1)}, u32[]{:S(2)}, u32[]{:S(2)}) collective-permute-start(bf16[64,256]{1,0:T(8,128)(2,1)} %pad_maximum_fusion.3), channel_id=1, source_target_pairs={{0,2},{2,0},{1,3},{3,1},{4,6},{6,4},{5,7},{7,5},{8,10},{10,8},{9,1... | collective-permute-start | bytes 98312 | tf_op jit(solution)/shard_map/ppermute | solution.py:21
  4.1 23.4 %collective-permute-start = (f32[2,2]{1,0:T(2,128)}, f32[2,2]{1,0:T(2,128)}, u32[]{:S(2)}, u32[]{:S(2)}) collective-permute-start(f32[2,2]{1,0:T(2,128)} %pad_maximum_fusion.4), channel_id=1, source_target_pairs={{0,1},{1,0},{2,3},{3,2},{4,5},{5,4},{6,7},{7,6},{8,9},{9,8},{10,11... | collective-permute-start | bytes 56 | tf_op jit(solution)/shard_map/ppermute | solution.py:107
  4.1 9.9 %copy-start.8 = (bf16[512,32]{0,1:T(8,128)(2,1)S(1)}, bf16[512,32]{0,1:T(8,128)(2,1)}, u32[]{:S(2)}) copy-start(bf16[512,32]{0,1:T(8,128)(2,1)} %param.12) | copy-start | bytes 98308
  4.1 9.9 %copy-start.9 = (bf16[512,32]{0,1:T(8,128)(2,1)S(1)}, bf16[512,32]{0,1:T(8,128)(2,1)}, u32[]{:S(2)}) copy-start(bf16[512,32]{0,1:T(8,128)(2,1)} %param.14) | copy-start | bytes 98308
  6.6 19.2 %copy-start.12 = (f32[512]{0:T(512)S(1)}, f32[512]{0:T(512)}, u32[]{:S(2)}) copy-start(f32[512]{0:T(512)} %param.16) | copy-start | bytes 6148
  6.6 19.2 %copy-start.13 = (f32[512]{0:T(512)S(1)}, f32[512]{0:T(512)}, u32[]{:S(2)}) copy-start(f32[512]{0:T(512)} %param.15) | copy-start | bytes 6148
  6.6 19.8 %copy-start = (bf16[512,2048]{1,0:T(8,128)(2,1)S(1)}, bf16[512,2048]{1,0:T(8,128)(2,1)}, u32[]{:S(2)}) copy-start(bf16[512,2048]{1,0:T(8,128)(2,1)} %param.21) | copy-start | bytes 6291460
  7.4 33.2 %collective-permute-start.4 = (bf16[512,128]{1,0:T(8,128)(2,1)}, bf16[512,128]{1,0:T(8,128)(2,1)S(1)}, u32[]{:S(2)}, u32[]{:S(2)}) collective-permute-start(bf16[512,128]{1,0:T(8,128)(2,1)} %bitcast.11), channel_id=1, source_target_pairs={{0,16},{16,0},{32,48},{48,32},{1,17},{17,1},{33,49},{49,33},{2,18}... | collective-permute-start | bytes 393224 | tf_op jit(solution)/shard_map/ppermute | solution.py:17
  11.0 29.7 %collective-permute-start.5 = (bf16[512,128]{1,0:T(8,128)(2,1)}, bf16[512,128]{1,0:T(8,128)(2,1)S(1)}, u32[]{:S(2)}, u32[]{:S(2)}) collective-permute-start(bf16[512,128]{1,0:T(8,128)(2,1)} %bitcast.12), channel_id=1, source_target_pairs={{0,32},{16,48},{32,0},{48,16},{1,33},{17,49},{33,1},{49,17},{2,34}... | collective-permute-start | bytes 393224 | tf_op jit(solution)/shard_map/ppermute | solution.py:17
  11.9 28.8 %collective-permute-start.6 = (bf16[512,128]{1,0:T(8,128)(2,1)}, bf16[512,128]{1,0:T(8,128)(2,1)S(1)}, u32[]{:S(2)}, u32[]{:S(2)}) collective-permute-start(bf16[512,128]{1,0:T(8,128)(2,1)} %bitcast.13), channel_id=1, source_target_pairs={{0,48},{16,32},{32,16},{48,0},{1,49},{17,33},{33,17},{49,1},{2,50}... | collective-permute-start | bytes 393224 | tf_op jit(solution)/shard_map/ppermute | solution.py:17
  14.9 27.0 %all-to-all-start = ((bf16[16,32,512]{2,1,0:T(8,128)(2,1)}), bf16[16,32,512]{2,1,0:T(8,128)(2,1)S(1)}, u32[]{:S(2)}, u32[]{:S(2)}) async-start(bf16[16,32,512]{2,1,0:T(8,128)(2,1)} %broadcast_in_dim.2), calls=%async_computation | async-start | bytes 1048576 | tf_op jit(solution)/shard_map/all_to_all | solution.py:101
  26.4 9.4 %copy-start.10 = (f32[512]{0:T(512)S(1)}, f32[512]{0:T(512)}, u32[]{:S(2)}) copy-start(f32[512]{0:T(512)} %get-tuple-element.65) | copy-start | bytes 6148
  26.4 9.4 %copy-start.11 = (f32[512]{0:T(512)S(1)}, f32[512]{0:T(512)}, u32[]{:S(2)}) copy-start(f32[512]{0:T(512)} %get-tuple-element.66) | copy-start | bytes 6148
  29.1 4.4 %collective-permute-start.2 = (bf16[128,256]{1,0:T(8,128)(2,1)S(1)}, bf16[128,256]{1,0:T(8,128)(2,1)S(1)}, u32[]{:S(2)}, u32[]{:S(2)}) collective-permute-start(bf16[128,256]{1,0:T(8,128)(2,1)S(1)} %pad_maximum_fusion.2), channel_id=1, source_target_pairs={{0,4},{4,0},{1,5},{5,1},{2,6},{6,2},{3,7},{7,3},{8,12},{12,8},{9,1... | collective-permute-start | bytes 196616 | tf_op jit(solution)/shard_map/ppermute | solution.py:21
  33.5 6.6 %collective-permute-start.3 = (bf16[256,256]{1,0:T(8,128)(2,1)S(1)}, bf16[256,256]{1,0:T(8,128)(2,1)S(1)}, u32[]{:S(2)}, u32[]{:S(2)}) collective-permute-start(bf16[256,256]{1,0:T(8,128)(2,1)S(1)} %pad_maximum_fusion.1), channel_id=1, source_target_pairs={{0,8},{8,0},{1,9},{9,1},{2,10},{10,2},{3,11},{11,3},{4,12},{12,4},... | collective-permute-start | bytes 393224 | tf_op jit(solution)/shard_map/ppermute | solution.py:21
  41.9 1.9 %collective-permute-start.7 = (bf16[512,512]{1,0:T(8,128)(2,1)S(1)}, bf16[512,512]{1,0:T(8,128)(2,1)S(1)}, u32[]{:S(2)}, u32[]{:S(2)}) collective-permute-start(bf16[512,512]{1,0:T(8,128)(2,1)S(1)} %bitcast.55), channel_id=1, source_target_pairs={{0,1},{1,0},{2,3},{3,2},{4,5},{5,4},{6,7},{7,6},{8,9},{9,8},{10,11... | collective-permute-start | bytes 1572872 | tf_op jit(solution)/shard_map/ppermute | solution.py:132
  44.8 9.1 %copy-start.2 = (bf16[512,128]{1,0:T(8,128)(2,1)S(1)}, bf16[512,128]{1,0:T(8,128)(2,1)}, u32[]{:S(2)}) copy-start(bf16[512,128]{1,0:T(8,128)(2,1)} %get-tuple-element.34) | copy-start | bytes 393220
  44.8 9.7 %copy-start.1 = (bf16[512,128]{1,0:T(8,128)(2,1)S(1)}, bf16[512,128]{1,0:T(8,128)(2,1)}, u32[]{:S(2)}) copy-start(bf16[512,128]{1,0:T(8,128)(2,1)} %get-tuple-element.33) | copy-start | bytes 393220
  45.1 10.0 %collective-permute-start.14 = (bf16[512,128]{1,0:T(8,128)(2,1)S(1)}, bf16[512,128]{1,0:T(8,128)(2,1)S(1)}, u32[]{:S(2)}, u32[]{:S(2)}) collective-permute-start(bf16[512,128]{1,0:T(8,128)(2,1)S(1)} %convolution_convert_fusion), channel_id=1, source_target_pairs={{0,10},{2,8},{4,14},{6,12},{8,2},{10,0},{12,6},{14,4},{1,11},{3,9}... | collective-permute-start | bytes 393224 | tf_op jit(solution)/shard_map/ppermute | solution.py:17
  47.4 12.5 %collective-permute-start.13 = (bf16[512,128]{1,0:T(8,128)(2,1)S(1)}, bf16[512,128]{1,0:T(8,128)(2,1)S(1)}, u32[]{:S(2)}, u32[]{:S(2)}) collective-permute-start(bf16[512,128]{1,0:T(8,128)(2,1)S(1)} %convolution_convert_fusion.1), channel_id=1, source_target_pairs={{0,8},{2,10},{4,12},{6,14},{8,0},{10,2},{12,4},{14,6},{1,9},{3,11}... | collective-permute-start | bytes 393224 | tf_op jit(solution)/shard_map/ppermute | solution.py:17
  49.0 11.2 %collective-permute-start.12 = (bf16[512,128]{1,0:T(8,128)(2,1)S(1)}, bf16[512,128]{1,0:T(8,128)(2,1)S(1)}, u32[]{:S(2)}, u32[]{:S(2)}) collective-permute-start(bf16[512,128]{1,0:T(8,128)(2,1)S(1)} %convolution_convert_fusion.2), channel_id=1, source_target_pairs={{0,14},{2,12},{4,10},{6,8},{8,6},{10,4},{12,2},{14,0},{1,15},{3,13... | collective-permute-start | bytes 393224 | tf_op jit(solution)/shard_map/ppermute | solution.py:17
  52.3 8.1 %collective-permute-start.11 = (bf16[512,128]{1,0:T(8,128)(2,1)S(1)}, bf16[512,128]{1,0:T(8,128)(2,1)S(1)}, u32[]{:S(2)}, u32[]{:S(2)}) collective-permute-start(bf16[512,128]{1,0:T(8,128)(2,1)S(1)} %convolution_convert_fusion.3), channel_id=1, source_target_pairs={{0,6},{2,4},{4,2},{6,0},{8,14},{10,12},{12,10},{14,8},{1,7},{3,5},... | collective-permute-start | bytes 393224 | tf_op jit(solution)/shard_map/ppermute | solution.py:17
  54.2 7.3 %collective-permute-start.10 = (bf16[512,128]{1,0:T(8,128)(2,1)S(1)}, bf16[512,128]{1,0:T(8,128)(2,1)S(1)}, u32[]{:S(2)}, u32[]{:S(2)}) collective-permute-start(bf16[512,128]{1,0:T(8,128)(2,1)S(1)} %convolution_convert_fusion.4), channel_id=1, source_target_pairs={{0,12},{2,14},{4,8},{6,10},{8,4},{10,6},{12,0},{14,2},{1,13},{3,15... | collective-permute-start | bytes 393224 | tf_op jit(solution)/shard_map/ppermute | solution.py:17
  54.8 28.5 %copy-start.14 = (f32[4]{0:T(128)S(1)}, f32[4]{0:T(128)}, u32[]{:S(2)}) copy-start(f32[4]{0:T(128)} %param.19) | copy-start | bytes 52
  55.1 7.3 %collective-permute-start.9 = (bf16[512,128]{1,0:T(8,128)(2,1)S(1)}, bf16[512,128]{1,0:T(8,128)(2,1)S(1)}, u32[]{:S(2)}, u32[]{:S(2)}) collective-permute-start(bf16[512,128]{1,0:T(8,128)(2,1)S(1)} %convolution_convert_fusion.5), channel_id=1, source_target_pairs={{0,4},{2,6},{4,0},{6,2},{8,12},{10,14},{12,8},{14,10},{1,5},{3,7},... | collective-permute-start | bytes 393224 | tf_op jit(solution)/shard_map/ppermute | solution.py:17
  60.0 5.3 %collective-permute-start.8 = (bf16[512,128]{1,0:T(8,128)(2,1)S(1)}, bf16[512,128]{1,0:T(8,128)(2,1)S(1)}, u32[]{:S(2)}, u32[]{:S(2)}) collective-permute-start(bf16[512,128]{1,0:T(8,128)(2,1)S(1)} %convolution_convert_fusion.6), channel_id=1, source_target_pairs={{0,2},{2,0},{4,6},{6,4},{8,10},{10,8},{12,14},{14,12},{1,3},{3,1},... | collective-permute-start | bytes 393224 | tf_op jit(solution)/shard_map/ppermute | solution.py:17
  65.4 7.3 %collective-permute-start.15 = (bf16[128,512]{1,0:T(8,128)(2,1)S(1)}, bf16[128,512]{1,0:T(8,128)(2,1)S(1)}, u32[]{:S(2)}, u32[]{:S(2)}) collective-permute-start(bf16[128,512]{1,0:T(8,128)(2,1)S(1)} %summed.1.refs_4_), channel_id=1, source_target_pairs={{0,16},{16,0},{32,48},{48,32},{1,17},{17,1},{33,49},{49,33},{2,18}... | collective-permute-start | bytes 393224 | tf_op jit(solution)/shard_map/ppermute | solution.py:17
  66.0 6.8 %collective-permute-start.16 = (bf16[128,512]{1,0:T(8,128)(2,1)S(1)}, bf16[128,512]{1,0:T(8,128)(2,1)S(1)}, u32[]{:S(2)}, u32[]{:S(2)}) collective-permute-start(bf16[128,512]{1,0:T(8,128)(2,1)S(1)} %summed.1.refs_4_), channel_id=1, source_target_pairs={{0,32},{16,48},{32,0},{48,16},{1,33},{17,49},{33,1},{49,17},{2,34}... | collective-permute-start | bytes 393224 | tf_op jit(solution)/shard_map/ppermute | solution.py:17
  67.8 8.1 %collective-permute-start.17 = (bf16[128,512]{1,0:T(8,128)(2,1)S(1)}, bf16[128,512]{1,0:T(8,128)(2,1)S(1)}, u32[]{:S(2)}, u32[]{:S(2)}) collective-permute-start(bf16[128,512]{1,0:T(8,128)(2,1)S(1)} %summed.1.refs_4_), channel_id=1, source_target_pairs={{0,48},{16,32},{32,16},{48,0},{1,49},{17,33},{33,17},{49,1},{2,50}... | collective-permute-start | bytes 393224 | tf_op jit(solution)/shard_map/ppermute | solution.py:17
  76.6 10.4 %collective-permute-start.18 = (bf16[128,512]{1,0:T(8,128)(2,1)S(1)}, bf16[128,512]{1,0:T(8,128)(2,1)S(1)}, u32[]{:S(2)}, u32[]{:S(2)}) collective-permute-start(bf16[128,512]{1,0:T(8,128)(2,1)S(1)} %get-tuple-element.40), channel_id=1, source_target_pairs={{0,64},{64,0},{128,192},{192,128},{1,65},{65,1},{129,193},{193,129... | collective-permute-start | bytes 393224 | tf_op jit(solution)/shard_map/ppermute | solution.py:17
  78.8 11.6 %collective-permute-start.19 = (bf16[128,512]{1,0:T(8,128)(2,1)S(1)}, bf16[128,512]{1,0:T(8,128)(2,1)S(1)}, u32[]{:S(2)}, u32[]{:S(2)}) collective-permute-start(bf16[128,512]{1,0:T(8,128)(2,1)S(1)} %get-tuple-element.41), channel_id=1, source_target_pairs={{0,128},{64,192},{128,0},{192,64},{1,129},{65,193},{129,1},{193,65... | collective-permute-start | bytes 393224 | tf_op jit(solution)/shard_map/ppermute | solution.py:17
  80.8 13.5 %collective-permute-start.20 = (bf16[128,512]{1,0:T(8,128)(2,1)S(1)}, bf16[128,512]{1,0:T(8,128)(2,1)S(1)}, u32[]{:S(2)}, u32[]{:S(2)}) collective-permute-start(bf16[128,512]{1,0:T(8,128)(2,1)S(1)} %get-tuple-element.42), channel_id=1, source_target_pairs={{0,192},{64,128},{128,64},{192,0},{1,193},{65,129},{129,65},{193,1... | collective-permute-start | bytes 393224 | tf_op jit(solution)/shard_map/ppermute | solution.py:17
  (5 other events, 24.5 us)

commit v3 on v2

v3 whole, which is shorter than its diff:
```python
import jax
import jax.numpy as jnp
from jax import lax
from jax.experimental import pallas as pl
from jax.experimental.pallas import tpu as pltpu
from jax.sharding import Mesh
from jax.sharding import PartitionSpec as P


ROW = ("z2", "z1", "z0", "xh")
COL = ("y2", "y1", "xl")
SWAP = [(0, 1), (1, 0)]
SMALL = pltpu.CompilerParams(vmem_limit_bytes=6 * 2**20)


def exchange(block, axes, mask):
    return lax.ppermute(block, axes, [(i, i ^ mask) for i in range(lax.axis_size(axes))])


def doubled(block, axis):
    other = lax.ppermute(block, axis, SWAP)
    low = lax.axis_index(axis) == 0
    return jnp.concatenate([jnp.where(low, block, other), jnp.where(low, other, block)], axis=0)


def vmem(count):
    return [pl.BlockSpec(memory_space=pltpu.VMEM)] * count


SCALARS = pl.BlockSpec(memory_space=pltpu.SMEM)


def scale_kernel(place, rows, factor_a, factor_b, scaled_a, scaled_b):
    for m2 in range(4):
        ats = [pl.ds(pl.multiple_of(((place[0] ^ m1) * 4 + (place[1] ^ m2)) * 32, 32), 32) for m1 in range(4)]
        block = jnp.concatenate([rows[at, :] for at in ats], axis=0).astype(jnp.float32)
        for kind, factor, scaled in ((0, factor_a, scaled_a), (1, factor_b, scaled_b)):
            piece = block[:, kind * 128 : kind * 128 + 128].T
            gains = jnp.concatenate([factor[at, :] for at in ats], axis=0).T
            for t in range(4):
                made = piece * gains[t : t + 1, :]
                scaled[t * 128 : t * 128 + 128, m2 * 128 : m2 * 128 + 128] = made.astype(jnp.bfloat16)


def scaled_rows(place, rows, factor_a, factor_b):
    return pl.pallas_call(
        scale_kernel,
        name="scaled_rows",
        out_shape=[jax.ShapeDtypeStruct((512, 512), jnp.bfloat16)] * 2,
        in_specs=[SCALARS] + vmem(3),
        out_specs=vmem(2),
        compiler_params=SMALL,
        cost_estimate=pl.CostEstimate(flops=1_000_000, bytes_accessed=1_800_000, transcendentals=0),
    )(place, rows, factor_a, factor_b)


def copy_kernel(core, block, out):
    out[...] = block[...]


def halved(core, aux_cols):
    return pl.pallas_call(
        copy_kernel,
        name="halved",
        out_shape=jax.ShapeDtypeStruct((512, 1024), jnp.bfloat16),
        grid_spec=pltpu.PrefetchScalarGridSpec(
            num_scalar_prefetch=1,
            grid=(8,),
            in_specs=[pl.BlockSpec((512, 128), lambda j, core: (0, 2 * j + core[0]))],
            out_specs=pl.BlockSpec((512, 128), lambda j, core: (0, j)),
        ),
        compiler_params=SMALL,
        cost_estimate=pl.CostEstimate(flops=0, bytes_accessed=2_000_000, transcendentals=0),
    )(core, aux_cols)


def right_kernel(scaled_a, scaled_b, *refs):
    arrived_a, arrived_b, (aux, out, cols_a, cols_b) = refs[:4], refs[4:8], refs[8:]
    for m in range(4):
        cols_a[m * 128 : m * 128 + 128, :] = arrived_a[m][...]
        cols_b[m * 128 : m * 128 + 128, :] = arrived_b[m][...]
    for t in range(4):
        here = slice(t * 128, t * 128 + 128)
        green_a = jnp.dot(scaled_a[here, :], cols_a[...], preferred_element_type=jnp.float32)
        green_b = jnp.dot(scaled_b[here, :], cols_b[...], preferred_element_type=jnp.float32)
        chi = (green_a * green_b).astype(jnp.bfloat16)
        right = jnp.dot(chi, aux[...], preferred_element_type=jnp.float32).astype(jnp.bfloat16)
        for j in range(8):
            out[j, here, :] = right[:, j * 128 : j * 128 + 128]


def right_parts(scaled_a, scaled_b, cols_a, cols_b, aux):
    return pl.pallas_call(
        right_kernel,
        name="right_parts",
        out_shape=jax.ShapeDtypeStruct((8, 512, 128), jnp.bfloat16),
        in_specs=vmem(11),
        out_specs=vmem(1)[0],
        scratch_shapes=[pltpu.VMEM((512, 512), jnp.bfloat16)] * 2,
        compiler_params=pltpu.CompilerParams(vmem_limit_bytes=12 * 2**20),
        cost_estimate=pl.CostEstimate(flops=1_070_000_000, bytes_accessed=5_000_000, transcendentals=0),
    )(scaled_a, scaled_b, *cols_a, *cols_b, aux)


def turn_kernel(place, aux, mine, theirs):
    for blocks, xh in ((mine, place[2]), (theirs, 1 - place[2])):
        for n in range(8):
            at = pl.ds(pl.multiple_of((2 * n + xh) * 128, 128), 128)
            blocks[n] = aux[:, at].T


def turned(place, aux_rows):
    return pl.pallas_call(
        turn_kernel,
        name="turned",
        out_shape=[jax.ShapeDtypeStruct((8, 128, 128), jnp.bfloat16)] * 2,
        in_specs=[SCALARS] + vmem(1),
        out_specs=vmem(2),
        compiler_params=SMALL,
        cost_estimate=pl.CostEstimate(flops=500_000, bytes_accessed=1_000_000, transcendentals=0),
    )(place, aux_rows)


def sum_kernel(parts, out):
    for t in range(4):
        here = slice(t * 128, t * 128 + 128)
        out[:, here] = sum(parts[j, here, :].astype(jnp.float32) for j in range(8)).astype(jnp.bfloat16)


def summed(parts):
    return pl.pallas_call(
        sum_kernel,
        name="summed",
        out_shape=jax.ShapeDtypeStruct((128, 512), jnp.bfloat16),
        in_specs=vmem(1),
        out_specs=vmem(1)[0],
        compiler_params=SMALL,
        cost_estimate=pl.CostEstimate(flops=500_000, bytes_accessed=1_300_000, transcendentals=0),
    )(parts)


def left_kernel(place, mine, xh_aux, z_aux, *refs):
    right, outs, (left, stacked) = refs[:4], refs[4:8], refs[8:]
    for m in range(4):
        stacked[m * 128 : m * 128 + 128, :] = right[m][...]
    for e in range(4):
        p = place[0] ^ e
        blocks = (mine[2 * p + place[3]], xh_aux[2 * p + place[3]], z_aux[0, p], z_aux[1, p])
        for m, block in enumerate(blocks):
            left[e * 128 : e * 128 + 128, m * 128 : m * 128 + 128] = block
    made = jnp.dot(left[...], stacked[...], preferred_element_type=jnp.float32)
    for e in range(4):
        outs[e][...] = made[e * 128 : e * 128 + 128, :].astype(outs[e].dtype)


def left_parts(place, mine, xh_aux, z_aux, right):
    return pl.pallas_call(
        left_kernel,
        name="left_parts",
        out_shape=[jax.ShapeDtypeStruct((128, 512), jnp.bfloat16 if e else jnp.float32) for e in range(4)],
        in_specs=[SCALARS] + vmem(7),
        out_specs=vmem(4),
        scratch_shapes=[pltpu.VMEM((512, 512), jnp.bfloat16)] * 2,
        compiler_params=SMALL,
        cost_estimate=pl.CostEstimate(flops=270_000_000, bytes_accessed=1_700_000, transcendentals=0),
    )(place, mine, xh_aux, z_aux, *right)


def mix_kernel(coef, *refs):
    parts, out = refs[:4], refs[4]
    whole = [sum(part[:, t * 128 : t * 128 + 128].astype(jnp.float32) for part in parts) for t in range(4)]
    for w in range(4):
        out[w] = sum(coef[w, t] * whole[t] for t in range(4))


def mix(coef, parts):
    return pl.pallas_call(
        mix_kernel,
        name="mix",
        out_shape=jax.ShapeDtypeStruct((4, 128, 128), jnp.float32),
        in_specs=[SCALARS] + vmem(4),
        out_specs=vmem(1)[0],
        compiler_params=SMALL,
    )(coef, *parts)


def per_device(
    occ_rows,
    occ_cols,
    emp_rows,
    emp_cols,
    occ_gap,
    emp_gap,
    times,
    time_weights,
    freqs,
    aux_rows,
    aux_cols,
):
    core = lax.axis_index("tm")
    first = core == 0
    z2, z1, z0, xh = (lax.axis_index(a) for a in ROW)
    place = jnp.stack([2 * z2 + z1, 2 * z0 + xh, xh, z0]).astype(jnp.int32)

    cols = jnp.where(first, occ_cols, emp_cols).T
    cols = jnp.concatenate([cols] + [exchange(cols, ("z2", "z1"), m) for m in (1, 2, 3)], axis=0)
    cols_a = [cols] + [exchange(cols, ("z0", "xh"), m) for m in (1, 2, 3)]
    cols_b = [lax.ppermute(c, "tm", SWAP) for c in cols_a]

    rows = jnp.where(first, occ_rows, emp_rows).T, jnp.where(first, emp_rows, occ_rows).T
    rows = jnp.concatenate(rows, axis=1)
    for axis in reversed(COL):
        rows = doubled(rows, axis)

    mine = jnp.stack([times, time_weights])
    other = lax.ppermute(mine, "tm", SWAP)
    every = jnp.concatenate([jnp.where(first, mine, other), jnp.where(first, other, mine)], axis=1)
    coef = every[1][None, :] * jnp.cos(freqs[:, None] * every[0][None, :])

    moments = jnp.tile(every[0], 32)
    factor_a = jnp.exp(-jnp.where(first, occ_gap, emp_gap)[:, None] * moments[None, :])
    factor_b = jnp.exp(-jnp.where(first, emp_gap, occ_gap)[:, None] * moments[None, :])
    scaled_a, scaled_b = scaled_rows(place, rows, factor_a, factor_b)

    mine, theirs = turned(place, aux_rows)
    xh_aux = exchange(theirs, "xh", 1)

    parts = right_parts(scaled_a, scaled_b, cols_a, cols_b, halved(core.astype(jnp.int32).reshape(1), aux_cols))
    parts = lax.all_to_all(parts, COL, 0, 0, tiled=True)

    z_aux = jnp.stack([mine, xh_aux]).reshape(2, 4, 2, 128, 128)
    z_aux = lax.dynamic_index_in_dim(z_aux, 1 - z0, 2, keepdims=False)
    z_aux = exchange(z_aux, "z0", 1)

    right = summed(parts)
    right = [right] + [exchange(right, ("z0", "xh"), m) for m in (1, 2, 3)]
    parts = left_parts(place, mine, xh_aux, z_aux, right)
    parts = [parts[0]] + [exchange(parts[e], ("z2", "z1"), e) for e in (1, 2, 3)]
    return mix(coef, parts)


def solution(mesh):
    torus = Mesh(mesh.devices.reshape((2,) * 8), (*ROW, *COL, "tm"))
    return jax.shard_map(
        per_device,
        mesh=torus,
        in_specs=(
            P(ROW, COL),
            P(COL, ROW),
            P(ROW, COL),
            P(COL, ROW),
            P(),
            P(),
            P("tm"),
            P("tm"),
            P(),
            P(ROW, None),
            P(COL, None),
        ),
        out_specs=P(None, ROW, (*COL, "tm")),
        check_vma=False,
    )
```

time: 96.1 us -> 90 us (0.937)
  the two profiles are of different devices: /device:TPU:40 before, /device:TPU:32 now
where the time goes in v3:
time: 90 us; the launch traced here: 89.6 us
  starting transfers between devices  39.9 us (44%)
  waiting for transfers between devices  36.7 us (41%)
  Pallas kernels  7.53 us (8%)
  other arithmetic  3.57 us (4%)
  local copies, waits for them, and re-layouts  1.73 us (2%)
    ppermute x14, waiting for transfers between devices, exchange(): lax.ppermute(block, axes, [(i, i ^ mask) for i in range(lax.axis_size(axe...  36.2 us
    ppermute x14, starting transfers between devices, exchange(): lax.ppermute(block, axes, [(i, i ^ mask) for i in range(lax.axis_size(axe...  28.9 us
    ppermute x3, starting transfers between devices, doubled(): other = lax.ppermute(block, axis, SWAP)  6.23 us
    all_to_all x1, starting transfers between devices, per_device(): parts = lax.all_to_all(parts, COL, 0, 0, tiled=True)  4.19 us
    pallas_call x1, Pallas kernels, right_parts(): pl.pallas_call(right_kernel, name='right_parts', out_shape=jax.ShapeDtype...  2.7 us
  transfers between devices with their start and end apart: 23, of which 10 were waited for; matrix products, arithmetic and copies ran while one was open for 3% of the time, Pallas kernels for 3%

profile of v3, /device:TPU:32, one launch (start us, length us, event | category | flops | bytes accessed | tf_op | source)
XLA Modules:
  0.0 89.6 jit_solution(3349636781318226677)
XLA Ops:
  0.0 0.8 select_bitcast_fusion
  0.8 3.3 %collective-permute-start.6 = (bf16[32,512]{1,0:T(8,128)(2,1)S(1)}, bf16[32,512]{1,0:T(8,128)(2,1)S(1)}, u32[]{:S(2)}, u32[]{:S(2)}) collective-permute-start(bf16[32,512]{1,0:T(8,128)(2,1)S(1)} %select_bitcast_fusion), channel_id=1, source_target_pairs={{0,64},{64,0},{128,192},{192,128},{1,65},{65,1},{129,193},{193,129... | collective-permute-start | bytes 98312 | tf_op jit(solution)/shard_map/ppermute | solution.py:17
  4.1 4.5 %collective-permute-start.7 = (bf16[32,512]{1,0:T(8,128)(2,1)S(1)}, bf16[32,512]{1,0:T(8,128)(2,1)S(1)}, u32[]{:S(2)}, u32[]{:S(2)}) collective-permute-start(bf16[32,512]{1,0:T(8,128)(2,1)S(1)} %select_bitcast_fusion), channel_id=1, source_target_pairs={{0,128},{64,192},{128,0},{192,64},{1,129},{65,193},{129,1},{193,65... | collective-permute-start | bytes 98312 | tf_op jit(solution)/shard_map/ppermute | solution.py:17
  8.6 0.7 select_bitcast_fusion.2
  9.3 1.6 %collective-permute-start.3 = (bf16[64,256]{1,0:T(8,128)(2,1)S(1)}, bf16[64,256]{1,0:T(8,128)(2,1)S(1)}, u32[]{:S(2)}, u32[]{:S(2)}) collective-permute-start(bf16[64,256]{1,0:T(8,128)(2,1)S(1)} %pad_maximum_fusion.4), channel_id=1, source_target_pairs={{0,2},{2,0},{1,3},{3,1},{4,6},{6,4},{5,7},{7,5},{8,10},{10,8},{9,1... | collective-permute-start | bytes 98312 | tf_op jit(solution)/shard_map/ppermute | solution.py:21
  12.3 1.6 %copy-done = bf16[512,2048]{1,0:T(8,128)(2,1)S(1)} copy-done((bf16[512,2048]{1,0:T(8,128)(2,1)S(1)}, bf16[512,2048]{1,0:T(8,128)(2,1)}, u32[]{:S(2)}) %copy-start) | copy-done | bytes 2097176
  13.9 0.7 halved.1.refs_8_
  15.0 1.7 %collective-permute-start.4 = (bf16[128,256]{1,0:T(8,128)(2,1)S(1)}, bf16[128,256]{1,0:T(8,128)(2,1)S(1)}, u32[]{:S(2)}, u32[]{:S(2)}) collective-permute-start(bf16[128,256]{1,0:T(8,128)(2,1)S(1)} %pad_maximum_fusion.3), channel_id=1, source_target_pairs={{0,4},{4,0},{1,5},{5,1},{2,6},{6,2},{3,7},{7,3},{8,12},{12,8},{9,1... | collective-permute-start | bytes 196616 | tf_op jit(solution)/shard_map/ppermute | solution.py:21
  16.7 2.8 %collective-permute-start.9 = (bf16[128,512]{1,0:T(8,128)(2,1)S(1)}, bf16[128,512]{1,0:T(8,128)(2,1)S(1)}, u32[]{:S(2)}, u32[]{:S(2)}) collective-permute-start(bf16[128,512]{1,0:T(8,128)(2,1)S(1)} %pad_maximum_fusion.2.refs_0_), channel_id=1, source_target_pairs={{0,16},{16,0},{32,48},{48,32},{1,17},{17,1},{33,49},{49,33},{2,18}... | collective-permute-start | bytes 393224 | tf_op jit(solution)/shard_map/ppermute | solution.py:17
  19.5 1.0 %collective-permute-start.10 = (bf16[128,512]{1,0:T(8,128)(2,1)S(1)}, bf16[128,512]{1,0:T(8,128)(2,1)S(1)}, u32[]{:S(2)}, u32[]{:S(2)}) collective-permute-start(bf16[128,512]{1,0:T(8,128)(2,1)S(1)} %pad_maximum_fusion.2.refs_0_), channel_id=1, source_target_pairs={{0,32},{16,48},{32,0},{48,16},{1,33},{17,49},{33,1},{49,17},{2,34}... | collective-permute-start | bytes 393224 | tf_op jit(solution)/shard_map/ppermute | solution.py:17
  20.5 1.3 %collective-permute-start.11 = (bf16[128,512]{1,0:T(8,128)(2,1)S(1)}, bf16[128,512]{1,0:T(8,128)(2,1)S(1)}, u32[]{:S(2)}, u32[]{:S(2)}) collective-permute-start(bf16[128,512]{1,0:T(8,128)(2,1)S(1)} %pad_maximum_fusion.2.refs_0_), channel_id=1, source_target_pairs={{0,48},{16,32},{32,16},{48,0},{1,49},{17,33},{33,17},{49,1},{2,50}... | collective-permute-start | bytes 393224 | tf_op jit(solution)/shard_map/ppermute | solution.py:17
  21.8 3.0 %collective-permute-start.5 = (bf16[256,256]{1,0:T(8,128)(2,1)S(1)}, bf16[256,256]{1,0:T(8,128)(2,1)S(1)}, u32[]{:S(2)}, u32[]{:S(2)}) collective-permute-start(bf16[256,256]{1,0:T(8,128)(2,1)S(1)} %pad_maximum_fusion.1), channel_id=1, source_target_pairs={{0,8},{8,0},{1,9},{9,1},{2,10},{10,2},{3,11},{11,3},{4,12},{12,4},... | collective-permute-start | bytes 393224 | tf_op jit(solution)/shard_map/ppermute | solution.py:21
  25.9 2.1 %collective-permute-done.11.refs_3_ = bf16[128,512]{1,0:T(8,128)(2,1)S(1)} collective-permute-done((bf16[128,512]{1,0:T(8,128)(2,1)S(1)}, bf16[128,512]{1,0:T(8,128)(2,1)S(1)}, u32[]{:S(2)}, u32[]{:S(2)}) %collective-permute-start.11) | collective-permute-done | bytes 131104 | tf_op jit(solution)/shard_map/ppermute | solution.py:17
  28.5 0.8 scaled_rows.1
  29.4 2.7 %right_parts.1 = bf16[8,512,128]{2,1,0:T(8,128)(2,1)} custom-call(bf16[512,512]{1,0:T(8,128)(2,1)S(1)} %get-tuple-element.15.scaled_a, bf16[512,512]{1,0:T(8,128)(2,1)S(1)} %get-tuple-element.16.scaled_b, bf16[128,512]{1,0:T(8,128)(2,1)S(1)} %pad_maximum_fusion.2.refs_0_, bf16[128,512]{1,0:T(8,128)(2,1)S(1)} %collective-permute-done.9.refs_1_, ...), custom_call_target="tpu_custom_call" | custom-call | flops 1070000000 | bytes 5000000 | tf_op jit(solution)/shard_map/right_parts/pallas_call | solution.py:93
  32.1 4.2 %all-to-all-start = ((bf16[8,512,128]{2,1,0:T(8,128)(2,1)}), bf16[8,512,128]{2,1,0:T(8,128)(2,1)S(1)}, u32[]{:S(2)}, u32[]{:S(2)}) async-start(bf16[8,512,128]{2,1,0:T(8,128)(2,1)} %right_parts.1), calls=%async_computation | async-start | bytes 2097152 | tf_op jit(solution)/shard_map/all_to_all | solution.py:229
  37.0 3.1 %collective-permute-start.1 = (bf16[8,128,128]{2,1,0:T(8,128)(2,1)S(1)}, bf16[8,128,128]{2,1,0:T(8,128)(2,1)S(1)}, u32[]{:S(2)}, u32[]{:S(2)}) collective-permute-start(bf16[8,128,128]{2,1,0:T(8,128)(2,1)S(1)} %get-tuple-element.14), channel_id=1, source_target_pairs={{0,16},{16,0},{1,17},{17,1},{2,18},{18,2},{3,19},{19,3},{4,20},{20... | collective-permute-start | bytes 786440 | tf_op jit(solution)/shard_map/ppermute | solution.py:17
  40.1 16.8 %collective-permute-done.1.xh_aux = bf16[8,128,128]{2,1,0:T(8,128)(2,1)S(1)} collective-permute-done((bf16[8,128,128]{2,1,0:T(8,128)(2,1)S(1)}, bf16[8,128,128]{2,1,0:T(8,128)(2,1)S(1)}, u32[]{:S(2)}, u32[]{:S(2)}) %collective-permute-start.1) | collective-permute-done | bytes 262176 | tf_op jit(solution)/shard_map/ppermute | solution.py:17
  57.0 1.1 %collective-permute-start.2 = (bf16[2,4,128,128]{3,2,1,0:T(8,128)(2,1)S(1)}, bf16[2,4,128,128]{3,2,1,0:T(8,128)(2,1)S(1)}, u32[]{:S(2)}, u32[]{:S(2)}) collective-permute-start(bf16[2,4,128,128]{3,2,1,0:T(8,128)(2,1)S(1)} %fusion.1), channel_id=1, source_target_pairs={{0,32},{32,0},{1,33},{33,1},{2,34},{34,2},{3,35},{35,3},{4,36},{36... | collective-permute-start | bytes 786440 | tf_op jit(solution)/shard_map/ppermute | solution.py:17
  58.2 0.9 %collective-permute-start.16 = (bf16[128,512]{1,0:T(8,128)(2,1)S(1)}, bf16[128,512]{1,0:T(8,128)(2,1)S(1)}, u32[]{:S(2)}, u32[]{:S(2)}) collective-permute-start(bf16[128,512]{1,0:T(8,128)(2,1)S(1)} %summed.1.refs_0_), channel_id=1, source_target_pairs={{0,16},{16,0},{32,48},{48,32},{1,17},{17,1},{33,49},{49,33},{2,18}... | collective-permute-start | bytes 393224 | tf_op jit(solution)/shard_map/ppermute | solution.py:17
  59.1 1.0 %collective-permute-start.17 = (bf16[128,512]{1,0:T(8,128)(2,1)S(1)}, bf16[128,512]{1,0:T(8,128)(2,1)S(1)}, u32[]{:S(2)}, u32[]{:S(2)}) collective-permute-start(bf16[128,512]{1,0:T(8,128)(2,1)S(1)} %summed.1.refs_0_), channel_id=1, source_target_pairs={{0,32},{16,48},{32,0},{48,16},{1,33},{17,49},{33,1},{49,17},{2,34}... | collective-permute-start | bytes 393224 | tf_op jit(solution)/shard_map/ppermute | solution.py:17
  60.1 3.4 %collective-permute-start.18 = (bf16[128,512]{1,0:T(8,128)(2,1)S(1)}, bf16[128,512]{1,0:T(8,128)(2,1)S(1)}, u32[]{:S(2)}, u32[]{:S(2)}) collective-permute-start(bf16[128,512]{1,0:T(8,128)(2,1)S(1)} %summed.1.refs_0_), channel_id=1, source_target_pairs={{0,48},{16,32},{32,16},{48,0},{1,49},{17,33},{33,17},{49,1},{2,50}... | collective-permute-start | bytes 393224 | tf_op jit(solution)/shard_map/ppermute | solution.py:17
  63.5 2.8 %collective-permute-done.2.z_aux = bf16[2,4,128,128]{3,2,1,0:T(8,128)(2,1)S(1)} collective-permute-done((bf16[2,4,128,128]{3,2,1,0:T(8,128)(2,1)S(1)}, bf16[2,4,128,128]{3,2,1,0:T(8,128)(2,1)S(1)}, u32[]{:S(2)}, u32[]{:S(2)}) %collective-permute-start.2) | collective-permute-done | bytes 262176 | tf_op jit(solution)/shard_map/ppermute | solution.py:17
  66.2 2.4 %collective-permute-done.17.refs_2_ = bf16[128,512]{1,0:T(8,128)(2,1)S(1)} collective-permute-done((bf16[128,512]{1,0:T(8,128)(2,1)S(1)}, bf16[128,512]{1,0:T(8,128)(2,1)S(1)}, u32[]{:S(2)}, u32[]{:S(2)}) %collective-permute-start.17) | collective-permute-done | bytes 131104 | tf_op jit(solution)/shard_map/ppermute | solution.py:17
  68.6 1.5 %collective-permute-done.18.refs_3_ = bf16[128,512]{1,0:T(8,128)(2,1)S(1)} collective-permute-done((bf16[128,512]{1,0:T(8,128)(2,1)S(1)}, bf16[128,512]{1,0:T(8,128)(2,1)S(1)}, u32[]{:S(2)}, u32[]{:S(2)}) %collective-permute-start.18) | collective-permute-done | bytes 131104 | tf_op jit(solution)/shard_map/ppermute | solution.py:17
  70.2 1.0 %left_parts.1 = (f32[128,512]{1,0:T(8,128)S(1)}, bf16[128,512]{1,0:T(8,128)(2,1)S(1)}, bf16[128,512]{1,0:T(8,128)(2,1)S(1)}, bf16[128,512]{1,0:T(8,128)(2,1)S(1)}) custom-call(s32[4]{0:T(128)S(1)} %pad_add_fusion.place, bf16[8,128,128]{2,1,0:T(8,128)(2,1)S(1)} %get-tuple-element.13.mine, bf16[8,128,128]{2,1,0:T(8,128)(2,1)S(1)} %collective-permute-done.1.xh_aux, ...), custom_call_target="tpu_custom_call" | custom-call | flops 270000000 | bytes 1700000 | tf_op jit(solution)/shard_map/left_parts/pallas_call | solution.py:157
  71.2 1.9 %collective-permute-start.19 = (bf16[128,512]{1,0:T(8,128)(2,1)S(1)}, bf16[128,512]{1,0:T(8,128)(2,1)S(1)}, u32[]{:S(2)}, u32[]{:S(2)}) collective-permute-start(bf16[128,512]{1,0:T(8,128)(2,1)S(1)} %get-tuple-element.18), channel_id=1, source_target_pairs={{0,64},{64,0},{128,192},{192,128},{1,65},{65,1},{129,193},{193,129... | collective-permute-start | bytes 393224 | tf_op jit(solution)/shard_map/ppermute | solution.py:17
  73.1 4.7 %collective-permute-start.20 = (bf16[128,512]{1,0:T(8,128)(2,1)S(1)}, bf16[128,512]{1,0:T(8,128)(2,1)S(1)}, u32[]{:S(2)}, u32[]{:S(2)}) collective-permute-start(bf16[128,512]{1,0:T(8,128)(2,1)S(1)} %get-tuple-element.19), channel_id=1, source_target_pairs={{0,128},{64,192},{128,0},{192,64},{1,129},{65,193},{129,1},{193,65... | collective-permute-start | bytes 393224 | tf_op jit(solution)/shard_map/ppermute | solution.py:17
  77.9 2.6 %collective-permute-done.19.refs_1_ = bf16[128,512]{1,0:T(8,128)(2,1)S(1)} collective-permute-done((bf16[128,512]{1,0:T(8,128)(2,1)S(1)}, bf16[128,512]{1,0:T(8,128)(2,1)S(1)}, u32[]{:S(2)}, u32[]{:S(2)}) %collective-permute-start.19) | collective-permute-done | bytes 131104 | tf_op jit(solution)/shard_map/ppermute | solution.py:17
  80.5 3.1 %collective-permute-done.20.refs_2_ = bf16[128,512]{1,0:T(8,128)(2,1)S(1)} collective-permute-done((bf16[128,512]{1,0:T(8,128)(2,1)S(1)}, bf16[128,512]{1,0:T(8,128)(2,1)S(1)}, u32[]{:S(2)}, u32[]{:S(2)}) %collective-permute-start.20) | collective-permute-done | bytes 131104 | tf_op jit(solution)/shard_map/ppermute | solution.py:17
  83.6 4.6 %collective-permute-done.21.refs_3_ = bf16[128,512]{1,0:T(8,128)(2,1)S(1)} collective-permute-done((bf16[128,512]{1,0:T(8,128)(2,1)S(1)}, bf16[128,512]{1,0:T(8,128)(2,1)S(1)}, u32[]{:S(2)}, u32[]{:S(2)}) %collective-permute-start.21) | collective-permute-done | bytes 131104 | tf_op jit(solution)/shard_map/ppermute | solution.py:17
  88.2 1.4 %mix.1 = f32[4,128,128]{2,1,0:T(8,128)} custom-call(f32[4,4]{1,0:T(4,128)S(1)} %cosine_multiply_fusion.coef, f32[128,512]{1,0:T(8,128)S(1)} %get-tuple-element.17.refs_0_, bf16[128,512]{1,0:T(8,128)(2,1)S(1)} %collective-permute-done.19.refs_1_, bf16[128,512]{1,0:T(8,128)(2,1)S(1)} %collective-permute-done.20.refs_2_, ...), custom_call_target="tpu_custom_call" | custom-call | tf_op jit(solution)/shard_map/mix/pallas_call | solution.py:177
  (52 shorter events, 4.4 us)
Async XLA Ops:
  0.0 14.7 %copy-start.3 = (f32[2]{0:T(128)S(1)}, f32[2]{0:T(128)}, u32[]{:S(2)}) copy-start(f32[2]{0:T(128)} %param.17) | copy-start | bytes 28
  0.0 14.7 %copy-start.2 = (f32[2]{0:T(128)S(1)}, f32[2]{0:T(128)}, u32[]{:S(2)}) copy-start(f32[2]{0:T(128)} %param.18) | copy-start | bytes 28
  0.8 15.9 %collective-permute-start.6 = (bf16[32,512]{1,0:T(8,128)(2,1)S(1)}, bf16[32,512]{1,0:T(8,128)(2,1)S(1)}, u32[]{:S(2)}, u32[]{:S(2)}) collective-permute-start(bf16[32,512]{1,0:T(8,128)(2,1)S(1)} %select_bitcast_fusion), channel_id=1, source_target_pairs={{0,64},{64,0},{128,192},{192,128},{1,65},{65,1},{129,193},{193,129... | collective-permute-start | bytes 98312 | tf_op jit(solution)/shard_map/ppermute | solution.py:17
  4.1 12.6 %collective-permute-start.7 = (bf16[32,512]{1,0:T(8,128)(2,1)S(1)}, bf16[32,512]{1,0:T(8,128)(2,1)S(1)}, u32[]{:S(2)}, u32[]{:S(2)}) collective-permute-start(bf16[32,512]{1,0:T(8,128)(2,1)S(1)} %select_bitcast_fusion), channel_id=1, source_target_pairs={{0,128},{64,192},{128,0},{192,64},{1,129},{65,193},{129,1},{193,65... | collective-permute-start | bytes 98312 | tf_op jit(solution)/shard_map/ppermute | solution.py:17
  8.6 8.1 %collective-permute-start.8 = (bf16[32,512]{1,0:T(8,128)(2,1)S(1)}, bf16[32,512]{1,0:T(8,128)(2,1)S(1)}, u32[]{:S(2)}, u32[]{:S(2)}) collective-permute-start(bf16[32,512]{1,0:T(8,128)(2,1)S(1)} %select_bitcast_fusion), channel_id=1, source_target_pairs={{0,192},{64,128},{128,64},{192,0},{1,193},{65,129},{129,65},{193,1... | collective-permute-start | bytes 98312 | tf_op jit(solution)/shard_map/ppermute | solution.py:17
  9.3 5.7 %collective-permute-start.3 = (bf16[64,256]{1,0:T(8,128)(2,1)S(1)}, bf16[64,256]{1,0:T(8,128)(2,1)S(1)}, u32[]{:S(2)}, u32[]{:S(2)}) collective-permute-start(bf16[64,256]{1,0:T(8,128)(2,1)S(1)} %pad_maximum_fusion.4), channel_id=1, source_target_pairs={{0,2},{2,0},{1,3},{3,1},{4,6},{6,4},{5,7},{7,5},{8,10},{10,8},{9,1... | collective-permute-start | bytes 98312 | tf_op jit(solution)/shard_map/ppermute | solution.py:21
  11.6 3.2 %collective-permute-start = (f32[2,2]{1,0:T(2,128)S(1)}, f32[2,2]{1,0:T(2,128)S(1)}, u32[]{:S(2)}, u32[]{:S(2)}) collective-permute-start(f32[2,2]{1,0:T(2,128)S(1)} %pad_maximum_fusion.5), channel_id=1, source_target_pairs={{0,1},{1,0},{2,3},{3,2},{4,5},{5,4},{6,7},{7,6},{8,9},{9,8},{10,11... | collective-permute-start | bytes 56 | tf_op jit(solution)/shard_map/ppermute | solution.py:216
  12.3 1.6 %copy-start = (bf16[512,2048]{1,0:T(8,128)(2,1)S(1)}, bf16[512,2048]{1,0:T(8,128)(2,1)}, u32[]{:S(2)}) copy-start(bf16[512,2048]{1,0:T(8,128)(2,1)} %block.1) | copy-start | bytes 6291460
  15.0 6.8 %collective-permute-start.4 = (bf16[128,256]{1,0:T(8,128)(2,1)S(1)}, bf16[128,256]{1,0:T(8,128)(2,1)S(1)}, u32[]{:S(2)}, u32[]{:S(2)}) collective-permute-start(bf16[128,256]{1,0:T(8,128)(2,1)S(1)} %pad_maximum_fusion.3), channel_id=1, source_target_pairs={{0,4},{4,0},{1,5},{5,1},{2,6},{6,2},{3,7},{7,3},{8,12},{12,8},{9,1... | collective-permute-start | bytes 196616 | tf_op jit(solution)/shard_map/ppermute | solution.py:21
  16.7 8.4 %collective-permute-start.9 = (bf16[128,512]{1,0:T(8,128)(2,1)S(1)}, bf16[128,512]{1,0:T(8,128)(2,1)S(1)}, u32[]{:S(2)}, u32[]{:S(2)}) collective-permute-start(bf16[128,512]{1,0:T(8,128)(2,1)S(1)} %pad_maximum_fusion.2.refs_0_), channel_id=1, source_target_pairs={{0,16},{16,0},{32,48},{48,32},{1,17},{17,1},{33,49},{49,33},{2,18}... | collective-permute-start | bytes 393224 | tf_op jit(solution)/shard_map/ppermute | solution.py:17
  19.5 6.4 %collective-permute-start.10 = (bf16[128,512]{1,0:T(8,128)(2,1)S(1)}, bf16[128,512]{1,0:T(8,128)(2,1)S(1)}, u32[]{:S(2)}, u32[]{:S(2)}) collective-permute-start(bf16[128,512]{1,0:T(8,128)(2,1)S(1)} %pad_maximum_fusion.2.refs_0_), channel_id=1, source_target_pairs={{0,32},{16,48},{32,0},{48,16},{1,33},{17,49},{33,1},{49,17},{2,34}... | collective-permute-start | bytes 393224 | tf_op jit(solution)/shard_map/ppermute | solution.py:17
  20.5 7.4 %collective-permute-start.11 = (bf16[128,512]{1,0:T(8,128)(2,1)S(1)}, bf16[128,512]{1,0:T(8,128)(2,1)S(1)}, u32[]{:S(2)}, u32[]{:S(2)}) collective-permute-start(bf16[128,512]{1,0:T(8,128)(2,1)S(1)} %pad_maximum_fusion.2.refs_0_), channel_id=1, source_target_pairs={{0,48},{16,32},{32,16},{48,0},{1,49},{17,33},{33,17},{49,1},{2,50}... | collective-permute-start | bytes 393224 | tf_op jit(solution)/shard_map/ppermute | solution.py:17
  21.8 6.6 %collective-permute-start.5 = (bf16[256,256]{1,0:T(8,128)(2,1)S(1)}, bf16[256,256]{1,0:T(8,128)(2,1)S(1)}, u32[]{:S(2)}, u32[]{:S(2)}) collective-permute-start(bf16[256,256]{1,0:T(8,128)(2,1)S(1)} %pad_maximum_fusion.1), channel_id=1, source_target_pairs={{0,8},{8,0},{1,9},{9,1},{2,10},{10,2},{3,11},{11,3},{4,12},{12,4},... | collective-permute-start | bytes 393224 | tf_op jit(solution)/shard_map/ppermute | solution.py:21
  25.0 4.3 %collective-permute-start.12 = (bf16[128,512]{1,0:T(8,128)(2,1)S(1)}, bf16[128,512]{1,0:T(8,128)(2,1)S(1)}, u32[]{:S(2)}, u32[]{:S(2)}) collective-permute-start(bf16[128,512]{1,0:T(8,128)(2,1)S(1)} %pad_maximum_fusion.2.refs_0_), channel_id=1, source_target_pairs={{0,1},{1,0},{2,3},{3,2},{4,5},{5,4},{6,7},{7,6},{8,9},{9,8},{10,11... | collective-permute-start | bytes 393224 | tf_op jit(solution)/shard_map/ppermute | solution.py:208
  25.1 4.2 %collective-permute-start.13 = (bf16[128,512]{1,0:T(8,128)(2,1)S(1)}, bf16[128,512]{1,0:T(8,128)(2,1)S(1)}, u32[]{:S(2)}, u32[]{:S(2)}) collective-permute-start(bf16[128,512]{1,0:T(8,128)(2,1)S(1)} %collective-permute-done.9.refs_1_), channel_id=1, source_target_pairs={{0,1},{1,0},{2,3},{3,2},{4,5},{5,4},{6,7},{7,6},{8,9},{9,8},{10,11... | collective-permute-start | bytes 393224 | tf_op jit(solution)/shard_map/ppermute | solution.py:208
  25.9 3.4 %collective-permute-start.14 = (bf16[128,512]{1,0:T(8,128)(2,1)S(1)}, bf16[128,512]{1,0:T(8,128)(2,1)S(1)}, u32[]{:S(2)}, u32[]{:S(2)}) collective-permute-start(bf16[128,512]{1,0:T(8,128)(2,1)S(1)} %collective-permute-done.10.refs_2_), channel_id=1, source_target_pairs={{0,1},{1,0},{2,3},{3,2},{4,5},{5,4},{6,7},{7,6},{8,9},{9,8},{10,11... | collective-permute-start | bytes 393224 | tf_op jit(solution)/shard_map/ppermute | solution.py:208
  28.0 1.4 %collective-permute-start.15 = (bf16[128,512]{1,0:T(8,128)(2,1)S(1)}, bf16[128,512]{1,0:T(8,128)(2,1)S(1)}, u32[]{:S(2)}, u32[]{:S(2)}) collective-permute-start(bf16[128,512]{1,0:T(8,128)(2,1)S(1)} %collective-permute-done.11.refs_3_), channel_id=1, source_target_pairs={{0,1},{1,0},{2,3},{3,2},{4,5},{5,4},{6,7},{7,6},{8,9},{9,8},{10,11... | collective-permute-start | bytes 393224 | tf_op jit(solution)/shard_map/ppermute | solution.py:208
  29.4 6.9 %copy-start.1 = (bf16[128,2048]{1,0:T(8,128)(2,1)S(1)}, bf16[128,2048]{1,0:T(8,128)(2,1)}, u32[]{:S(2)}) copy-start(bf16[128,2048]{1,0:T(8,128)(2,1)} %aux.1) | copy-start | bytes 1572868
  32.1 26.0 %all-to-all-start = ((bf16[8,512,128]{2,1,0:T(8,128)(2,1)}), bf16[8,512,128]{2,1,0:T(8,128)(2,1)S(1)}, u32[]{:S(2)}, u32[]{:S(2)}) async-start(bf16[8,512,128]{2,1,0:T(8,128)(2,1)} %right_parts.1), calls=%async_computation | async-start | bytes 2097152 | tf_op jit(solution)/shard_map/all_to_all | solution.py:229
  36.3 41.5 %copy-start.4 = (f32[4]{0:T(128)S(1)}, f32[4]{0:T(128)}, u32[]{:S(2)}) copy-start(f32[4]{0:T(128)} %param.19) | copy-start | bytes 52
  37.0 19.9 %collective-permute-start.1 = (bf16[8,128,128]{2,1,0:T(8,128)(2,1)S(1)}, bf16[8,128,128]{2,1,0:T(8,128)(2,1)S(1)}, u32[]{:S(2)}, u32[]{:S(2)}) collective-permute-start(bf16[8,128,128]{2,1,0:T(8,128)(2,1)S(1)} %get-tuple-element.14), channel_id=1, source_target_pairs={{0,16},{16,0},{1,17},{17,1},{2,18},{18,2},{3,19},{19,3},{4,20},{20... | collective-permute-start | bytes 786440 | tf_op jit(solution)/shard_map/ppermute | solution.py:17
  57.0 9.3 %collective-permute-start.2 = (bf16[2,4,128,128]{3,2,1,0:T(8,128)(2,1)S(1)}, bf16[2,4,128,128]{3,2,1,0:T(8,128)(2,1)S(1)}, u32[]{:S(2)}, u32[]{:S(2)}) collective-permute-start(bf16[2,4,128,128]{3,2,1,0:T(8,128)(2,1)S(1)} %fusion.1), channel_id=1, source_target_pairs={{0,32},{32,0},{1,33},{33,1},{2,34},{34,2},{3,35},{35,3},{4,36},{36... | collective-permute-start | bytes 786440 | tf_op jit(solution)/shard_map/ppermute | solution.py:17
  58.2 8.0 %collective-permute-start.16 = (bf16[128,512]{1,0:T(8,128)(2,1)S(1)}, bf16[128,512]{1,0:T(8,128)(2,1)S(1)}, u32[]{:S(2)}, u32[]{:S(2)}) collective-permute-start(bf16[128,512]{1,0:T(8,128)(2,1)S(1)} %summed.1.refs_0_), channel_id=1, source_target_pairs={{0,16},{16,0},{32,48},{48,32},{1,17},{17,1},{33,49},{49,33},{2,18}... | collective-permute-start | bytes 393224 | tf_op jit(solution)/shard_map/ppermute | solution.py:17
  59.1 9.5 %collective-permute-start.17 = (bf16[128,512]{1,0:T(8,128)(2,1)S(1)}, bf16[128,512]{1,0:T(8,128)(2,1)S(1)}, u32[]{:S(2)}, u32[]{:S(2)}) collective-permute-start(bf16[128,512]{1,0:T(8,128)(2,1)S(1)} %summed.1.refs_0_), channel_id=1, source_target_pairs={{0,32},{16,48},{32,0},{48,16},{1,33},{17,49},{33,1},{49,17},{2,34}... | collective-permute-start | bytes 393224 | tf_op jit(solution)/shard_map/ppermute | solution.py:17
  60.1 10.1 %collective-permute-start.18 = (bf16[128,512]{1,0:T(8,128)(2,1)S(1)}, bf16[128,512]{1,0:T(8,128)(2,1)S(1)}, u32[]{:S(2)}, u32[]{:S(2)}) collective-permute-start(bf16[128,512]{1,0:T(8,128)(2,1)S(1)} %summed.1.refs_0_), channel_id=1, source_target_pairs={{0,48},{16,32},{32,16},{48,0},{1,49},{17,33},{33,17},{49,1},{2,50}... | collective-permute-start | bytes 393224 | tf_op jit(solution)/shard_map/ppermute | solution.py:17
  71.2 9.4 %collective-permute-start.19 = (bf16[128,512]{1,0:T(8,128)(2,1)S(1)}, bf16[128,512]{1,0:T(8,128)(2,1)S(1)}, u32[]{:S(2)}, u32[]{:S(2)}) collective-permute-start(bf16[128,512]{1,0:T(8,128)(2,1)S(1)} %get-tuple-element.18), channel_id=1, source_target_pairs={{0,64},{64,0},{128,192},{192,128},{1,65},{65,1},{129,193},{193,129... | collective-permute-start | bytes 393224 | tf_op jit(solution)/shard_map/ppermute | solution.py:17
  73.1 10.5 %collective-permute-start.20 = (bf16[128,512]{1,0:T(8,128)(2,1)S(1)}, bf16[128,512]{1,0:T(8,128)(2,1)S(1)}, u32[]{:S(2)}, u32[]{:S(2)}) collective-permute-start(bf16[128,512]{1,0:T(8,128)(2,1)S(1)} %get-tuple-element.19), channel_id=1, source_target_pairs={{0,128},{64,192},{128,0},{192,64},{1,129},{65,193},{129,1},{193,65... | collective-permute-start | bytes 393224 | tf_op jit(solution)/shard_map/ppermute | solution.py:17
  77.8 10.5 %collective-permute-start.21 = (bf16[128,512]{1,0:T(8,128)(2,1)S(1)}, bf16[128,512]{1,0:T(8,128)(2,1)S(1)}, u32[]{:S(2)}, u32[]{:S(2)}) collective-permute-start(bf16[128,512]{1,0:T(8,128)(2,1)S(1)} %get-tuple-element.20), channel_id=1, source_target_pairs={{0,192},{64,128},{128,64},{192,0},{1,193},{65,129},{129,65},{193,1... | collective-permute-start | bytes 393224 | tf_op jit(solution)/shard_map/ppermute | solution.py:17

commit v4 on v3

v4 whole, which is shorter than its diff:
```python
import jax
import jax.numpy as jnp
from jax import lax
from jax.experimental import pallas as pl
from jax.experimental.pallas import tpu as pltpu
from jax.sharding import Mesh
from jax.sharding import PartitionSpec as P


ROW = ("z2", "z1", "z0", "xh")
COL = ("y2", "y1", "xl")
SWAP = [(0, 1), (1, 0)]
SMALL = pltpu.CompilerParams(vmem_limit_bytes=6 * 2**20)

NEAR = (1, 2, 6, 3, 7, 4, 5, 0)


def exchange(block, axes, mask):
    return lax.ppermute(block, axes, [(i, i ^ mask) for i in range(lax.axis_size(axes))])


def doubled(block, axis):
    other = lax.ppermute(block, axis, SWAP)
    low = lax.axis_index(axis) == 0
    return jnp.concatenate([jnp.where(low, block, other), jnp.where(low, other, block)], axis=0)


def vmem(count):
    return [pl.BlockSpec(memory_space=pltpu.VMEM)] * count


SCALARS = pl.BlockSpec(memory_space=pltpu.SMEM)


def index_over(*axes):
    place = 0
    for axis in axes:
        place = 2 * place + lax.axis_index(axis)
    return place


def scale_kernel(mine, other, gap_0, gap_1, rows, aux_cols, scaled_0, scaled_1, aux_to, landed):
    core, here = lax.axis_index("tm"), index_over(*COL)
    fetches = []
    for g, s in enumerate(NEAR):
        block = aux_cols.at[:, pl.ds(pl.multiple_of((2 * (here ^ s) + core) * 128, 128), 128)]
        fetches.append(pltpu.make_async_copy(block, aux_to.at[g], landed.at[g]))
        fetches[g].start()

    first, outer, inner = core == 0, index_over("z2", "z1"), index_over("z0", "xh")
    times = [jnp.where(first == low, mine[i], other[i]) for low in (True, False) for i in range(2)]
    lane = lax.broadcasted_iota(jnp.int32, (1, 128), 1) // 32
    for m2 in range(4):
        ats = [pl.ds(pl.multiple_of(((outer ^ m1) * 4 + (inner ^ m2)) * 32, 32), 32) for m1 in range(4)]
        block = jnp.concatenate([rows[at, :] for at in ats], axis=0).astype(jnp.float32)
        gaps = [jnp.zeros((1, 128), jnp.float32)] * 2
        for m1 in range(4):
            at = pl.ds(outer ^ m1, 1)
            shift = ((m1 - (inner ^ m2)) & 3) * 32
            for kind, gap in enumerate((gap_0, gap_1)):
                gaps[kind] = jnp.where(lane == m1, pltpu.roll(gap[at, :], shift, 1), gaps[kind])
        for kind, scaled in enumerate((scaled_0, scaled_1)):
            piece = block[:, kind * 128 : kind * 128 + 128].T
            gap = jnp.where(first, gaps[kind], gaps[1 - kind])
            for t in range(4):
                made = piece * jnp.exp(-gap * times[t])
                scaled[t * 128 : t * 128 + 128, m2 * 128 : m2 * 128 + 128] = made.astype(jnp.bfloat16)
    for fetch in fetches:
        fetch.wait()


def scaled_rows(mine, other, occ_gap, emp_gap, rows, aux_cols):
    return pl.pallas_call(
        scale_kernel,
        name="scaled_rows",
        out_shape=[jax.ShapeDtypeStruct((512, 512), jnp.bfloat16)] * 2
        + [jax.ShapeDtypeStruct((8, 512, 128), jnp.bfloat16)],
        in_specs=[SCALARS] * 2 + vmem(3) + [pl.BlockSpec(memory_space=pltpu.HBM)],
        out_specs=vmem(3),
        scratch_shapes=[pltpu.SemaphoreType.DMA((8,))],
        compiler_params=SMALL,
        cost_estimate=pl.CostEstimate(flops=1_000_000, bytes_accessed=3_800_000, transcendentals=0),
    )(mine, other, occ_gap.reshape(4, 128), emp_gap.reshape(4, 128), rows, aux_cols)


def chi_kernel(scaled_a, scaled_b, *refs):
    arrived_a, arrived_b, (chi, cols_a, cols_b) = refs[:4], refs[4:8], refs[8:]
    for m in range(4):
        cols_a[m * 128 : m * 128 + 128, :] = arrived_a[m][...]
        cols_b[m * 128 : m * 128 + 128, :] = arrived_b[m][...]
    for t in range(4):
        here = slice(t * 128, t * 128 + 128)
        green_a = jnp.dot(scaled_a[here, :], cols_a[...], preferred_element_type=jnp.float32)
        green_b = jnp.dot(scaled_b[here, :], cols_b[...], preferred_element_type=jnp.float32)
        chi[here, :] = (green_a * green_b).astype(jnp.bfloat16)


def chi_times(scaled_a, scaled_b, cols_a, cols_b):
    return pl.pallas_call(
        chi_kernel,
        name="chi_times",
        out_shape=jax.ShapeDtypeStruct((512, 512), jnp.bfloat16),
        in_specs=vmem(10),
        out_specs=vmem(1)[0],
        scratch_shapes=[pltpu.VMEM((512, 512), jnp.bfloat16)] * 2,
        compiler_params=SMALL,
        cost_estimate=pl.CostEstimate(flops=540_000_000, bytes_accessed=3_000_000, transcendentals=0),
    )(scaled_a, scaled_b, *cols_a, *cols_b)


def turn_kernel(aux, mine, theirs):
    here = lax.axis_index("xh")
    for blocks, xh in ((mine, here), (theirs, 1 - here)):
        for n in range(8):
            at = pl.ds(pl.multiple_of((2 * n + xh) * 128, 128), 128)
            blocks[n] = aux[:, at].T


def turned(aux_rows):
    return pl.pallas_call(
        turn_kernel,
        name="turned",
        out_shape=[jax.ShapeDtypeStruct((8, 128, 128), jnp.bfloat16)] * 2,
        in_specs=vmem(1),
        out_specs=vmem(2),
        compiler_params=SMALL,
        cost_estimate=pl.CostEstimate(flops=500_000, bytes_accessed=1_000_000, transcendentals=0),
    )(aux_rows)


def sum_kernel(*refs):
    parts, out = refs[:-1], refs[-1]
    for t in range(4):
        here = slice(t * 128, t * 128 + 128)
        out[:, here] = sum(part[here, :].astype(jnp.float32) for part in parts).astype(jnp.bfloat16)


def summed(parts):
    return pl.pallas_call(
        sum_kernel,
        name="summed",
        out_shape=jax.ShapeDtypeStruct((128, 512), jnp.bfloat16),
        in_specs=vmem(8),
        out_specs=vmem(1)[0],
        compiler_params=SMALL,
        cost_estimate=pl.CostEstimate(flops=500_000, bytes_accessed=1_300_000, transcendentals=0),
    )(*parts)


def left_kernel(mine, xh_aux, z_aux, *refs):
    right, outs, (left, stacked) = refs[:4], refs[4:8], refs[8:]
    for m in range(4):
        stacked[m * 128 : m * 128 + 128, :] = right[m][...]
    here, z0 = index_over("z2", "z1"), lax.axis_index("z0")
    for e in range(4):
        p = here ^ e
        blocks = (mine[2 * p + z0], xh_aux[2 * p + z0], z_aux[0, p], z_aux[1, p])
        for m, block in enumerate(blocks):
            left[e * 128 : e * 128 + 128, m * 128 : m * 128 + 128] = block
    made = jnp.dot(left[...], stacked[...], preferred_element_type=jnp.float32)
    for e in range(4):
        outs[e][...] = made[e * 128 : e * 128 + 128, :].astype(outs[e].dtype)


def left_parts(mine, xh_aux, z_aux, right):
    return pl.pallas_call(
        left_kernel,
        name="left_parts",
        out_shape=[jax.ShapeDtypeStruct((128, 512), jnp.bfloat16 if e else jnp.float32) for e in range(4)],
        in_specs=vmem(7),
        out_specs=vmem(4),
        scratch_shapes=[pltpu.VMEM((512, 512), jnp.bfloat16)] * 2,
        compiler_params=SMALL,
        cost_estimate=pl.CostEstimate(flops=270_000_000, bytes_accessed=1_700_000, transcendentals=0),
    )(mine, xh_aux, z_aux, *right)


def mix_kernel(coef, *refs):
    parts, out = refs[:4], refs[4]
    whole = [sum(part[:, t * 128 : t * 128 + 128].astype(jnp.float32) for part in parts) for t in range(4)]
    for w in range(4):
        out[w] = sum(coef[w, t] * whole[t] for t in range(4))


def mix(coef, parts):
    return pl.pallas_call(
        mix_kernel,
        name="mix",
        out_shape=jax.ShapeDtypeStruct((4, 128, 128), jnp.float32),
        in_specs=[SCALARS] + vmem(4),
        out_specs=vmem(1)[0],
        compiler_params=SMALL,
    )(coef, *parts)


def per_device(
    occ_rows,
    occ_cols,
    emp_rows,
    emp_cols,
    occ_gap,
    emp_gap,
    times,
    time_weights,
    freqs,
    aux_rows,
    aux_cols,
):
    core = lax.axis_index("tm")
    first = core == 0
    z0 = lax.axis_index("z0")

    cols = jnp.where(first, occ_cols, emp_cols).T
    far = exchange(cols, ("z2", "z1"), 2)
    near = [exchange(cols, ("z2", "z1"), m) for m in (1, 3)]
    cols = jnp.concatenate([cols, near[0], far, near[1]], axis=0)
    cols_a = [cols] + [exchange(cols, ("z0", "xh"), m) for m in (1, 2, 3)]
    cols_b = [lax.ppermute(c, "tm", SWAP) for c in cols_a]

    rows = jnp.where(first, occ_rows, emp_rows).T, jnp.where(first, emp_rows, occ_rows).T
    rows = jnp.concatenate(rows, axis=1)
    for axis in reversed(COL):
        rows = doubled(rows, axis)

    other_times = lax.ppermute(times, "tm", SWAP)
    scaled_a, scaled_b, aux_to = scaled_rows(times, other_times, occ_gap, emp_gap, rows, aux_cols)

    mine, theirs = turned(aux_rows)
    xh_aux = exchange(theirs, "xh", 1)

    chi = chi_times(scaled_a, scaled_b, cols_a, cols_b)
    parts = []
    for g, s in enumerate(NEAR):
        part = jnp.dot(chi, aux_to[g], preferred_element_type=jnp.float32)
        parts.append(exchange(part.astype(jnp.bfloat16), COL, s) if s else part)

    z_aux = jnp.stack([mine, xh_aux]).reshape(2, 4, 2, 128, 128)
    z_aux = lax.dynamic_index_in_dim(z_aux, 1 - z0, 2, keepdims=False)
    z_aux = exchange(z_aux, "z0", 1)

    right = summed(parts)
    right = [right] + [exchange(right, ("z0", "xh"), m) for m in (1, 2, 3)]
    parts = left_parts(mine, xh_aux, z_aux, right)
    held = lax.optimization_barrier((parts[0], times, other_times, time_weights, freqs))
    own, times, other_times, time_weights, freqs = held
    parts = [own] + [exchange(parts[e], ("z2", "z1"), e) for e in (1, 2, 3)]
    other_weights = lax.ppermute(time_weights, "tm", SWAP)
    moments = jnp.where(first, jnp.stack([times, other_times]), jnp.stack([other_times, times])).reshape(4)
    weights = jnp.where(first, jnp.stack([time_weights, other_weights]), jnp.stack([other_weights, time_weights]))
    coef = weights.reshape(1, 4) * jnp.cos(freqs[:, None] * moments[None, :])
    return mix(coef, parts)


def solution(mesh):
    torus = Mesh(mesh.devices.reshape((2,) * 8), (*ROW, *COL, "tm"))
    return jax.shard_map(
        per_device,
        mesh=torus,
        in_specs=(
            P(ROW, COL),
            P(COL, ROW),
            P(ROW, COL),
            P(COL, ROW),
            P(),
            P(),
            P("tm"),
            P("tm"),
            P(),
            P(ROW, None),
            P(COL, None),
        ),
        out_specs=P(None, ROW, (*COL, "tm")),
        check_vma=False,
    )
```

time: 90 us -> 92.7 us (1.030)
  starting transfers between devices: 39.9 us -> 44.3 us
  Pallas kernels: 7.53 us -> 4.13 us
  matrix products: 0 us -> 2.36 us
  other arithmetic: 3.57 us -> 1.96 us
  local copies, waits for them, and re-layouts: 1.73 us -> 3.24 us
    ppermute x14 -> x21, starting transfers between devices: 28.9 us -> 37.4 us  [exchange(): lax.ppermute(block, axes, [(i, i ^ mask) for i in range(lax.axis_size(axe...]
    all_to_all x1 -> x0, starting transfers between devices: 4.19 us -> none  [per_device(): parts = lax.all_to_all(parts, COL, 0, 0, tiled=True)]
    ppermute x14 -> x21, waiting for transfers between devices: 36.2 us -> 32.6 us  [exchange(): lax.ppermute(block, axes, [(i, i ^ mask) for i in range(lax.axis_size(axe...]
    pallas_call x2 -> x1, Pallas kernels: 3.45 us -> 0.73 us  [chi_times(): pl.pallas_call(chi_kernel, name='chi_times', out_shape=jax.ShapeDtypeStru...]
    dot_general x0 -> x8, matrix products: none -> 2.36 us  [per_device(): part = jnp.dot(chi, aux_to[g], preferred_element_type=jnp.float32)]
    ppermute x3, waiting for transfers between devices: 0.43 us -> 2.43 us  [doubled(): other = lax.ppermute(block, axis, SWAP)]
    unnamed x10 -> x16, local copies, waits for them, and re-layouts: 1.61 us -> 3.08 us
    ppermute x1 -> x2, waiting for transfers between devices: 0.01 us -> 1.06 us  [the longest x1 1.05 us: per_device(): other_weights = lax.ppermute(time_weights, 'tm', SWAP)]
  transfers between devices with their start and end apart: 23 -> 30, of which waited for: 10 -> 14; matrix products, arithmetic and copies ran while one was open for 3% -> 4% of each run, Pallas kernels for 3% -> 2%
where the time goes in v4:
time: 92.7 us; the launch traced here: 92.4 us
  starting transfers between devices  44.3 us (48%)
  waiting for transfers between devices  36.1 us (39%)
  Pallas kernels  4.13 us (4%)
  local copies, waits for them, and re-layouts  3.24 us (3%)
  matrix products  2.36 us (3%)
  other arithmetic  1.96 us (2%)
    ppermute x21, starting transfers between devices, exchange(): lax.ppermute(block, axes, [(i, i ^ mask) for i in range(lax.axis_size(axe...  37.4 us
    ppermute x21, waiting for transfers between devices, exchange(): lax.ppermute(block, axes, [(i, i ^ mask) for i in range(lax.axis_size(axe...  32.6 us
    ppermute x3, starting transfers between devices, doubled(): other = lax.ppermute(block, axis, SWAP)  6.23 us
    unnamed x16, local copies, waits for them, and re-layouts  3.08 us
    ppermute x3, waiting for transfers between devices, doubled(): other = lax.ppermute(block, axis, SWAP)  2.43 us
    dot_general x8, matrix products, per_device(): part = jnp.dot(chi, aux_to[g], preferred_element_type=jnp.float32)  2.36 us
  transfers between devices with their start and end apart: 30, of which 14 were waited for; matrix products, arithmetic and copies ran while one was open for 4% of the time, Pallas kernels for 2%

profile of v4, /device:TPU:32, one launch (start us, length us, event | category | flops | bytes accessed | tf_op | source)
XLA Modules:
  0.0 92.4 jit_solution(9920591329478489284)
XLA Ops:
  0.9 1.6 %collective-permute-start.3 = (bf16[64,256]{1,0:T(8,128)(2,1)S(1)}, bf16[64,256]{1,0:T(8,128)(2,1)S(1)}, u32[]{:S(2)}, u32[]{:S(2)}) collective-permute-start(bf16[64,256]{1,0:T(8,128)(2,1)S(1)} %pad_maximum_fusion.4), channel_id=1, source_target_pairs={{0,2},{2,0},{1,3},{3,1},{4,6},{6,4},{5,7},{7,5},{8,10},{10,8},{9,1... | collective-permute-start | bytes 98312 | tf_op jit(solution)/shard_map/ppermute | solution.py:23
  2.5 2.4 %collective-permute-done.3 = bf16[64,256]{1,0:T(8,128)(2,1)S(1)} collective-permute-done((bf16[64,256]{1,0:T(8,128)(2,1)S(1)}, bf16[64,256]{1,0:T(8,128)(2,1)S(1)}, u32[]{:S(2)}, u32[]{:S(2)}) %collective-permute-start.3) | collective-permute-done | bytes 32800 | tf_op jit(solution)/shard_map/ppermute | solution.py:23
  4.9 1.7 %collective-permute-start.4 = (bf16[128,256]{1,0:T(8,128)(2,1)S(1)}, bf16[128,256]{1,0:T(8,128)(2,1)S(1)}, u32[]{:S(2)}, u32[]{:S(2)}) collective-permute-start(bf16[128,256]{1,0:T(8,128)(2,1)S(1)} %pad_maximum_fusion.3), channel_id=1, source_target_pairs={{0,4},{4,0},{1,5},{5,1},{2,6},{6,2},{3,7},{7,3},{8,12},{12,8},{9,1... | collective-permute-start | bytes 196616 | tf_op jit(solution)/shard_map/ppermute | solution.py:23
  7.4 3.3 %collective-permute-start.6 = (bf16[32,512]{1,0:T(8,128)(2,1)S(1)}, bf16[32,512]{1,0:T(8,128)(2,1)S(1)}, u32[]{:S(2)}, u32[]{:S(2)}) collective-permute-start(bf16[32,512]{1,0:T(8,128)(2,1)S(1)} %select_bitcast_fusion), channel_id=1, source_target_pairs={{0,64},{64,0},{128,192},{192,128},{1,65},{65,1},{129,193},{193,129... | collective-permute-start | bytes 98312 | tf_op jit(solution)/shard_map/ppermute | solution.py:19
  10.6 4.5 %collective-permute-start.7 = (bf16[32,512]{1,0:T(8,128)(2,1)S(1)}, bf16[32,512]{1,0:T(8,128)(2,1)S(1)}, u32[]{:S(2)}, u32[]{:S(2)}) collective-permute-start(bf16[32,512]{1,0:T(8,128)(2,1)S(1)} %select_bitcast_fusion), channel_id=1, source_target_pairs={{0,128},{64,192},{128,0},{192,64},{1,129},{65,193},{129,1},{193,65... | collective-permute-start | bytes 98312 | tf_op jit(solution)/shard_map/ppermute | solution.py:19
  15.2 3.0 %collective-permute-start.5 = (bf16[256,256]{1,0:T(8,128)(2,1)S(1)}, bf16[256,256]{1,0:T(8,128)(2,1)S(1)}, u32[]{:S(2)}, u32[]{:S(2)}) collective-permute-start(bf16[256,256]{1,0:T(8,128)(2,1)S(1)} %pad_maximum_fusion.1), channel_id=1, source_target_pairs={{0,8},{8,0},{1,9},{9,1},{2,10},{10,2},{3,11},{11,3},{4,12},{12,4},... | collective-permute-start | bytes 393224 | tf_op jit(solution)/shard_map/ppermute | solution.py:23
  18.2 1.0 %copy-done.1 = bf16[128,2048]{1,0:T(8,128)(2,1)S(1)} copy-done((bf16[128,2048]{1,0:T(8,128)(2,1)S(1)}, bf16[128,2048]{1,0:T(8,128)(2,1)}, u32[]{:S(2)}) %copy-start.1) | copy-done | bytes 524312
  19.4 3.1 %collective-permute-start = (bf16[8,128,128]{2,1,0:T(8,128)(2,1)S(1)}, bf16[8,128,128]{2,1,0:T(8,128)(2,1)S(1)}, u32[]{:S(2)}, u32[]{:S(2)}) collective-permute-start(bf16[8,128,128]{2,1,0:T(8,128)(2,1)S(1)} %get-tuple-element.20), channel_id=1, source_target_pairs={{0,16},{16,0},{1,17},{17,1},{2,18},{18,2},{3,19},{19,3},{4,20},{20... | collective-permute-start | bytes 786440 | tf_op jit(solution)/shard_map/ppermute | solution.py:19
  22.6 1.7 %collective-permute-start.9 = (bf16[128,512]{1,0:T(8,128)(2,1)S(1)}, bf16[128,512]{1,0:T(8,128)(2,1)S(1)}, u32[]{:S(2)}, u32[]{:S(2)}) collective-permute-start(bf16[128,512]{1,0:T(8,128)(2,1)S(1)} %pad_maximum_fusion.2.refs_0_), channel_id=1, source_target_pairs={{0,16},{16,0},{32,48},{48,32},{1,17},{17,1},{33,49},{49,33},{2,18}... | collective-permute-start | bytes 393224 | tf_op jit(solution)/shard_map/ppermute | solution.py:19
  25.3 2.4 %collective-permute-start.11 = (bf16[128,512]{1,0:T(8,128)(2,1)S(1)}, bf16[128,512]{1,0:T(8,128)(2,1)S(1)}, u32[]{:S(2)}, u32[]{:S(2)}) collective-permute-start(bf16[128,512]{1,0:T(8,128)(2,1)S(1)} %pad_maximum_fusion.2.refs_0_), channel_id=1, source_target_pairs={{0,48},{16,32},{32,16},{48,0},{1,49},{17,33},{33,17},{49,1},{2,50}... | collective-permute-start | bytes 393224 | tf_op jit(solution)/shard_map/ppermute | solution.py:19
  27.8 7.5 %collective-permute-done.9.refs_1_ = bf16[128,512]{1,0:T(8,128)(2,1)S(1)} collective-permute-done((bf16[128,512]{1,0:T(8,128)(2,1)S(1)}, bf16[128,512]{1,0:T(8,128)(2,1)S(1)}, u32[]{:S(2)}, u32[]{:S(2)}) %collective-permute-start.9) | collective-permute-done | bytes 131104 | tf_op jit(solution)/shard_map/ppermute | solution.py:19
  38.0 1.2 %scaled_rows.1 = (bf16[512,512]{1,0:T(8,128)(2,1)S(1)}, bf16[512,512]{1,0:T(8,128)(2,1)S(1)}, bf16[8,512,128]{2,1,0:T(8,128)(2,1)S(1)}) custom-call(f32[2]{0:T(128)S(1)} %copy-done.2, f32[2]{0:T(128)S(1)} %collective-permute-done.2.other, f32[4,128]{1,0:T(4,128)S(1)} %bitcast.54, f32[4,128]{1,0:T(4,128)S(1)} %bitcast.55, ...), custom_call_target="tpu_custom_call" | custom-call | flops 1000000 | bytes 3800000 | tf_op jit(solution)/shard_map/scaled_rows/pallas_call | solution.py:73
  39.3 1.1 %collective-permute-start.1 = (bf16[2,4,128,128]{3,2,1,0:T(8,128)(2,1)S(1)}, bf16[2,4,128,128]{3,2,1,0:T(8,128)(2,1)S(1)}, u32[]{:S(2)}, u32[]{:S(2)}) collective-permute-start(bf16[2,4,128,128]{3,2,1,0:T(8,128)(2,1)S(1)} %fusion.1), channel_id=1, source_target_pairs={{0,32},{32,0},{1,33},{33,1},{2,34},{34,2},{3,35},{35,3},{4,36},{36... | collective-permute-start | bytes 786440 | tf_op jit(solution)/shard_map/ppermute | solution.py:19
  43.0 1.8 %collective-permute-start.22 = (bf16[512,128]{1,0:T(8,128)(2,1)S(1)}, bf16[512,128]{1,0:T(8,128)(2,1)S(1)}, u32[]{:S(2)}, u32[]{:S(2)}) collective-permute-start(bf16[512,128]{1,0:T(8,128)(2,1)S(1)} %convolution_convert_fusion), channel_id=1, source_target_pairs={{0,10},{2,8},{4,14},{6,12},{8,2},{10,0},{12,6},{14,4},{1,11},{3,9}... | collective-permute-start | bytes 393224 | tf_op jit(solution)/shard_map/ppermute | solution.py:19
  44.8 2.9 %collective-permute-start.21 = (bf16[512,128]{1,0:T(8,128)(2,1)S(1)}, bf16[512,128]{1,0:T(8,128)(2,1)S(1)}, u32[]{:S(2)}, u32[]{:S(2)}) collective-permute-start(bf16[512,128]{1,0:T(8,128)(2,1)S(1)} %convolution_convert_fusion.1), channel_id=1, source_target_pairs={{0,8},{2,10},{4,12},{6,14},{8,0},{10,2},{12,4},{14,6},{1,9},{3,11}... | collective-permute-start | bytes 393224 | tf_op jit(solution)/shard_map/ppermute | solution.py:19
  47.9 1.3 %collective-permute-start.19 = (bf16[512,128]{1,0:T(8,128)(2,1)S(1)}, bf16[512,128]{1,0:T(8,128)(2,1)S(1)}, u32[]{:S(2)}, u32[]{:S(2)}) collective-permute-start(bf16[512,128]{1,0:T(8,128)(2,1)S(1)} %convolution_convert_fusion.3), channel_id=1, source_target_pairs={{0,6},{2,4},{4,2},{6,0},{8,14},{10,12},{12,10},{14,8},{1,7},{3,5},... | collective-permute-start | bytes 393224 | tf_op jit(solution)/shard_map/ppermute | solution.py:19
  49.5 2.0 %collective-permute-done.22.refs_6_ = bf16[512,128]{1,0:T(8,128)(2,1)S(1)} collective-permute-done((bf16[512,128]{1,0:T(8,128)(2,1)S(1)}, bf16[512,128]{1,0:T(8,128)(2,1)S(1)}, u32[]{:S(2)}, u32[]{:S(2)}) %collective-permute-start.22) | collective-permute-done | bytes 131104 | tf_op jit(solution)/shard_map/ppermute | solution.py:19
  51.8 4.3 %collective-permute-done.21.refs_5_ = bf16[512,128]{1,0:T(8,128)(2,1)S(1)} collective-permute-done((bf16[512,128]{1,0:T(8,128)(2,1)S(1)}, bf16[512,128]{1,0:T(8,128)(2,1)S(1)}, u32[]{:S(2)}, u32[]{:S(2)}) %collective-permute-start.21) | collective-permute-done | bytes 131104 | tf_op jit(solution)/shard_map/ppermute | solution.py:19
  57.1 1.2 %collective-permute-start.16 = (bf16[512,128]{1,0:T(8,128)(2,1)S(1)}, bf16[512,128]{1,0:T(8,128)(2,1)S(1)}, u32[]{:S(2)}, u32[]{:S(2)}) collective-permute-start(bf16[512,128]{1,0:T(8,128)(2,1)S(1)} %convolution_convert_fusion.6), channel_id=1, source_target_pairs={{0,2},{2,0},{4,6},{6,4},{8,10},{10,8},{12,14},{14,12},{1,3},{3,1},... | collective-permute-start | bytes 393224 | tf_op jit(solution)/shard_map/ppermute | solution.py:19
  58.6 1.0 %collective-permute-done.18.refs_2_ = bf16[512,128]{1,0:T(8,128)(2,1)S(1)} collective-permute-done((bf16[512,128]{1,0:T(8,128)(2,1)S(1)}, bf16[512,128]{1,0:T(8,128)(2,1)S(1)}, u32[]{:S(2)}, u32[]{:S(2)}) %collective-permute-start.18) | collective-permute-done | bytes 131104 | tf_op jit(solution)/shard_map/ppermute | solution.py:19
  59.6 1.5 %collective-permute-done.17.refs_1_ = bf16[512,128]{1,0:T(8,128)(2,1)S(1)} collective-permute-done((bf16[512,128]{1,0:T(8,128)(2,1)S(1)}, bf16[512,128]{1,0:T(8,128)(2,1)S(1)}, u32[]{:S(2)}, u32[]{:S(2)}) %collective-permute-start.17) | collective-permute-done | bytes 131104 | tf_op jit(solution)/shard_map/ppermute | solution.py:19
  62.2 3.1 %collective-permute-start.23 = (bf16[128,512]{1,0:T(8,128)(2,1)S(1)}, bf16[128,512]{1,0:T(8,128)(2,1)S(1)}, u32[]{:S(2)}, u32[]{:S(2)}) collective-permute-start(bf16[128,512]{1,0:T(8,128)(2,1)S(1)} %summed.1.refs_0_), channel_id=1, source_target_pairs={{0,16},{16,0},{32,48},{48,32},{1,17},{17,1},{33,49},{49,33},{2,18}... | collective-permute-start | bytes 393224 | tf_op jit(solution)/shard_map/ppermute | solution.py:19
  67.3 1.9 %collective-permute-done.23.refs_1_ = bf16[128,512]{1,0:T(8,128)(2,1)S(1)} collective-permute-done((bf16[128,512]{1,0:T(8,128)(2,1)S(1)}, bf16[128,512]{1,0:T(8,128)(2,1)S(1)}, u32[]{:S(2)}, u32[]{:S(2)}) %collective-permute-start.23) | collective-permute-done | bytes 131104 | tf_op jit(solution)/shard_map/ppermute | solution.py:19
  69.2 1.3 %collective-permute-done.24.refs_2_ = bf16[128,512]{1,0:T(8,128)(2,1)S(1)} collective-permute-done((bf16[128,512]{1,0:T(8,128)(2,1)S(1)}, bf16[128,512]{1,0:T(8,128)(2,1)S(1)}, u32[]{:S(2)}, u32[]{:S(2)}) %collective-permute-start.24) | collective-permute-done | bytes 131104 | tf_op jit(solution)/shard_map/ppermute | solution.py:19
  70.5 3.2 %collective-permute-done.25.refs_3_ = bf16[128,512]{1,0:T(8,128)(2,1)S(1)} collective-permute-done((bf16[128,512]{1,0:T(8,128)(2,1)S(1)}, bf16[128,512]{1,0:T(8,128)(2,1)S(1)}, u32[]{:S(2)}, u32[]{:S(2)}) %collective-permute-start.25) | collective-permute-done | bytes 131104 | tf_op jit(solution)/shard_map/ppermute | solution.py:19
  74.1 2.1 %collective-permute-start.27 = (bf16[128,512]{1,0:T(8,128)(2,1)S(1)}, bf16[128,512]{1,0:T(8,128)(2,1)S(1)}, u32[]{:S(2)}, u32[]{:S(2)}) collective-permute-start(bf16[128,512]{1,0:T(8,128)(2,1)S(1)} %get-tuple-element.30), channel_id=1, source_target_pairs={{0,64},{64,0},{128,192},{192,128},{1,65},{65,1},{129,193},{193,129... | collective-permute-start | bytes 393224 | tf_op jit(solution)/shard_map/ppermute | solution.py:19
  76.2 4.5 %collective-permute-start.28 = (bf16[128,512]{1,0:T(8,128)(2,1)S(1)}, bf16[128,512]{1,0:T(8,128)(2,1)S(1)}, u32[]{:S(2)}, u32[]{:S(2)}) collective-permute-start(bf16[128,512]{1,0:T(8,128)(2,1)S(1)} %get-tuple-element.31), channel_id=1, source_target_pairs={{0,128},{64,192},{128,0},{192,64},{1,129},{65,193},{129,1},{193,65... | collective-permute-start | bytes 393224 | tf_op jit(solution)/shard_map/ppermute | solution.py:19
  80.8 1.1 %collective-permute-done.26 = f32[2]{0:T(128)S(1)} collective-permute-done((f32[2]{0:T(128)S(1)}, f32[2]{0:T(128)S(1)}, u32[]{:S(2)}, u32[]{:S(2)}) %collective-permute-start.26) | collective-permute-done | bytes 40 | tf_op jit(solution)/shard_map/ppermute | solution.py:247
  82.1 3.6 %collective-permute-done.27.refs_1_ = bf16[128,512]{1,0:T(8,128)(2,1)S(1)} collective-permute-done((bf16[128,512]{1,0:T(8,128)(2,1)S(1)}, bf16[128,512]{1,0:T(8,128)(2,1)S(1)}, u32[]{:S(2)}, u32[]{:S(2)}) %collective-permute-start.27) | collective-permute-done | bytes 131104 | tf_op jit(solution)/shard_map/ppermute | solution.py:19
  85.7 4.1 %collective-permute-done.28.refs_2_ = bf16[128,512]{1,0:T(8,128)(2,1)S(1)} collective-permute-done((bf16[128,512]{1,0:T(8,128)(2,1)S(1)}, bf16[128,512]{1,0:T(8,128)(2,1)S(1)}, u32[]{:S(2)}, u32[]{:S(2)}) %collective-permute-start.28) | collective-permute-done | bytes 131104 | tf_op jit(solution)/shard_map/ppermute | solution.py:19
  89.8 1.2 %collective-permute-done.29.refs_3_ = bf16[128,512]{1,0:T(8,128)(2,1)S(1)} collective-permute-done((bf16[128,512]{1,0:T(8,128)(2,1)S(1)}, bf16[128,512]{1,0:T(8,128)(2,1)S(1)}, u32[]{:S(2)}, u32[]{:S(2)}) %collective-permute-start.29) | collective-permute-done | bytes 131104 | tf_op jit(solution)/shard_map/ppermute | solution.py:19
  91.0 1.4 %mix.1 = f32[4,128,128]{2,1,0:T(8,128)} custom-call(f32[4,4]{1,0:T(4,128)S(1)} %cosine_multiply_fusion.coef, f32[128,512]{1,0:T(8,128)S(1)} %get-tuple-element.29.refs_0_, bf16[128,512]{1,0:T(8,128)(2,1)S(1)} %collective-permute-done.27.refs_1_, bf16[128,512]{1,0:T(8,128)(2,1)S(1)} %collective-permute-done.28.refs_2_, ...), custom_call_target="tpu_custom_call" | custom-call | tf_op jit(solution)/shard_map/mix/pallas_call | solution.py:186
  (74 shorter events, 14.2 us)
Async XLA Ops:
  0.9 4.0 %collective-permute-start.3 = (bf16[64,256]{1,0:T(8,128)(2,1)S(1)}, bf16[64,256]{1,0:T(8,128)(2,1)S(1)}, u32[]{:S(2)}, u32[]{:S(2)}) collective-permute-start(bf16[64,256]{1,0:T(8,128)(2,1)S(1)} %pad_maximum_fusion.4), channel_id=1, source_target_pairs={{0,2},{2,0},{1,3},{3,1},{4,6},{6,4},{5,7},{7,5},{8,10},{10,8},{9,1... | collective-permute-start | bytes 98312 | tf_op jit(solution)/shard_map/ppermute | solution.py:23
  4.9 10.2 %collective-permute-start.4 = (bf16[128,256]{1,0:T(8,128)(2,1)S(1)}, bf16[128,256]{1,0:T(8,128)(2,1)S(1)}, u32[]{:S(2)}, u32[]{:S(2)}) collective-permute-start(bf16[128,256]{1,0:T(8,128)(2,1)S(1)} %pad_maximum_fusion.3), channel_id=1, source_target_pairs={{0,4},{4,0},{1,5},{5,1},{2,6},{6,2},{3,7},{7,3},{8,12},{12,8},{9,1... | collective-permute-start | bytes 196616 | tf_op jit(solution)/shard_map/ppermute | solution.py:23
  7.4 12.1 %collective-permute-start.6 = (bf16[32,512]{1,0:T(8,128)(2,1)S(1)}, bf16[32,512]{1,0:T(8,128)(2,1)S(1)}, u32[]{:S(2)}, u32[]{:S(2)}) collective-permute-start(bf16[32,512]{1,0:T(8,128)(2,1)S(1)} %select_bitcast_fusion), channel_id=1, source_target_pairs={{0,64},{64,0},{128,192},{192,128},{1,65},{65,1},{129,193},{193,129... | collective-permute-start | bytes 98312 | tf_op jit(solution)/shard_map/ppermute | solution.py:19
  10.6 11.9 %collective-permute-start.7 = (bf16[32,512]{1,0:T(8,128)(2,1)S(1)}, bf16[32,512]{1,0:T(8,128)(2,1)S(1)}, u32[]{:S(2)}, u32[]{:S(2)}) collective-permute-start(bf16[32,512]{1,0:T(8,128)(2,1)S(1)} %select_bitcast_fusion), channel_id=1, source_target_pairs={{0,128},{64,192},{128,0},{192,64},{1,129},{65,193},{129,1},{193,65... | collective-permute-start | bytes 98312 | tf_op jit(solution)/shard_map/ppermute | solution.py:19
  15.1 7.4 %collective-permute-start.8 = (bf16[32,512]{1,0:T(8,128)(2,1)S(1)}, bf16[32,512]{1,0:T(8,128)(2,1)S(1)}, u32[]{:S(2)}, u32[]{:S(2)}) collective-permute-start(bf16[32,512]{1,0:T(8,128)(2,1)S(1)} %select_bitcast_fusion), channel_id=1, source_target_pairs={{0,192},{64,128},{128,64},{192,0},{1,193},{65,129},{129,65},{193,1... | collective-permute-start | bytes 98312 | tf_op jit(solution)/shard_map/ppermute | solution.py:19
  15.2 10.1 %collective-permute-start.5 = (bf16[256,256]{1,0:T(8,128)(2,1)S(1)}, bf16[256,256]{1,0:T(8,128)(2,1)S(1)}, u32[]{:S(2)}, u32[]{:S(2)}) collective-permute-start(bf16[256,256]{1,0:T(8,128)(2,1)S(1)} %pad_maximum_fusion.1), channel_id=1, source_target_pairs={{0,8},{8,0},{1,9},{9,1},{2,10},{10,2},{3,11},{11,3},{4,12},{12,4},... | collective-permute-start | bytes 393224 | tf_op jit(solution)/shard_map/ppermute | solution.py:23
  18.2 9.5 %collective-permute-start.2 = (f32[2]{0:T(128)}, f32[2]{0:T(128)S(1)}, u32[]{:S(2)}, u32[]{:S(2)}) collective-permute-start(f32[2]{0:T(128)} %mine.1), channel_id=1, source_target_pairs={{0,1},{1,0},{2,3},{3,2},{4,5},{5,4},{6,7},{7,6},{8,9},{9,8},{10,11... | collective-permute-start | bytes 32 | tf_op jit(solution)/shard_map/ppermute | solution.py:225
  19.4 19.8 %collective-permute-start = (bf16[8,128,128]{2,1,0:T(8,128)(2,1)S(1)}, bf16[8,128,128]{2,1,0:T(8,128)(2,1)S(1)}, u32[]{:S(2)}, u32[]{:S(2)}) collective-permute-start(bf16[8,128,128]{2,1,0:T(8,128)(2,1)S(1)} %get-tuple-element.20), channel_id=1, source_target_pairs={{0,16},{16,0},{1,17},{17,1},{2,18},{18,2},{3,19},{19,3},{4,20},{20... | collective-permute-start | bytes 786440 | tf_op jit(solution)/shard_map/ppermute | solution.py:19
  22.6 12.8 %collective-permute-start.9 = (bf16[128,512]{1,0:T(8,128)(2,1)S(1)}, bf16[128,512]{1,0:T(8,128)(2,1)S(1)}, u32[]{:S(2)}, u32[]{:S(2)}) collective-permute-start(bf16[128,512]{1,0:T(8,128)(2,1)S(1)} %pad_maximum_fusion.2.refs_0_), channel_id=1, source_target_pairs={{0,16},{16,0},{32,48},{48,32},{1,17},{17,1},{33,49},{49,33},{2,18}... | collective-permute-start | bytes 393224 | tf_op jit(solution)/shard_map/ppermute | solution.py:19
  24.3 11.1 %collective-permute-start.10 = (bf16[128,512]{1,0:T(8,128)(2,1)S(1)}, bf16[128,512]{1,0:T(8,128)(2,1)S(1)}, u32[]{:S(2)}, u32[]{:S(2)}) collective-permute-start(bf16[128,512]{1,0:T(8,128)(2,1)S(1)} %pad_maximum_fusion.2.refs_0_), channel_id=1, source_target_pairs={{0,32},{16,48},{32,0},{48,16},{1,33},{17,49},{33,1},{49,17},{2,34}... | collective-permute-start | bytes 393224 | tf_op jit(solution)/shard_map/ppermute | solution.py:19
  25.3 10.6 %collective-permute-start.11 = (bf16[128,512]{1,0:T(8,128)(2,1)S(1)}, bf16[128,512]{1,0:T(8,128)(2,1)S(1)}, u32[]{:S(2)}, u32[]{:S(2)}) collective-permute-start(bf16[128,512]{1,0:T(8,128)(2,1)S(1)} %pad_maximum_fusion.2.refs_0_), channel_id=1, source_target_pairs={{0,48},{16,32},{32,16},{48,0},{1,49},{17,33},{33,17},{49,1},{2,50}... | collective-permute-start | bytes 393224 | tf_op jit(solution)/shard_map/ppermute | solution.py:19
  27.7 12.7 %collective-permute-start.12 = (bf16[128,512]{1,0:T(8,128)(2,1)S(1)}, bf16[128,512]{1,0:T(8,128)(2,1)S(1)}, u32[]{:S(2)}, u32[]{:S(2)}) collective-permute-start(bf16[128,512]{1,0:T(8,128)(2,1)S(1)} %pad_maximum_fusion.2.refs_0_), channel_id=1, source_target_pairs={{0,1},{1,0},{2,3},{3,2},{4,5},{5,4},{6,7},{7,6},{8,9},{9,8},{10,11... | collective-permute-start | bytes 393224 | tf_op jit(solution)/shard_map/ppermute | solution.py:218
  35.4 5.1 %collective-permute-start.13 = (bf16[128,512]{1,0:T(8,128)(2,1)S(1)}, bf16[128,512]{1,0:T(8,128)(2,1)S(1)}, u32[]{:S(2)}, u32[]{:S(2)}) collective-permute-start(bf16[128,512]{1,0:T(8,128)(2,1)S(1)} %collective-permute-done.9.refs_1_), channel_id=1, source_target_pairs={{0,1},{1,0},{2,3},{3,2},{4,5},{5,4},{6,7},{7,6},{8,9},{9,8},{10,11... | collective-permute-start | bytes 393224 | tf_op jit(solution)/shard_map/ppermute | solution.py:218
  35.4 5.1 %collective-permute-start.14 = (bf16[128,512]{1,0:T(8,128)(2,1)S(1)}, bf16[128,512]{1,0:T(8,128)(2,1)S(1)}, u32[]{:S(2)}, u32[]{:S(2)}) collective-permute-start(bf16[128,512]{1,0:T(8,128)(2,1)S(1)} %collective-permute-done.10.refs_2_), channel_id=1, source_target_pairs={{0,1},{1,0},{2,3},{3,2},{4,5},{5,4},{6,7},{7,6},{8,9},{9,8},{10,11... | collective-permute-start | bytes 393224 | tf_op jit(solution)/shard_map/ppermute | solution.py:218
  35.9 4.6 %collective-permute-start.15 = (bf16[128,512]{1,0:T(8,128)(2,1)S(1)}, bf16[128,512]{1,0:T(8,128)(2,1)S(1)}, u32[]{:S(2)}, u32[]{:S(2)}) collective-permute-start(bf16[128,512]{1,0:T(8,128)(2,1)S(1)} %collective-permute-done.11.refs_3_), channel_id=1, source_target_pairs={{0,1},{1,0},{2,3},{3,2},{4,5},{5,4},{6,7},{7,6},{8,9},{9,8},{10,11... | collective-permute-start | bytes 393224 | tf_op jit(solution)/shard_map/ppermute | solution.py:218
  39.3 27.9 %collective-permute-start.1 = (bf16[2,4,128,128]{3,2,1,0:T(8,128)(2,1)S(1)}, bf16[2,4,128,128]{3,2,1,0:T(8,128)(2,1)S(1)}, u32[]{:S(2)}, u32[]{:S(2)}) collective-permute-start(bf16[2,4,128,128]{3,2,1,0:T(8,128)(2,1)S(1)} %fusion.1), channel_id=1, source_target_pairs={{0,32},{32,0},{1,33},{33,1},{2,34},{34,2},{3,35},{35,3},{4,36},{36... | collective-permute-start | bytes 786440 | tf_op jit(solution)/shard_map/ppermute | solution.py:19
  43.0 37.8 %copy-start.6 = (f32[2]{0:T(128)S(1)}, f32[2]{0:T(128)}, u32[]{:S(2)}) copy-start(f32[2]{0:T(128)} %param.18) | copy-start | bytes 28
  43.0 39.0 %copy-start.7 = (f32[4]{0:T(128)S(1)}, f32[4]{0:T(128)}, u32[]{:S(2)}) copy-start(f32[4]{0:T(128)} %param.19) | copy-start | bytes 52
  43.0 8.5 %collective-permute-start.22 = (bf16[512,128]{1,0:T(8,128)(2,1)S(1)}, bf16[512,128]{1,0:T(8,128)(2,1)S(1)}, u32[]{:S(2)}, u32[]{:S(2)}) collective-permute-start(bf16[512,128]{1,0:T(8,128)(2,1)S(1)} %convolution_convert_fusion), channel_id=1, source_target_pairs={{0,10},{2,8},{4,14},{6,12},{8,2},{10,0},{12,6},{14,4},{1,11},{3,9}... | collective-permute-start | bytes 393224 | tf_op jit(solution)/shard_map/ppermute | solution.py:19
  44.8 11.3 %collective-permute-start.21 = (bf16[512,128]{1,0:T(8,128)(2,1)S(1)}, bf16[512,128]{1,0:T(8,128)(2,1)S(1)}, u32[]{:S(2)}, u32[]{:S(2)}) collective-permute-start(bf16[512,128]{1,0:T(8,128)(2,1)S(1)} %convolution_convert_fusion.1), channel_id=1, source_target_pairs={{0,8},{2,10},{4,12},{6,14},{8,0},{10,2},{12,4},{14,6},{1,9},{3,11}... | collective-permute-start | bytes 393224 | tf_op jit(solution)/shard_map/ppermute | solution.py:19
  47.7 9.4 %collective-permute-start.20 = (bf16[512,128]{1,0:T(8,128)(2,1)S(1)}, bf16[512,128]{1,0:T(8,128)(2,1)S(1)}, u32[]{:S(2)}, u32[]{:S(2)}) collective-permute-start(bf16[512,128]{1,0:T(8,128)(2,1)S(1)} %convolution_convert_fusion.2), channel_id=1, source_target_pairs={{0,14},{2,12},{4,10},{6,8},{8,6},{10,4},{12,2},{14,0},{1,15},{3,13... | collective-permute-start | bytes 393224 | tf_op jit(solution)/shard_map/ppermute | solution.py:19
  47.9 10.7 %collective-permute-start.19 = (bf16[512,128]{1,0:T(8,128)(2,1)S(1)}, bf16[512,128]{1,0:T(8,128)(2,1)S(1)}, u32[]{:S(2)}, u32[]{:S(2)}) collective-permute-start(bf16[512,128]{1,0:T(8,128)(2,1)S(1)} %convolution_convert_fusion.3), channel_id=1, source_target_pairs={{0,6},{2,4},{4,2},{6,0},{8,14},{10,12},{12,10},{14,8},{1,7},{3,5},... | collective-permute-start | bytes 393224 | tf_op jit(solution)/shard_map/ppermute | solution.py:19
  51.5 8.1 %collective-permute-start.18 = (bf16[512,128]{1,0:T(8,128)(2,1)S(1)}, bf16[512,128]{1,0:T(8,128)(2,1)S(1)}, u32[]{:S(2)}, u32[]{:S(2)}) collective-permute-start(bf16[512,128]{1,0:T(8,128)(2,1)S(1)} %convolution_convert_fusion.4), channel_id=1, source_target_pairs={{0,12},{2,14},{4,8},{6,10},{8,4},{10,6},{12,0},{14,2},{1,13},{3,15... | collective-permute-start | bytes 393224 | tf_op jit(solution)/shard_map/ppermute | solution.py:19
  56.1 5.0 %collective-permute-start.17 = (bf16[512,128]{1,0:T(8,128)(2,1)S(1)}, bf16[512,128]{1,0:T(8,128)(2,1)S(1)}, u32[]{:S(2)}, u32[]{:S(2)}) collective-permute-start(bf16[512,128]{1,0:T(8,128)(2,1)S(1)} %convolution_convert_fusion.5), channel_id=1, source_target_pairs={{0,4},{2,6},{4,0},{6,2},{8,12},{10,14},{12,8},{14,10},{1,5},{3,7},... | collective-permute-start | bytes 393224 | tf_op jit(solution)/shard_map/ppermute | solution.py:19
  57.1 5.0 %collective-permute-start.16 = (bf16[512,128]{1,0:T(8,128)(2,1)S(1)}, bf16[512,128]{1,0:T(8,128)(2,1)S(1)}, u32[]{:S(2)}, u32[]{:S(2)}) collective-permute-start(bf16[512,128]{1,0:T(8,128)(2,1)S(1)} %convolution_convert_fusion.6), channel_id=1, source_target_pairs={{0,2},{2,0},{4,6},{6,4},{8,10},{10,8},{12,14},{14,12},{1,3},{3,1},... | collective-permute-start | bytes 393224 | tf_op jit(solution)/shard_map/ppermute | solution.py:19
  62.2 7.0 %collective-permute-start.23 = (bf16[128,512]{1,0:T(8,128)(2,1)S(1)}, bf16[128,512]{1,0:T(8,128)(2,1)S(1)}, u32[]{:S(2)}, u32[]{:S(2)}) collective-permute-start(bf16[128,512]{1,0:T(8,128)(2,1)S(1)} %summed.1.refs_0_), channel_id=1, source_target_pairs={{0,16},{16,0},{32,48},{48,32},{1,17},{17,1},{33,49},{49,33},{2,18}... | collective-permute-start | bytes 393224 | tf_op jit(solution)/shard_map/ppermute | solution.py:19
  65.3 5.2 %collective-permute-start.24 = (bf16[128,512]{1,0:T(8,128)(2,1)S(1)}, bf16[128,512]{1,0:T(8,128)(2,1)S(1)}, u32[]{:S(2)}, u32[]{:S(2)}) collective-permute-start(bf16[128,512]{1,0:T(8,128)(2,1)S(1)} %summed.1.refs_0_), channel_id=1, source_target_pairs={{0,32},{16,48},{32,0},{48,16},{1,33},{17,49},{33,1},{49,17},{2,34}... | collective-permute-start | bytes 393224 | tf_op jit(solution)/shard_map/ppermute | solution.py:19
  66.3 7.4 %collective-permute-start.25 = (bf16[128,512]{1,0:T(8,128)(2,1)S(1)}, bf16[128,512]{1,0:T(8,128)(2,1)S(1)}, u32[]{:S(2)}, u32[]{:S(2)}) collective-permute-start(bf16[128,512]{1,0:T(8,128)(2,1)S(1)} %summed.1.refs_0_), channel_id=1, source_target_pairs={{0,48},{16,32},{32,16},{48,0},{1,49},{17,33},{33,17},{49,1},{2,50}... | collective-permute-start | bytes 393224 | tf_op jit(solution)/shard_map/ppermute | solution.py:19
  74.1 11.5 %collective-permute-start.27 = (bf16[128,512]{1,0:T(8,128)(2,1)S(1)}, bf16[128,512]{1,0:T(8,128)(2,1)S(1)}, u32[]{:S(2)}, u32[]{:S(2)}) collective-permute-start(bf16[128,512]{1,0:T(8,128)(2,1)S(1)} %get-tuple-element.30), channel_id=1, source_target_pairs={{0,64},{64,0},{128,192},{192,128},{1,65},{65,1},{129,193},{193,129... | collective-permute-start | bytes 393224 | tf_op jit(solution)/shard_map/ppermute | solution.py:19
  76.2 13.6 %collective-permute-start.28 = (bf16[128,512]{1,0:T(8,128)(2,1)S(1)}, bf16[128,512]{1,0:T(8,128)(2,1)S(1)}, u32[]{:S(2)}, u32[]{:S(2)}) collective-permute-start(bf16[128,512]{1,0:T(8,128)(2,1)S(1)} %get-tuple-element.31), channel_id=1, source_target_pairs={{0,128},{64,192},{128,0},{192,64},{1,129},{65,193},{129,1},{193,65... | collective-permute-start | bytes 393224 | tf_op jit(solution)/shard_map/ppermute | solution.py:19
  80.7 10.3 %collective-permute-start.29 = (bf16[128,512]{1,0:T(8,128)(2,1)S(1)}, bf16[128,512]{1,0:T(8,128)(2,1)S(1)}, u32[]{:S(2)}, u32[]{:S(2)}) collective-permute-start(bf16[128,512]{1,0:T(8,128)(2,1)S(1)} %get-tuple-element.32), channel_id=1, source_target_pairs={{0,192},{64,128},{128,64},{192,0},{1,193},{65,129},{129,65},{193,1... | collective-permute-start | bytes 393224 | tf_op jit(solution)/shard_map/ppermute | solution.py:19
  80.7 1.2 %collective-permute-start.26 = (f32[2]{0:T(128)S(1)}, f32[2]{0:T(128)S(1)}, u32[]{:S(2)}, u32[]{:S(2)}) collective-permute-start(f32[2]{0:T(128)S(1)} %copy-done.6), channel_id=1, source_target_pairs={{0,1},{1,0},{2,3},{3,2},{4,5},{5,4},{6,7},{7,6},{8,9},{9,8},{10,11... | collective-permute-start | bytes 32 | tf_op jit(solution)/shard_map/ppermute | solution.py:247
  (6 other events, 76.8 us)

commit v5 on v4

--- a/solution.py
+++ b/solution.py
@@ -20,7 +20,7 @@
 
 
 def doubled(block, axis):
-    other = lax.ppermute(block, axis, SWAP)
+    other = exchange(block, ("y2", "y1"), 3) if axis == "y2" else exchange(block, (axis,), 1)
     low = lax.axis_index(axis) == 0
     return jnp.concatenate([jnp.where(low, block, other), jnp.where(low, other, block)], axis=0)
 
@@ -39,14 +39,8 @@
     return place
 
 
-def scale_kernel(mine, other, gap_0, gap_1, rows, aux_cols, scaled_0, scaled_1, aux_to, landed):
-    core, here = lax.axis_index("tm"), index_over(*COL)
-    fetches = []
-    for g, s in enumerate(NEAR):
-        block = aux_cols.at[:, pl.ds(pl.multiple_of((2 * (here ^ s) + core) * 128, 128), 128)]
-        fetches.append(pltpu.make_async_copy(block, aux_to.at[g], landed.at[g]))
-        fetches[g].start()
-
+def scale_kernel(mine, other, gap_0, gap_1, rows, scaled_0, scaled_1):
+    core = lax.axis_index("tm")
     first, outer, inner = core == 0, index_over("z2", "z1"), index_over("z0", "xh")
     times = [jnp.where(first == low, mine[i], other[i]) for low in (True, False) for i in range(2)]
     lane = lax.broadcasted_iota(jnp.int32, (1, 128), 1) // 32
@@ -65,22 +59,18 @@
             for t in range(4):
                 made = piece * jnp.exp(-gap * times[t])
                 scaled[t * 128 : t * 128 + 128, m2 * 128 : m2 * 128 + 128] = made.astype(jnp.bfloat16)
-    for fetch in fetches:
-        fetch.wait()
-
-
-def scaled_rows(mine, other, occ_gap, emp_gap, rows, aux_cols):
+
+
+def scaled_rows(mine, other, occ_gap, emp_gap, rows):
     return pl.pallas_call(
         scale_kernel,
         name="scaled_rows",
-        out_shape=[jax.ShapeDtypeStruct((512, 512), jnp.bfloat16)] * 2
-        + [jax.ShapeDtypeStruct((8, 512, 128), jnp.bfloat16)],
-        in_specs=[SCALARS] * 2 + vmem(3) + [pl.BlockSpec(memory_space=pltpu.HBM)],
-        out_specs=vmem(3),
-        scratch_shapes=[pltpu.SemaphoreType.DMA((8,))],
+        out_shape=[jax.ShapeDtypeStruct((512, 512), jnp.bfloat16)] * 2,
+        in_specs=[SCALARS] * 2 + vmem(3),
+        out_specs=vmem(2),
         compiler_params=SMALL,
         cost_estimate=pl.CostEstimate(flops=1_000_000, bytes_accessed=3_800_000, transcendentals=0),
-    )(mine, other, occ_gap.reshape(4, 128), emp_gap.reshape(4, 128), rows, aux_cols)
+    )(mine, other, occ_gap.reshape(4, 128), emp_gap.reshape(4, 128), rows)
 
 
 def chi_kernel(scaled_a, scaled_b, *refs):
@@ -108,24 +98,34 @@
     )(scaled_a, scaled_b, *cols_a, *cols_b)
 
 
-def turn_kernel(aux, mine, theirs):
+def turn_kernel(aux, aux_cols, mine, theirs, aux_to, landed):
+    core, owner = lax.axis_index("tm"), index_over(*COL)
+    fetches = []
+    for g, s in enumerate(NEAR):
+        block = aux_cols.at[:, pl.ds(pl.multiple_of((2 * (owner ^ s) + core) * 128, 128), 128)]
+        fetches.append(pltpu.make_async_copy(block, aux_to.at[g], landed.at[g]))
+        fetches[g].start()
     here = lax.axis_index("xh")
     for blocks, xh in ((mine, here), (theirs, 1 - here)):
         for n in range(8):
             at = pl.ds(pl.multiple_of((2 * n + xh) * 128, 128), 128)
             blocks[n] = aux[:, at].T
-
-
-def turned(aux_rows):
+    for fetch in fetches:
+        fetch.wait()
+
+
+def turned(aux_rows, aux_cols):
     return pl.pallas_call(
         turn_kernel,
         name="turned",
-        out_shape=[jax.ShapeDtypeStruct((8, 128, 128), jnp.bfloat16)] * 2,
-        in_specs=vmem(1),
-        out_specs=vmem(2),
+        out_shape=[jax.ShapeDtypeStruct((8, 128, 128), jnp.bfloat16)] * 2
+        + [jax.ShapeDtypeStruct((8, 512, 128), jnp.bfloat16)],
+        in_specs=vmem(1) + [pl.BlockSpec(memory_space=pltpu.HBM)],
+        out_specs=vmem(3),
+        scratch_shapes=[pltpu.SemaphoreType.DMA((8,))],
         compiler_params=SMALL,
         cost_estimate=pl.CostEstimate(flops=500_000, bytes_accessed=1_000_000, transcendentals=0),
-    )(aux_rows)
+    )(aux_rows, aux_cols)
 
 
 def sum_kernel(*refs):
@@ -223,9 +223,10 @@
         rows = doubled(rows, axis)
 
     other_times = lax.ppermute(times, "tm", SWAP)
-    scaled_a, scaled_b, aux_to = scaled_rows(times, other_times, occ_gap, emp_gap, rows, aux_cols)
-
-    mine, theirs = turned(aux_rows)
+    other_weights = lax.ppermute(time_weights, "tm", SWAP)
+    scaled_a, scaled_b = scaled_rows(times, other_times, occ_gap, emp_gap, rows)
+
+    mine, theirs, aux_to = turned(aux_rows, aux_cols)
     xh_aux = exchange(theirs, "xh", 1)
 
     chi = chi_times(scaled_a, scaled_b, cols_a, cols_b)
@@ -241,10 +242,9 @@
     right = summed(parts)
     right = [right] + [exchange(right, ("z0", "xh"), m) for m in (1, 2, 3)]
     parts = left_parts(mine, xh_aux, z_aux, right)
-    held = lax.optimization_barrier((parts[0], times, other_times, time_weights, freqs))
-    own, times, other_times, time_weights, freqs = held
+    held = lax.optimization_barrier((parts[0], times, other_times, time_weights, other_weights, freqs))
+    own, times, other_times, time_weights, other_weights, freqs = held
     parts = [own] + [exchange(parts[e], ("z2", "z1"), e) for e in (1, 2, 3)]
-    other_weights = lax.ppermute(time_weights, "tm", SWAP)
     moments = jnp.where(first, jnp.stack([times, other_times]), jnp.stack([other_times, times])).reshape(4)
     weights = jnp.where(first, jnp.stack([time_weights, other_weights]), jnp.stack([other_weights, time_weights]))
     coef = weights.reshape(1, 4) * jnp.cos(freqs[:, None] * moments[None, :])

time: 92.7 us -> 89.6 us (0.967)
  waiting for transfers between devices: 36.1 us -> 34.1 us
    ppermute x3 -> x0, starting transfers between devices: 6.23 us -> none  [doubled(): other = lax.ppermute(block, axis, SWAP)]
    ppermute x21 -> x24, starting transfers between devices: 37.4 us -> 43.2 us  [exchange(): lax.ppermute(block, axes, [(i, i ^ mask) for i in range(lax.axis_size(axe...]
    ppermute x3 -> x0, waiting for transfers between devices: 2.43 us -> none  [doubled(): other = lax.ppermute(block, axis, SWAP)]
    ppermute x21 -> x24, waiting for transfers between devices: 32.6 us -> 34.1 us  [exchange(): lax.ppermute(block, axes, [(i, i ^ mask) for i in range(lax.axis_size(axe...]
    ppermute x1, waiting for transfers between devices: 1.05 us -> 0.01 us  [per_device(): other_weights = lax.ppermute(time_weights, 'tm', SWAP)]
    unnamed x16 -> x14, local copies, waits for them, and re-layouts: 3.08 us -> 2.66 us
  transfers between devices with their start and end apart: 30 -> 30, of which waited for: 14 -> 13; matrix products, arithmetic and copies ran while one was open for 4% -> 4% of each run, Pallas kernels for 2% -> 3%
where the time goes in v5:
time: 89.6 us; the launch traced here: 89.3 us
  starting transfers between devices  43.8 us (49%)
  waiting for transfers between devices  34.1 us (38%)
  Pallas kernels  4.12 us (5%)
  local copies, waits for them, and re-layouts  2.83 us (3%)
  matrix products  2.35 us (3%)
  other arithmetic  1.8 us (2%)
    ppermute x24, starting transfers between devices, exchange(): lax.ppermute(block, axes, [(i, i ^ mask) for i in range(lax.axis_size(axe...  43.2 us
    ppermute x24, waiting for transfers between devices, exchange(): lax.ppermute(block, axes, [(i, i ^ mask) for i in range(lax.axis_size(axe...  34.1 us
    unnamed x14, local copies, waits for them, and re-layouts  2.66 us
    dot_general x8, matrix products, per_device(): part = jnp.dot(chi, aux_to[g], preferred_element_type=jnp.float32)  2.35 us
  transfers between devices with their start and end apart: 30, of which 13 were waited for; matrix products, arithmetic and copies ran while one was open for 4% of the time, Pallas kernels for 3%

profile of v5, /device:TPU:32, one launch (start us, length us, event | category | flops | bytes accessed | tf_op | source)
XLA Modules:
  0.0 89.3 jit_solution(10607462602549556545)
XLA Ops:
  0.8 1.6 %collective-permute-start.3 = (bf16[64,256]{1,0:T(8,128)(2,1)S(1)}, bf16[64,256]{1,0:T(8,128)(2,1)S(1)}, u32[]{:S(2)}, u32[]{:S(2)}) collective-permute-start(bf16[64,256]{1,0:T(8,128)(2,1)S(1)} %pad_maximum_fusion.4), channel_id=1, source_target_pairs={{0,2},{2,0},{1,3},{3,1},{4,6},{6,4},{5,7},{7,5},{8,10},{10,8},{9,1... | collective-permute-start | bytes 98312 | tf_op jit(solution)/shard_map/ppermute | solution.py:19
  2.3 2.4 %collective-permute-done.3 = bf16[64,256]{1,0:T(8,128)(2,1)S(1)} collective-permute-done((bf16[64,256]{1,0:T(8,128)(2,1)S(1)}, bf16[64,256]{1,0:T(8,128)(2,1)S(1)}, u32[]{:S(2)}, u32[]{:S(2)}) %collective-permute-start.3) | collective-permute-done | bytes 32800 | tf_op jit(solution)/shard_map/ppermute | solution.py:19
  4.8 1.7 %collective-permute-start.4 = (bf16[128,256]{1,0:T(8,128)(2,1)S(1)}, bf16[128,256]{1,0:T(8,128)(2,1)S(1)}, u32[]{:S(2)}, u32[]{:S(2)}) collective-permute-start(bf16[128,256]{1,0:T(8,128)(2,1)S(1)} %pad_maximum_fusion.3), channel_id=1, source_target_pairs={{0,4},{4,0},{1,5},{5,1},{2,6},{6,2},{3,7},{7,3},{8,12},{12,8},{9,1... | collective-permute-start | bytes 196616 | tf_op jit(solution)/shard_map/ppermute | solution.py:19
  7.2 5.4 %collective-permute-start.8 = (bf16[32,512]{1,0:T(8,128)(2,1)S(1)}, bf16[32,512]{1,0:T(8,128)(2,1)S(1)}, u32[]{:S(2)}, u32[]{:S(2)}) collective-permute-start(bf16[32,512]{1,0:T(8,128)(2,1)S(1)} %select_bitcast_fusion), channel_id=1, source_target_pairs={{0,192},{64,128},{128,64},{192,0},{1,193},{65,129},{129,65},{193,1... | collective-permute-start | bytes 98312 | tf_op jit(solution)/shard_map/ppermute | solution.py:19
  12.6 1.4 %collective-permute-start.7 = (bf16[32,512]{1,0:T(8,128)(2,1)S(1)}, bf16[32,512]{1,0:T(8,128)(2,1)S(1)}, u32[]{:S(2)}, u32[]{:S(2)}) collective-permute-start(bf16[32,512]{1,0:T(8,128)(2,1)S(1)} %select_bitcast_fusion), channel_id=1, source_target_pairs={{0,128},{64,192},{128,0},{192,64},{1,129},{65,193},{129,1},{193,65... | collective-permute-start | bytes 98312 | tf_op jit(solution)/shard_map/ppermute | solution.py:19
  15.2 2.3 %collective-permute-start.5 = (bf16[256,256]{1,0:T(8,128)(2,1)S(1)}, bf16[256,256]{1,0:T(8,128)(2,1)S(1)}, u32[]{:S(2)}, u32[]{:S(2)}) collective-permute-start(bf16[256,256]{1,0:T(8,128)(2,1)S(1)} %pad_maximum_fusion.1), channel_id=1, source_target_pairs={{0,12},{4,8},{8,4},{12,0},{1,13},{5,9},{9,5},{13,1},{2,14},{6,10},... | collective-permute-start | bytes 393224 | tf_op jit(solution)/shard_map/ppermute | solution.py:19
  17.4 1.6 %copy-done = bf16[512,2048]{1,0:T(8,128)(2,1)S(1)} copy-done((bf16[512,2048]{1,0:T(8,128)(2,1)S(1)}, bf16[512,2048]{1,0:T(8,128)(2,1)}, u32[]{:S(2)}) %copy-start) | copy-done | bytes 2097176
  19.0 1.0 %copy-done.1 = bf16[128,2048]{1,0:T(8,128)(2,1)S(1)} copy-done((bf16[128,2048]{1,0:T(8,128)(2,1)S(1)}, bf16[128,2048]{1,0:T(8,128)(2,1)}, u32[]{:S(2)}) %copy-start.1) | copy-done | bytes 524312
  20.7 3.1 %collective-permute-start = (bf16[8,128,128]{2,1,0:T(8,128)(2,1)S(1)}, bf16[8,128,128]{2,1,0:T(8,128)(2,1)S(1)}, u32[]{:S(2)}, u32[]{:S(2)}) collective-permute-start(bf16[8,128,128]{2,1,0:T(8,128)(2,1)S(1)} %get-tuple-element.21), channel_id=1, source_target_pairs={{0,16},{16,0},{1,17},{17,1},{2,18},{18,2},{3,19},{19,3},{4,20},{20... | collective-permute-start | bytes 786440 | tf_op jit(solution)/shard_map/ppermute | solution.py:19
  23.8 1.0 %collective-permute-start.11 = (bf16[128,512]{1,0:T(8,128)(2,1)S(1)}, bf16[128,512]{1,0:T(8,128)(2,1)S(1)}, u32[]{:S(2)}, u32[]{:S(2)}) collective-permute-start(bf16[128,512]{1,0:T(8,128)(2,1)S(1)} %pad_maximum_fusion.2.refs_0_), channel_id=1, source_target_pairs={{0,48},{16,32},{32,16},{48,0},{1,49},{17,33},{33,17},{49,1},{2,50}... | collective-permute-start | bytes 393224 | tf_op jit(solution)/shard_map/ppermute | solution.py:19
  25.9 3.0 %collective-permute-start.9 = (bf16[128,512]{1,0:T(8,128)(2,1)S(1)}, bf16[128,512]{1,0:T(8,128)(2,1)S(1)}, u32[]{:S(2)}, u32[]{:S(2)}) collective-permute-start(bf16[128,512]{1,0:T(8,128)(2,1)S(1)} %pad_maximum_fusion.2.refs_0_), channel_id=1, source_target_pairs={{0,16},{16,0},{32,48},{48,32},{1,17},{17,1},{33,49},{49,33},{2,18}... | collective-permute-start | bytes 393224 | tf_op jit(solution)/shard_map/ppermute | solution.py:19
  29.0 3.7 %collective-permute-done.11.refs_3_ = bf16[128,512]{1,0:T(8,128)(2,1)S(1)} collective-permute-done((bf16[128,512]{1,0:T(8,128)(2,1)S(1)}, bf16[128,512]{1,0:T(8,128)(2,1)S(1)}, u32[]{:S(2)}, u32[]{:S(2)}) %collective-permute-start.11) | collective-permute-done | bytes 131104 | tf_op jit(solution)/shard_map/ppermute | solution.py:19
  33.2 3.4 %collective-permute-done.9.refs_1_ = bf16[128,512]{1,0:T(8,128)(2,1)S(1)} collective-permute-done((bf16[128,512]{1,0:T(8,128)(2,1)S(1)}, bf16[128,512]{1,0:T(8,128)(2,1)S(1)}, u32[]{:S(2)}, u32[]{:S(2)}) %collective-permute-start.9) | collective-permute-done | bytes 131104 | tf_op jit(solution)/shard_map/ppermute | solution.py:19
  37.6 1.1 %collective-permute-start.1 = (bf16[2,4,128,128]{3,2,1,0:T(8,128)(2,1)S(1)}, bf16[2,4,128,128]{3,2,1,0:T(8,128)(2,1)S(1)}, u32[]{:S(2)}, u32[]{:S(2)}) collective-permute-start(bf16[2,4,128,128]{3,2,1,0:T(8,128)(2,1)S(1)} %fusion.1), channel_id=1, source_target_pairs={{0,32},{32,0},{1,33},{33,1},{2,34},{34,2},{3,35},{35,3},{4,36},{36... | collective-permute-start | bytes 786440 | tf_op jit(solution)/shard_map/ppermute | solution.py:19
  41.2 1.8 %collective-permute-start.16 = (bf16[512,128]{1,0:T(8,128)(2,1)S(1)}, bf16[512,128]{1,0:T(8,128)(2,1)S(1)}, u32[]{:S(2)}, u32[]{:S(2)}) collective-permute-start(bf16[512,128]{1,0:T(8,128)(2,1)S(1)} %convolution_convert_fusion.6), channel_id=1, source_target_pairs={{0,2},{2,0},{4,6},{6,4},{8,10},{10,8},{12,14},{14,12},{1,3},{3,1},... | collective-permute-start | bytes 393224 | tf_op jit(solution)/shard_map/ppermute | solution.py:19
  44.4 1.1 %collective-permute-start.19 = (bf16[512,128]{1,0:T(8,128)(2,1)S(1)}, bf16[512,128]{1,0:T(8,128)(2,1)S(1)}, u32[]{:S(2)}, u32[]{:S(2)}) collective-permute-start(bf16[512,128]{1,0:T(8,128)(2,1)S(1)} %convolution_convert_fusion.3), channel_id=1, source_target_pairs={{0,6},{2,4},{4,2},{6,0},{8,14},{10,12},{12,10},{14,8},{1,7},{3,5},... | collective-permute-start | bytes 393224 | tf_op jit(solution)/shard_map/ppermute | solution.py:19
  45.8 1.6 %collective-permute-done.16.refs_0_ = bf16[512,128]{1,0:T(8,128)(2,1)S(1)} collective-permute-done((bf16[512,128]{1,0:T(8,128)(2,1)S(1)}, bf16[512,128]{1,0:T(8,128)(2,1)S(1)}, u32[]{:S(2)}, u32[]{:S(2)}) %collective-permute-start.16) | collective-permute-done | bytes 131104 | tf_op jit(solution)/shard_map/ppermute | solution.py:19
  47.4 1.9 %collective-permute-start.20 = (bf16[512,128]{1,0:T(8,128)(2,1)S(1)}, bf16[512,128]{1,0:T(8,128)(2,1)S(1)}, u32[]{:S(2)}, u32[]{:S(2)}) collective-permute-start(bf16[512,128]{1,0:T(8,128)(2,1)S(1)} %convolution_convert_fusion.2), channel_id=1, source_target_pairs={{0,14},{2,12},{4,10},{6,8},{8,6},{10,4},{12,2},{14,0},{1,15},{3,13... | collective-permute-start | bytes 393224 | tf_op jit(solution)/shard_map/ppermute | solution.py:19
  49.2 1.9 %collective-permute-done.17.refs_1_ = bf16[512,128]{1,0:T(8,128)(2,1)S(1)} collective-permute-done((bf16[512,128]{1,0:T(8,128)(2,1)S(1)}, bf16[512,128]{1,0:T(8,128)(2,1)S(1)}, u32[]{:S(2)}, u32[]{:S(2)}) %collective-permute-start.17) | collective-permute-done | bytes 131104 | tf_op jit(solution)/shard_map/ppermute | solution.py:19
  51.5 2.5 %collective-permute-start.22 = (bf16[512,128]{1,0:T(8,128)(2,1)S(1)}, bf16[512,128]{1,0:T(8,128)(2,1)S(1)}, u32[]{:S(2)}, u32[]{:S(2)}) collective-permute-start(bf16[512,128]{1,0:T(8,128)(2,1)S(1)} %convolution_convert_fusion), channel_id=1, source_target_pairs={{0,10},{2,8},{4,14},{6,12},{8,2},{10,0},{12,6},{14,4},{1,11},{3,9}... | collective-permute-start | bytes 393224 | tf_op jit(solution)/shard_map/ppermute | solution.py:19
  54.3 1.5 %collective-permute-done.20.refs_4_ = bf16[512,128]{1,0:T(8,128)(2,1)S(1)} collective-permute-done((bf16[512,128]{1,0:T(8,128)(2,1)S(1)}, bf16[512,128]{1,0:T(8,128)(2,1)S(1)}, u32[]{:S(2)}, u32[]{:S(2)}) %collective-permute-start.20) | collective-permute-done | bytes 131104 | tf_op jit(solution)/shard_map/ppermute | solution.py:19
  55.8 4.1 %collective-permute-done.21.refs_5_ = bf16[512,128]{1,0:T(8,128)(2,1)S(1)} collective-permute-done((bf16[512,128]{1,0:T(8,128)(2,1)S(1)}, bf16[512,128]{1,0:T(8,128)(2,1)S(1)}, u32[]{:S(2)}, u32[]{:S(2)}) %collective-permute-start.21) | collective-permute-done | bytes 131104 | tf_op jit(solution)/shard_map/ppermute | solution.py:19
  60.1 3.3 %collective-permute-start.25 = (bf16[128,512]{1,0:T(8,128)(2,1)S(1)}, bf16[128,512]{1,0:T(8,128)(2,1)S(1)}, u32[]{:S(2)}, u32[]{:S(2)}) collective-permute-start(bf16[128,512]{1,0:T(8,128)(2,1)S(1)} %summed.1.refs_0_), channel_id=1, source_target_pairs={{0,48},{16,32},{32,16},{48,0},{1,49},{17,33},{33,17},{49,1},{2,50}... | collective-permute-start | bytes 393224 | tf_op jit(solution)/shard_map/ppermute | solution.py:19
  65.2 2.5 %collective-permute-done.25.refs_3_ = bf16[128,512]{1,0:T(8,128)(2,1)S(1)} collective-permute-done((bf16[128,512]{1,0:T(8,128)(2,1)S(1)}, bf16[128,512]{1,0:T(8,128)(2,1)S(1)}, u32[]{:S(2)}, u32[]{:S(2)}) %collective-permute-start.25) | collective-permute-done | bytes 131104 | tf_op jit(solution)/shard_map/ppermute | solution.py:19
  67.6 1.1 %collective-permute-done.24.refs_2_ = bf16[128,512]{1,0:T(8,128)(2,1)S(1)} collective-permute-done((bf16[128,512]{1,0:T(8,128)(2,1)S(1)}, bf16[128,512]{1,0:T(8,128)(2,1)S(1)}, u32[]{:S(2)}, u32[]{:S(2)}) %collective-permute-start.24) | collective-permute-done | bytes 131104 | tf_op jit(solution)/shard_map/ppermute | solution.py:19
  68.7 2.1 %collective-permute-done.23.refs_1_ = bf16[128,512]{1,0:T(8,128)(2,1)S(1)} collective-permute-done((bf16[128,512]{1,0:T(8,128)(2,1)S(1)}, bf16[128,512]{1,0:T(8,128)(2,1)S(1)}, u32[]{:S(2)}, u32[]{:S(2)}) %collective-permute-start.23) | collective-permute-done | bytes 131104 | tf_op jit(solution)/shard_map/ppermute | solution.py:19
  71.5 1.5 %collective-permute-start.27 = (bf16[128,512]{1,0:T(8,128)(2,1)S(1)}, bf16[128,512]{1,0:T(8,128)(2,1)S(1)}, u32[]{:S(2)}, u32[]{:S(2)}) collective-permute-start(bf16[128,512]{1,0:T(8,128)(2,1)S(1)} %get-tuple-element.32), channel_id=1, source_target_pairs={{0,64},{64,0},{128,192},{192,128},{1,65},{65,1},{129,193},{193,129... | collective-permute-start | bytes 393224 | tf_op jit(solution)/shard_map/ppermute | solution.py:19
  72.9 4.9 %collective-permute-start.28 = (bf16[128,512]{1,0:T(8,128)(2,1)S(1)}, bf16[128,512]{1,0:T(8,128)(2,1)S(1)}, u32[]{:S(2)}, u32[]{:S(2)}) collective-permute-start(bf16[128,512]{1,0:T(8,128)(2,1)S(1)} %get-tuple-element.33), channel_id=1, source_target_pairs={{0,128},{64,192},{128,0},{192,64},{1,129},{65,193},{129,1},{193,65... | collective-permute-start | bytes 393224 | tf_op jit(solution)/shard_map/ppermute | solution.py:19
  78.1 3.2 %collective-permute-done.27.refs_1_ = bf16[128,512]{1,0:T(8,128)(2,1)S(1)} collective-permute-done((bf16[128,512]{1,0:T(8,128)(2,1)S(1)}, bf16[128,512]{1,0:T(8,128)(2,1)S(1)}, u32[]{:S(2)}, u32[]{:S(2)}) %collective-permute-start.27) | collective-permute-done | bytes 131104 | tf_op jit(solution)/shard_map/ppermute | solution.py:19
  81.3 2.5 %collective-permute-done.28.refs_2_ = bf16[128,512]{1,0:T(8,128)(2,1)S(1)} collective-permute-done((bf16[128,512]{1,0:T(8,128)(2,1)S(1)}, bf16[128,512]{1,0:T(8,128)(2,1)S(1)}, u32[]{:S(2)}, u32[]{:S(2)}) %collective-permute-start.28) | collective-permute-done | bytes 131104 | tf_op jit(solution)/shard_map/ppermute | solution.py:19
  83.8 4.1 %collective-permute-done.29.refs_3_ = bf16[128,512]{1,0:T(8,128)(2,1)S(1)} collective-permute-done((bf16[128,512]{1,0:T(8,128)(2,1)S(1)}, bf16[128,512]{1,0:T(8,128)(2,1)S(1)}, u32[]{:S(2)}, u32[]{:S(2)}) %collective-permute-start.29) | collective-permute-done | bytes 131104 | tf_op jit(solution)/shard_map/ppermute | solution.py:19
  87.9 1.4 %mix.1 = f32[4,128,128]{2,1,0:T(8,128)} custom-call(f32[4,4]{1,0:T(4,128)S(1)} %cosine_multiply_fusion.coef, f32[128,512]{1,0:T(8,128)S(1)} %get-tuple-element.31.refs_0_, bf16[128,512]{1,0:T(8,128)(2,1)S(1)} %collective-permute-done.27.refs_1_, bf16[128,512]{1,0:T(8,128)(2,1)S(1)} %collective-permute-done.28.refs_2_, ...), custom_call_target="tpu_custom_call" | custom-call | tf_op jit(solution)/shard_map/mix/pallas_call | solution.py:186
  (71 shorter events, 13.5 us)
Async XLA Ops:
  0.8 4.0 %collective-permute-start.3 = (bf16[64,256]{1,0:T(8,128)(2,1)S(1)}, bf16[64,256]{1,0:T(8,128)(2,1)S(1)}, u32[]{:S(2)}, u32[]{:S(2)}) collective-permute-start(bf16[64,256]{1,0:T(8,128)(2,1)S(1)} %pad_maximum_fusion.4), channel_id=1, source_target_pairs={{0,2},{2,0},{1,3},{3,1},{4,6},{6,4},{5,7},{7,5},{8,10},{10,8},{9,1... | collective-permute-start | bytes 98312 | tf_op jit(solution)/shard_map/ppermute | solution.py:19
  4.8 10.3 %collective-permute-start.4 = (bf16[128,256]{1,0:T(8,128)(2,1)S(1)}, bf16[128,256]{1,0:T(8,128)(2,1)S(1)}, u32[]{:S(2)}, u32[]{:S(2)}) collective-permute-start(bf16[128,256]{1,0:T(8,128)(2,1)S(1)} %pad_maximum_fusion.3), channel_id=1, source_target_pairs={{0,4},{4,0},{1,5},{5,1},{2,6},{6,2},{3,7},{7,3},{8,12},{12,8},{9,1... | collective-permute-start | bytes 196616 | tf_op jit(solution)/shard_map/ppermute | solution.py:19
  7.2 13.4 %collective-permute-start.8 = (bf16[32,512]{1,0:T(8,128)(2,1)S(1)}, bf16[32,512]{1,0:T(8,128)(2,1)S(1)}, u32[]{:S(2)}, u32[]{:S(2)}) collective-permute-start(bf16[32,512]{1,0:T(8,128)(2,1)S(1)} %select_bitcast_fusion), channel_id=1, source_target_pairs={{0,192},{64,128},{128,64},{192,0},{1,193},{65,129},{129,65},{193,1... | collective-permute-start | bytes 98312 | tf_op jit(solution)/shard_map/ppermute | solution.py:19
  12.6 11.2 %collective-permute-start.7 = (bf16[32,512]{1,0:T(8,128)(2,1)S(1)}, bf16[32,512]{1,0:T(8,128)(2,1)S(1)}, u32[]{:S(2)}, u32[]{:S(2)}) collective-permute-start(bf16[32,512]{1,0:T(8,128)(2,1)S(1)} %select_bitcast_fusion), channel_id=1, source_target_pairs={{0,128},{64,192},{128,0},{192,64},{1,129},{65,193},{129,1},{193,65... | collective-permute-start | bytes 98312 | tf_op jit(solution)/shard_map/ppermute | solution.py:19
  14.1 9.7 %collective-permute-start.6 = (bf16[32,512]{1,0:T(8,128)(2,1)S(1)}, bf16[32,512]{1,0:T(8,128)(2,1)S(1)}, u32[]{:S(2)}, u32[]{:S(2)}) collective-permute-start(bf16[32,512]{1,0:T(8,128)(2,1)S(1)} %select_bitcast_fusion), channel_id=1, source_target_pairs={{0,64},{64,0},{128,192},{192,128},{1,65},{65,1},{129,193},{193,129... | collective-permute-start | bytes 98312 | tf_op jit(solution)/shard_map/ppermute | solution.py:19
  15.2 10.7 %collective-permute-start.5 = (bf16[256,256]{1,0:T(8,128)(2,1)S(1)}, bf16[256,256]{1,0:T(8,128)(2,1)S(1)}, u32[]{:S(2)}, u32[]{:S(2)}) collective-permute-start(bf16[256,256]{1,0:T(8,128)(2,1)S(1)} %pad_maximum_fusion.1), channel_id=1, source_target_pairs={{0,12},{4,8},{8,4},{12,0},{1,13},{5,9},{9,5},{13,1},{2,14},{6,10},... | collective-permute-start | bytes 393224 | tf_op jit(solution)/shard_map/ppermute | solution.py:19
  17.4 11.5 %collective-permute-start.2 = (f32[2]{0:T(128)}, f32[2]{0:T(128)S(1)}, u32[]{:S(2)}, u32[]{:S(2)}) collective-permute-start(f32[2]{0:T(128)} %mine.1), channel_id=1, source_target_pairs={{0,1},{1,0},{2,3},{3,2},{4,5},{5,4},{6,7},{7,6},{8,9},{9,8},{10,11... | collective-permute-start | bytes 32 | tf_op jit(solution)/shard_map/ppermute | solution.py:225
  20.7 16.8 %collective-permute-start = (bf16[8,128,128]{2,1,0:T(8,128)(2,1)S(1)}, bf16[8,128,128]{2,1,0:T(8,128)(2,1)S(1)}, u32[]{:S(2)}, u32[]{:S(2)}) collective-permute-start(bf16[8,128,128]{2,1,0:T(8,128)(2,1)S(1)} %get-tuple-element.21), channel_id=1, source_target_pairs={{0,16},{16,0},{1,17},{17,1},{2,18},{18,2},{3,19},{19,3},{4,20},{20... | collective-permute-start | bytes 786440 | tf_op jit(solution)/shard_map/ppermute | solution.py:19
  23.8 8.9 %collective-permute-start.11 = (bf16[128,512]{1,0:T(8,128)(2,1)S(1)}, bf16[128,512]{1,0:T(8,128)(2,1)S(1)}, u32[]{:S(2)}, u32[]{:S(2)}) collective-permute-start(bf16[128,512]{1,0:T(8,128)(2,1)S(1)} %pad_maximum_fusion.2.refs_0_), channel_id=1, source_target_pairs={{0,48},{16,32},{32,16},{48,0},{1,49},{17,33},{33,17},{49,1},{2,50}... | collective-permute-start | bytes 393224 | tf_op jit(solution)/shard_map/ppermute | solution.py:19
  24.8 7.9 %collective-permute-start.10 = (bf16[128,512]{1,0:T(8,128)(2,1)S(1)}, bf16[128,512]{1,0:T(8,128)(2,1)S(1)}, u32[]{:S(2)}, u32[]{:S(2)}) collective-permute-start(bf16[128,512]{1,0:T(8,128)(2,1)S(1)} %pad_maximum_fusion.2.refs_0_), channel_id=1, source_target_pairs={{0,32},{16,48},{32,0},{48,16},{1,33},{17,49},{33,1},{49,17},{2,34}... | collective-permute-start | bytes 393224 | tf_op jit(solution)/shard_map/ppermute | solution.py:19
  25.9 10.7 %collective-permute-start.9 = (bf16[128,512]{1,0:T(8,128)(2,1)S(1)}, bf16[128,512]{1,0:T(8,128)(2,1)S(1)}, u32[]{:S(2)}, u32[]{:S(2)}) collective-permute-start(bf16[128,512]{1,0:T(8,128)(2,1)S(1)} %pad_maximum_fusion.2.refs_0_), channel_id=1, source_target_pairs={{0,16},{16,0},{32,48},{48,32},{1,17},{17,1},{33,49},{49,33},{2,18}... | collective-permute-start | bytes 393224 | tf_op jit(solution)/shard_map/ppermute | solution.py:19
  28.9 9.7 %collective-permute-start.12 = (bf16[128,512]{1,0:T(8,128)(2,1)S(1)}, bf16[128,512]{1,0:T(8,128)(2,1)S(1)}, u32[]{:S(2)}, u32[]{:S(2)}) collective-permute-start(bf16[128,512]{1,0:T(8,128)(2,1)S(1)} %pad_maximum_fusion.2.refs_0_), channel_id=1, source_target_pairs={{0,1},{1,0},{2,3},{3,2},{4,5},{5,4},{6,7},{7,6},{8,9},{9,8},{10,11... | collective-permute-start | bytes 393224 | tf_op jit(solution)/shard_map/ppermute | solution.py:218
  32.7 6.0 %collective-permute-start.15 = (bf16[128,512]{1,0:T(8,128)(2,1)S(1)}, bf16[128,512]{1,0:T(8,128)(2,1)S(1)}, u32[]{:S(2)}, u32[]{:S(2)}) collective-permute-start(bf16[128,512]{1,0:T(8,128)(2,1)S(1)} %collective-permute-done.11.refs_3_), channel_id=1, source_target_pairs={{0,1},{1,0},{2,3},{3,2},{4,5},{5,4},{6,7},{7,6},{8,9},{9,8},{10,11... | collective-permute-start | bytes 393224 | tf_op jit(solution)/shard_map/ppermute | solution.py:218
  32.7 6.0 %collective-permute-start.14 = (bf16[128,512]{1,0:T(8,128)(2,1)S(1)}, bf16[128,512]{1,0:T(8,128)(2,1)S(1)}, u32[]{:S(2)}, u32[]{:S(2)}) collective-permute-start(bf16[128,512]{1,0:T(8,128)(2,1)S(1)} %collective-permute-done.10.refs_2_), channel_id=1, source_target_pairs={{0,1},{1,0},{2,3},{3,2},{4,5},{5,4},{6,7},{7,6},{8,9},{9,8},{10,11... | collective-permute-start | bytes 393224 | tf_op jit(solution)/shard_map/ppermute | solution.py:218
  36.6 2.1 %collective-permute-start.13 = (bf16[128,512]{1,0:T(8,128)(2,1)S(1)}, bf16[128,512]{1,0:T(8,128)(2,1)S(1)}, u32[]{:S(2)}, u32[]{:S(2)}) collective-permute-start(bf16[128,512]{1,0:T(8,128)(2,1)S(1)} %collective-permute-done.9.refs_1_), channel_id=1, source_target_pairs={{0,1},{1,0},{2,3},{3,2},{4,5},{5,4},{6,7},{7,6},{8,9},{9,8},{10,11... | collective-permute-start | bytes 393224 | tf_op jit(solution)/shard_map/ppermute | solution.py:218
  37.6 27.6 %collective-permute-start.1 = (bf16[2,4,128,128]{3,2,1,0:T(8,128)(2,1)S(1)}, bf16[2,4,128,128]{3,2,1,0:T(8,128)(2,1)S(1)}, u32[]{:S(2)}, u32[]{:S(2)}) collective-permute-start(bf16[2,4,128,128]{3,2,1,0:T(8,128)(2,1)S(1)} %fusion.1), channel_id=1, source_target_pairs={{0,32},{32,0},{1,33},{33,1},{2,34},{34,2},{3,35},{35,3},{4,36},{36... | collective-permute-start | bytes 786440 | tf_op jit(solution)/shard_map/ppermute | solution.py:19
  40.9 24.2 %copy-start.5 = (f32[2]{0:T(128)S(1)}, f32[2]{0:T(128)}, u32[]{:S(2)}) copy-start(f32[2]{0:T(128)} %param.18) | copy-start | bytes 28
  41.2 36.7 %copy-start.6 = (f32[4]{0:T(128)S(1)}, f32[4]{0:T(128)}, u32[]{:S(2)}) copy-start(f32[4]{0:T(128)} %param.19) | copy-start | bytes 52
  41.2 6.1 %collective-permute-start.16 = (bf16[512,128]{1,0:T(8,128)(2,1)S(1)}, bf16[512,128]{1,0:T(8,128)(2,1)S(1)}, u32[]{:S(2)}, u32[]{:S(2)}) collective-permute-start(bf16[512,128]{1,0:T(8,128)(2,1)S(1)} %convolution_convert_fusion.6), channel_id=1, source_target_pairs={{0,2},{2,0},{4,6},{6,4},{8,10},{10,8},{12,14},{14,12},{1,3},{3,1},... | collective-permute-start | bytes 393224 | tf_op jit(solution)/shard_map/ppermute | solution.py:19
  43.0 8.1 %collective-permute-start.17 = (bf16[512,128]{1,0:T(8,128)(2,1)S(1)}, bf16[512,128]{1,0:T(8,128)(2,1)S(1)}, u32[]{:S(2)}, u32[]{:S(2)}) collective-permute-start(bf16[512,128]{1,0:T(8,128)(2,1)S(1)} %convolution_convert_fusion.5), channel_id=1, source_target_pairs={{0,4},{2,6},{4,0},{6,2},{8,12},{10,14},{12,8},{14,10},{1,5},{3,7},... | collective-permute-start | bytes 393224 | tf_op jit(solution)/shard_map/ppermute | solution.py:19
  43.7 7.9 %collective-permute-start.18 = (bf16[512,128]{1,0:T(8,128)(2,1)S(1)}, bf16[512,128]{1,0:T(8,128)(2,1)S(1)}, u32[]{:S(2)}, u32[]{:S(2)}) collective-permute-start(bf16[512,128]{1,0:T(8,128)(2,1)S(1)} %convolution_convert_fusion.4), channel_id=1, source_target_pairs={{0,12},{2,14},{4,8},{6,10},{8,4},{10,6},{12,0},{14,2},{1,13},{3,15... | collective-permute-start | bytes 393224 | tf_op jit(solution)/shard_map/ppermute | solution.py:19
  44.4 9.9 %collective-permute-start.19 = (bf16[512,128]{1,0:T(8,128)(2,1)S(1)}, bf16[512,128]{1,0:T(8,128)(2,1)S(1)}, u32[]{:S(2)}, u32[]{:S(2)}) collective-permute-start(bf16[512,128]{1,0:T(8,128)(2,1)S(1)} %convolution_convert_fusion.3), channel_id=1, source_target_pairs={{0,6},{2,4},{4,2},{6,0},{8,14},{10,12},{12,10},{14,8},{1,7},{3,5},... | collective-permute-start | bytes 393224 | tf_op jit(solution)/shard_map/ppermute | solution.py:19
  47.4 8.4 %collective-permute-start.20 = (bf16[512,128]{1,0:T(8,128)(2,1)S(1)}, bf16[512,128]{1,0:T(8,128)(2,1)S(1)}, u32[]{:S(2)}, u32[]{:S(2)}) collective-permute-start(bf16[512,128]{1,0:T(8,128)(2,1)S(1)} %convolution_convert_fusion.2), channel_id=1, source_target_pairs={{0,14},{2,12},{4,10},{6,8},{8,6},{10,4},{12,2},{14,0},{1,15},{3,13... | collective-permute-start | bytes 393224 | tf_op jit(solution)/shard_map/ppermute | solution.py:19
  51.1 8.8 %collective-permute-start.21 = (bf16[512,128]{1,0:T(8,128)(2,1)S(1)}, bf16[512,128]{1,0:T(8,128)(2,1)S(1)}, u32[]{:S(2)}, u32[]{:S(2)}) collective-permute-start(bf16[512,128]{1,0:T(8,128)(2,1)S(1)} %convolution_convert_fusion.1), channel_id=1, source_target_pairs={{0,8},{2,10},{4,12},{6,14},{8,0},{10,2},{12,4},{14,6},{1,9},{3,11}... | collective-permute-start | bytes 393224 | tf_op jit(solution)/shard_map/ppermute | solution.py:19
  51.5 8.4 %collective-permute-start.22 = (bf16[512,128]{1,0:T(8,128)(2,1)S(1)}, bf16[512,128]{1,0:T(8,128)(2,1)S(1)}, u32[]{:S(2)}, u32[]{:S(2)}) collective-permute-start(bf16[512,128]{1,0:T(8,128)(2,1)S(1)} %convolution_convert_fusion), channel_id=1, source_target_pairs={{0,10},{2,8},{4,14},{6,12},{8,2},{10,0},{12,6},{14,4},{1,11},{3,9}... | collective-permute-start | bytes 393224 | tf_op jit(solution)/shard_map/ppermute | solution.py:19
  60.1 7.6 %collective-permute-start.25 = (bf16[128,512]{1,0:T(8,128)(2,1)S(1)}, bf16[128,512]{1,0:T(8,128)(2,1)S(1)}, u32[]{:S(2)}, u32[]{:S(2)}) collective-permute-start(bf16[128,512]{1,0:T(8,128)(2,1)S(1)} %summed.1.refs_0_), channel_id=1, source_target_pairs={{0,48},{16,32},{32,16},{48,0},{1,49},{17,33},{33,17},{49,1},{2,50}... | collective-permute-start | bytes 393224 | tf_op jit(solution)/shard_map/ppermute | solution.py:19
  63.4 5.3 %collective-permute-start.24 = (bf16[128,512]{1,0:T(8,128)(2,1)S(1)}, bf16[128,512]{1,0:T(8,128)(2,1)S(1)}, u32[]{:S(2)}, u32[]{:S(2)}) collective-permute-start(bf16[128,512]{1,0:T(8,128)(2,1)S(1)} %summed.1.refs_0_), channel_id=1, source_target_pairs={{0,32},{16,48},{32,0},{48,16},{1,33},{17,49},{33,1},{49,17},{2,34}... | collective-permute-start | bytes 393224 | tf_op jit(solution)/shard_map/ppermute | solution.py:19
  64.3 6.5 %collective-permute-start.23 = (bf16[128,512]{1,0:T(8,128)(2,1)S(1)}, bf16[128,512]{1,0:T(8,128)(2,1)S(1)}, u32[]{:S(2)}, u32[]{:S(2)}) collective-permute-start(bf16[128,512]{1,0:T(8,128)(2,1)S(1)} %summed.1.refs_0_), channel_id=1, source_target_pairs={{0,16},{16,0},{32,48},{48,32},{1,17},{17,1},{33,49},{49,33},{2,18}... | collective-permute-start | bytes 393224 | tf_op jit(solution)/shard_map/ppermute | solution.py:19
  65.2 6.1 %collective-permute-start.26 = (f32[2]{0:T(128)S(1)}, f32[2]{0:T(128)S(1)}, u32[]{:S(2)}, u32[]{:S(2)}) collective-permute-start(f32[2]{0:T(128)S(1)} %copy-done.5), channel_id=1, source_target_pairs={{0,1},{1,0},{2,3},{3,2},{4,5},{5,4},{6,7},{7,6},{8,9},{9,8},{10,11... | collective-permute-start | bytes 32 | tf_op jit(solution)/shard_map/ppermute | solution.py:226
  71.5 9.8 %collective-permute-start.27 = (bf16[128,512]{1,0:T(8,128)(2,1)S(1)}, bf16[128,512]{1,0:T(8,128)(2,1)S(1)}, u32[]{:S(2)}, u32[]{:S(2)}) collective-permute-start(bf16[128,512]{1,0:T(8,128)(2,1)S(1)} %get-tuple-element.32), channel_id=1, source_target_pairs={{0,64},{64,0},{128,192},{192,128},{1,65},{65,1},{129,193},{193,129... | collective-permute-start | bytes 393224 | tf_op jit(solution)/shard_map/ppermute | solution.py:19
  72.9 10.8 %collective-permute-start.28 = (bf16[128,512]{1,0:T(8,128)(2,1)S(1)}, bf16[128,512]{1,0:T(8,128)(2,1)S(1)}, u32[]{:S(2)}, u32[]{:S(2)}) collective-permute-start(bf16[128,512]{1,0:T(8,128)(2,1)S(1)} %get-tuple-element.33), channel_id=1, source_target_pairs={{0,128},{64,192},{128,0},{192,64},{1,129},{65,193},{129,1},{193,65... | collective-permute-start | bytes 393224 | tf_op jit(solution)/shard_map/ppermute | solution.py:19
  77.9 10.0 %collective-permute-start.29 = (bf16[128,512]{1,0:T(8,128)(2,1)S(1)}, bf16[128,512]{1,0:T(8,128)(2,1)S(1)}, u32[]{:S(2)}, u32[]{:S(2)}) collective-permute-start(bf16[128,512]{1,0:T(8,128)(2,1)S(1)} %get-tuple-element.34), channel_id=1, source_target_pairs={{0,192},{64,128},{128,64},{192,0},{1,193},{65,129},{129,65},{193,1... | collective-permute-start | bytes 393224 | tf_op jit(solution)/shard_map/ppermute | solution.py:19
  (5 other events, 67.2 us)

commit v6 on v5

--- a/solution.py
+++ b/solution.py
@@ -74,7 +74,7 @@
 
 
 def chi_kernel(scaled_a, scaled_b, *refs):
-    arrived_a, arrived_b, (chi, cols_a, cols_b) = refs[:4], refs[4:8], refs[8:]
+    arrived_a, arrived_b, (aux, chi, *parts, cols_a, cols_b) = refs[:4], refs[4:8], refs[8:]
     for m in range(4):
         cols_a[m * 128 : m * 128 + 128, :] = arrived_a[m][...]
         cols_b[m * 128 : m * 128 + 128, :] = arrived_b[m][...]
@@ -83,19 +83,22 @@
         green_a = jnp.dot(scaled_a[here, :], cols_a[...], preferred_element_type=jnp.float32)
         green_b = jnp.dot(scaled_b[here, :], cols_b[...], preferred_element_type=jnp.float32)
         chi[here, :] = (green_a * green_b).astype(jnp.bfloat16)
-
-
-def chi_times(scaled_a, scaled_b, cols_a, cols_b):
+    for g, part in enumerate(parts):
+        part[...] = jnp.dot(chi[...], aux[g], preferred_element_type=jnp.float32).astype(jnp.bfloat16)
+
+
+def chi_times(scaled_a, scaled_b, cols_a, cols_b, aux_to):
     return pl.pallas_call(
         chi_kernel,
         name="chi_times",
-        out_shape=jax.ShapeDtypeStruct((512, 512), jnp.bfloat16),
-        in_specs=vmem(10),
-        out_specs=vmem(1)[0],
+        out_shape=[jax.ShapeDtypeStruct((512, 512), jnp.bfloat16)]
+        + [jax.ShapeDtypeStruct((512, 128), jnp.bfloat16)] * 2,
+        in_specs=vmem(11),
+        out_specs=vmem(3),
         scratch_shapes=[pltpu.VMEM((512, 512), jnp.bfloat16)] * 2,
         compiler_params=SMALL,
         cost_estimate=pl.CostEstimate(flops=540_000_000, bytes_accessed=3_000_000, transcendentals=0),
-    )(scaled_a, scaled_b, *cols_a, *cols_b)
+    )(scaled_a, scaled_b, *cols_a, *cols_b, aux_to)
 
 
 def turn_kernel(aux, aux_cols, mine, theirs, aux_to, landed):
@@ -229,10 +232,10 @@
     mine, theirs, aux_to = turned(aux_rows, aux_cols)
     xh_aux = exchange(theirs, "xh", 1)
 
-    chi = chi_times(scaled_a, scaled_b, cols_a, cols_b)
+    chi, *ready = chi_times(scaled_a, scaled_b, cols_a, cols_b, aux_to)
     parts = []
     for g, s in enumerate(NEAR):
-        part = jnp.dot(chi, aux_to[g], preferred_element_type=jnp.float32)
+        part = ready[g] if g < 2 else jnp.dot(chi, aux_to[g], preferred_element_type=jnp.float32)
         parts.append(exchange(part.astype(jnp.bfloat16), COL, s) if s else part)
 
     z_aux = jnp.stack([mine, xh_aux]).reshape(2, 4, 2, 128, 128)

time: 89.6 us -> 92.6 us (1.033)
  starting transfers between devices: 43.8 us -> 46.5 us
    ppermute x24, starting transfers between devices: 43.2 us -> 45.8 us  [exchange(): lax.ppermute(block, axes, [(i, i ^ mask) for i in range(lax.axis_size(axe...]
    dot_general x8 -> x6, matrix products: 2.35 us -> 1.76 us  [per_device(): jnp.dot(chi, aux_to[g], preferred_element_type=jnp.float32)]
  transfers between devices with their start and end apart: 30 -> 30, of which waited for: 13 -> 12; matrix products, arithmetic and copies ran while one was open for 4% -> 3% of each run, Pallas kernels for 3% -> 3%
where the time goes in v6:
time: 92.6 us; the launch traced here: 92.3 us
  starting transfers between devices  46.5 us (50%)
  waiting for transfers between devices  34.7 us (37%)
  Pallas kernels  4.4 us (5%)
  local copies, waits for them, and re-layouts  2.83 us (3%)
  other arithmetic  1.8 us (2%)
  matrix products  1.76 us (2%)
    ppermute x24, starting transfers between devices, exchange(): lax.ppermute(block, axes, [(i, i ^ mask) for i in range(lax.axis_size(axe...  45.8 us
    ppermute x24, waiting for transfers between devices, exchange(): lax.ppermute(block, axes, [(i, i ^ mask) for i in range(lax.axis_size(axe...  34.7 us
    unnamed x14, local copies, waits for them, and re-layouts  2.66 us
  transfers between devices with their start and end apart: 30, of which 12 were waited for; matrix products, arithmetic and copies ran while one was open for 3% of the time, Pallas kernels for 3%

profile of v6, /device:TPU:32, one launch (start us, length us, event | category | flops | bytes accessed | tf_op | source)
XLA Modules:
  0.0 92.3 jit_solution(3733405941579075139)
XLA Ops:
  0.8 1.6 %collective-permute-start.3 = (bf16[64,256]{1,0:T(8,128)(2,1)S(1)}, bf16[64,256]{1,0:T(8,128)(2,1)S(1)}, u32[]{:S(2)}, u32[]{:S(2)}) collective-permute-start(bf16[64,256]{1,0:T(8,128)(2,1)S(1)} %pad_maximum_fusion.4), channel_id=1, source_target_pairs={{0,2},{2,0},{1,3},{3,1},{4,6},{6,4},{5,7},{7,5},{8,10},{10,8},{9,1... | collective-permute-start | bytes 98312 | tf_op jit(solution)/shard_map/ppermute | solution.py:19
  2.3 2.4 %collective-permute-done.3 = bf16[64,256]{1,0:T(8,128)(2,1)S(1)} collective-permute-done((bf16[64,256]{1,0:T(8,128)(2,1)S(1)}, bf16[64,256]{1,0:T(8,128)(2,1)S(1)}, u32[]{:S(2)}, u32[]{:S(2)}) %collective-permute-start.3) | collective-permute-done | bytes 32800 | tf_op jit(solution)/shard_map/ppermute | solution.py:19
  4.8 1.7 %collective-permute-start.4 = (bf16[128,256]{1,0:T(8,128)(2,1)S(1)}, bf16[128,256]{1,0:T(8,128)(2,1)S(1)}, u32[]{:S(2)}, u32[]{:S(2)}) collective-permute-start(bf16[128,256]{1,0:T(8,128)(2,1)S(1)} %pad_maximum_fusion.3), channel_id=1, source_target_pairs={{0,4},{4,0},{1,5},{5,1},{2,6},{6,2},{3,7},{7,3},{8,12},{12,8},{9,1... | collective-permute-start | bytes 196616 | tf_op jit(solution)/shard_map/ppermute | solution.py:19
  7.2 3.3 %collective-permute-start.6 = (bf16[32,512]{1,0:T(8,128)(2,1)S(1)}, bf16[32,512]{1,0:T(8,128)(2,1)S(1)}, u32[]{:S(2)}, u32[]{:S(2)}) collective-permute-start(bf16[32,512]{1,0:T(8,128)(2,1)S(1)} %select_bitcast_fusion), channel_id=1, source_target_pairs={{0,64},{64,0},{128,192},{192,128},{1,65},{65,1},{129,193},{193,129... | collective-permute-start | bytes 98312 | tf_op jit(solution)/shard_map/ppermute | solution.py:19
  10.5 4.5 %collective-permute-start.7 = (bf16[32,512]{1,0:T(8,128)(2,1)S(1)}, bf16[32,512]{1,0:T(8,128)(2,1)S(1)}, u32[]{:S(2)}, u32[]{:S(2)}) collective-permute-start(bf16[32,512]{1,0:T(8,128)(2,1)S(1)} %select_bitcast_fusion), channel_id=1, source_target_pairs={{0,128},{64,192},{128,0},{192,64},{1,129},{65,193},{129,1},{193,65... | collective-permute-start | bytes 98312 | tf_op jit(solution)/shard_map/ppermute | solution.py:19
  15.1 2.3 %collective-permute-start.5 = (bf16[256,256]{1,0:T(8,128)(2,1)S(1)}, bf16[256,256]{1,0:T(8,128)(2,1)S(1)}, u32[]{:S(2)}, u32[]{:S(2)}) collective-permute-start(bf16[256,256]{1,0:T(8,128)(2,1)S(1)} %pad_maximum_fusion.1), channel_id=1, source_target_pairs={{0,12},{4,8},{8,4},{12,0},{1,13},{5,9},{9,5},{13,1},{2,14},{6,10},... | collective-permute-start | bytes 393224 | tf_op jit(solution)/shard_map/ppermute | solution.py:19
  17.3 1.6 %copy-done = bf16[512,2048]{1,0:T(8,128)(2,1)S(1)} copy-done((bf16[512,2048]{1,0:T(8,128)(2,1)S(1)}, bf16[512,2048]{1,0:T(8,128)(2,1)}, u32[]{:S(2)}) %copy-start) | copy-done | bytes 2097176
  18.9 1.0 %copy-done.1 = bf16[128,2048]{1,0:T(8,128)(2,1)S(1)} copy-done((bf16[128,2048]{1,0:T(8,128)(2,1)S(1)}, bf16[128,2048]{1,0:T(8,128)(2,1)}, u32[]{:S(2)}) %copy-start.1) | copy-done | bytes 524312
  20.6 3.1 %collective-permute-start = (bf16[8,128,128]{2,1,0:T(8,128)(2,1)S(1)}, bf16[8,128,128]{2,1,0:T(8,128)(2,1)S(1)}, u32[]{:S(2)}, u32[]{:S(2)}) collective-permute-start(bf16[8,128,128]{2,1,0:T(8,128)(2,1)S(1)} %get-tuple-element.24), channel_id=1, source_target_pairs={{0,16},{16,0},{1,17},{17,1},{2,18},{18,2},{3,19},{19,3},{4,20},{20... | collective-permute-start | bytes 786440 | tf_op jit(solution)/shard_map/ppermute | solution.py:19
  25.3 3.5 %collective-permute-start.11 = (bf16[128,512]{1,0:T(8,128)(2,1)S(1)}, bf16[128,512]{1,0:T(8,128)(2,1)S(1)}, u32[]{:S(2)}, u32[]{:S(2)}) collective-permute-start(bf16[128,512]{1,0:T(8,128)(2,1)S(1)} %pad_maximum_fusion.2.refs_0_), channel_id=1, source_target_pairs={{0,48},{16,32},{32,16},{48,0},{1,49},{17,33},{33,17},{49,1},{2,50}... | collective-permute-start | bytes 393224 | tf_op jit(solution)/shard_map/ppermute | solution.py:19
  29.0 7.6 %collective-permute-done.9.refs_1_ = bf16[128,512]{1,0:T(8,128)(2,1)S(1)} collective-permute-done((bf16[128,512]{1,0:T(8,128)(2,1)S(1)}, bf16[128,512]{1,0:T(8,128)(2,1)S(1)}, u32[]{:S(2)}, u32[]{:S(2)}) %collective-permute-start.9) | collective-permute-done | bytes 131104 | tf_op jit(solution)/shard_map/ppermute | solution.py:19
  38.1 1.1 %collective-permute-start.1 = (bf16[2,4,128,128]{3,2,1,0:T(8,128)(2,1)S(1)}, bf16[2,4,128,128]{3,2,1,0:T(8,128)(2,1)S(1)}, u32[]{:S(2)}, u32[]{:S(2)}) collective-permute-start(bf16[2,4,128,128]{3,2,1,0:T(8,128)(2,1)S(1)} %fusion.1), channel_id=1, source_target_pairs={{0,32},{32,0},{1,33},{33,1},{2,34},{34,2},{3,35},{35,3},{4,36},{36... | collective-permute-start | bytes 786440 | tf_op jit(solution)/shard_map/ppermute | solution.py:19
  41.4 2.0 %collective-permute-start.22 = (bf16[512,128]{1,0:T(8,128)(2,1)S(1)}, bf16[512,128]{1,0:T(8,128)(2,1)S(1)}, u32[]{:S(2)}, u32[]{:S(2)}) collective-permute-start(bf16[512,128]{1,0:T(8,128)(2,1)S(1)} %convolution_convert_fusion), channel_id=1, source_target_pairs={{0,10},{2,8},{4,14},{6,12},{8,2},{10,0},{12,6},{14,4},{1,11},{3,9}... | collective-permute-start | bytes 393224 | tf_op jit(solution)/shard_map/ppermute | solution.py:19
  43.4 2.7 %collective-permute-start.21 = (bf16[512,128]{1,0:T(8,128)(2,1)S(1)}, bf16[512,128]{1,0:T(8,128)(2,1)S(1)}, u32[]{:S(2)}, u32[]{:S(2)}) collective-permute-start(bf16[512,128]{1,0:T(8,128)(2,1)S(1)} %convolution_convert_fusion.1), channel_id=1, source_target_pairs={{0,8},{2,10},{4,12},{6,14},{8,0},{10,2},{12,4},{14,6},{1,9},{3,11}... | collective-permute-start | bytes 393224 | tf_op jit(solution)/shard_map/ppermute | solution.py:19
  46.2 1.0 %collective-permute-start.20 = (bf16[512,128]{1,0:T(8,128)(2,1)S(1)}, bf16[512,128]{1,0:T(8,128)(2,1)S(1)}, u32[]{:S(2)}, u32[]{:S(2)}) collective-permute-start(bf16[512,128]{1,0:T(8,128)(2,1)S(1)} %convolution_convert_fusion.2), channel_id=1, source_target_pairs={{0,14},{2,12},{4,10},{6,8},{8,6},{10,4},{12,2},{14,0},{1,15},{3,13... | collective-permute-start | bytes 393224 | tf_op jit(solution)/shard_map/ppermute | solution.py:19
  48.1 1.6 %collective-permute-done.22.refs_6_ = bf16[512,128]{1,0:T(8,128)(2,1)S(1)} collective-permute-done((bf16[512,128]{1,0:T(8,128)(2,1)S(1)}, bf16[512,128]{1,0:T(8,128)(2,1)S(1)}, u32[]{:S(2)}, u32[]{:S(2)}) %collective-permute-start.22) | collective-permute-done | bytes 131104 | tf_op jit(solution)/shard_map/ppermute | solution.py:19
  49.7 1.0 %collective-permute-start.18 = (bf16[512,128]{1,0:T(8,128)(2,1)S(1)}, bf16[512,128]{1,0:T(8,128)(2,1)S(1)}, u32[]{:S(2)}, u32[]{:S(2)}) collective-permute-start(bf16[512,128]{1,0:T(8,128)(2,1)S(1)} %convolution_convert_fusion.4), channel_id=1, source_target_pairs={{0,12},{2,14},{4,8},{6,10},{8,4},{10,6},{12,0},{14,2},{1,13},{3,15... | collective-permute-start | bytes 393224 | tf_op jit(solution)/shard_map/ppermute | solution.py:19
  50.8 3.8 %collective-permute-done.21.refs_5_ = bf16[512,128]{1,0:T(8,128)(2,1)S(1)} collective-permute-done((bf16[512,128]{1,0:T(8,128)(2,1)S(1)}, bf16[512,128]{1,0:T(8,128)(2,1)S(1)}, u32[]{:S(2)}, u32[]{:S(2)}) %collective-permute-start.21) | collective-permute-done | bytes 131104 | tf_op jit(solution)/shard_map/ppermute | solution.py:19
  54.6 1.7 %collective-permute-start.16 = (bf16[512,128]{1,0:T(8,128)(2,1)S(1)}, bf16[512,128]{1,0:T(8,128)(2,1)S(1)}, u32[]{:S(2)}, u32[]{:S(2)}) collective-permute-start(bf16[512,128]{1,0:T(8,128)(2,1)S(1)} %get-tuple-element.28), channel_id=1, source_target_pairs={{0,2},{2,0},{4,6},{6,4},{8,10},{10,8},{12,14},{14,12},{1,3},{3,1},... | collective-permute-start | bytes 393224 | tf_op jit(solution)/shard_map/ppermute | solution.py:19
  56.2 2.5 %collective-permute-start.17 = (bf16[512,128]{1,0:T(8,128)(2,1)S(1)}, bf16[512,128]{1,0:T(8,128)(2,1)S(1)}, u32[]{:S(2)}, u32[]{:S(2)}) collective-permute-start(bf16[512,128]{1,0:T(8,128)(2,1)S(1)} %get-tuple-element.29), channel_id=1, source_target_pairs={{0,4},{2,6},{4,0},{6,2},{8,12},{10,14},{12,8},{14,10},{1,5},{3,7},... | collective-permute-start | bytes 393224 | tf_op jit(solution)/shard_map/ppermute | solution.py:19
  59.6 2.4 %collective-permute-done.17.refs_1_ = bf16[512,128]{1,0:T(8,128)(2,1)S(1)} collective-permute-done((bf16[512,128]{1,0:T(8,128)(2,1)S(1)}, bf16[512,128]{1,0:T(8,128)(2,1)S(1)}, u32[]{:S(2)}, u32[]{:S(2)}) %collective-permute-start.17) | collective-permute-done | bytes 131104 | tf_op jit(solution)/shard_map/ppermute | solution.py:19
  62.1 2.9 %collective-permute-start.23 = (bf16[128,512]{1,0:T(8,128)(2,1)S(1)}, bf16[128,512]{1,0:T(8,128)(2,1)S(1)}, u32[]{:S(2)}, u32[]{:S(2)}) collective-permute-start(bf16[128,512]{1,0:T(8,128)(2,1)S(1)} %summed.1.refs_0_), channel_id=1, source_target_pairs={{0,16},{16,0},{32,48},{48,32},{1,17},{17,1},{33,49},{49,33},{2,18}... | collective-permute-start | bytes 393224 | tf_op jit(solution)/shard_map/ppermute | solution.py:19
  66.0 1.2 %collective-permute-start.25 = (bf16[128,512]{1,0:T(8,128)(2,1)S(1)}, bf16[128,512]{1,0:T(8,128)(2,1)S(1)}, u32[]{:S(2)}, u32[]{:S(2)}) collective-permute-start(bf16[128,512]{1,0:T(8,128)(2,1)S(1)} %summed.1.refs_0_), channel_id=1, source_target_pairs={{0,48},{16,32},{32,16},{48,0},{1,49},{17,33},{33,17},{49,1},{2,50}... | collective-permute-start | bytes 393224 | tf_op jit(solution)/shard_map/ppermute | solution.py:19
  67.2 1.6 %collective-permute-done.23.refs_1_ = bf16[128,512]{1,0:T(8,128)(2,1)S(1)} collective-permute-done((bf16[128,512]{1,0:T(8,128)(2,1)S(1)}, bf16[128,512]{1,0:T(8,128)(2,1)S(1)}, u32[]{:S(2)}, u32[]{:S(2)}) %collective-permute-start.23) | collective-permute-done | bytes 131104 | tf_op jit(solution)/shard_map/ppermute | solution.py:19
  68.8 1.7 %collective-permute-done.24.refs_2_ = bf16[128,512]{1,0:T(8,128)(2,1)S(1)} collective-permute-done((bf16[128,512]{1,0:T(8,128)(2,1)S(1)}, bf16[128,512]{1,0:T(8,128)(2,1)S(1)}, u32[]{:S(2)}, u32[]{:S(2)}) %collective-permute-start.24) | collective-permute-done | bytes 131104 | tf_op jit(solution)/shard_map/ppermute | solution.py:19
  70.6 2.8 %collective-permute-done.25.refs_3_ = bf16[128,512]{1,0:T(8,128)(2,1)S(1)} collective-permute-done((bf16[128,512]{1,0:T(8,128)(2,1)S(1)}, bf16[128,512]{1,0:T(8,128)(2,1)S(1)}, u32[]{:S(2)}, u32[]{:S(2)}) %collective-permute-start.25) | collective-permute-done | bytes 131104 | tf_op jit(solution)/shard_map/ppermute | solution.py:19
  73.8 2.1 %collective-permute-start.27 = (bf16[128,512]{1,0:T(8,128)(2,1)S(1)}, bf16[128,512]{1,0:T(8,128)(2,1)S(1)}, u32[]{:S(2)}, u32[]{:S(2)}) collective-permute-start(bf16[128,512]{1,0:T(8,128)(2,1)S(1)} %get-tuple-element.38), channel_id=1, source_target_pairs={{0,64},{64,0},{128,192},{192,128},{1,65},{65,1},{129,193},{193,129... | collective-permute-start | bytes 393224 | tf_op jit(solution)/shard_map/ppermute | solution.py:19
  75.9 4.5 %collective-permute-start.28 = (bf16[128,512]{1,0:T(8,128)(2,1)S(1)}, bf16[128,512]{1,0:T(8,128)(2,1)S(1)}, u32[]{:S(2)}, u32[]{:S(2)}) collective-permute-start(bf16[128,512]{1,0:T(8,128)(2,1)S(1)} %get-tuple-element.39), channel_id=1, source_target_pairs={{0,128},{64,192},{128,0},{192,64},{1,129},{65,193},{129,1},{193,65... | collective-permute-start | bytes 393224 | tf_op jit(solution)/shard_map/ppermute | solution.py:19
  80.7 4.8 %collective-permute-done.27.refs_1_ = bf16[128,512]{1,0:T(8,128)(2,1)S(1)} collective-permute-done((bf16[128,512]{1,0:T(8,128)(2,1)S(1)}, bf16[128,512]{1,0:T(8,128)(2,1)S(1)}, u32[]{:S(2)}, u32[]{:S(2)}) %collective-permute-start.27) | collective-permute-done | bytes 131104 | tf_op jit(solution)/shard_map/ppermute | solution.py:19
  85.5 4.3 %collective-permute-done.28.refs_2_ = bf16[128,512]{1,0:T(8,128)(2,1)S(1)} collective-permute-done((bf16[128,512]{1,0:T(8,128)(2,1)S(1)}, bf16[128,512]{1,0:T(8,128)(2,1)S(1)}, u32[]{:S(2)}, u32[]{:S(2)}) %collective-permute-start.28) | collective-permute-done | bytes 131104 | tf_op jit(solution)/shard_map/ppermute | solution.py:19
  89.7 1.1 %collective-permute-done.29.refs_3_ = bf16[128,512]{1,0:T(8,128)(2,1)S(1)} collective-permute-done((bf16[128,512]{1,0:T(8,128)(2,1)S(1)}, bf16[128,512]{1,0:T(8,128)(2,1)S(1)}, u32[]{:S(2)}, u32[]{:S(2)}) %collective-permute-start.29) | collective-permute-done | bytes 131104 | tf_op jit(solution)/shard_map/ppermute | solution.py:19
  90.9 1.4 %mix.1 = f32[4,128,128]{2,1,0:T(8,128)} custom-call(f32[4,4]{1,0:T(4,128)S(1)} %cosine_multiply_fusion.coef, f32[128,512]{1,0:T(8,128)S(1)} %get-tuple-element.37.refs_0_, bf16[128,512]{1,0:T(8,128)(2,1)S(1)} %collective-permute-done.27.refs_1_, bf16[128,512]{1,0:T(8,128)(2,1)S(1)} %collective-permute-done.28.refs_2_, ...), custom_call_target="tpu_custom_call" | custom-call | tf_op jit(solution)/shard_map/mix/pallas_call | solution.py:189
  (69 shorter events, 11.3 us)
Async XLA Ops:
  0.8 4.0 %collective-permute-start.3 = (bf16[64,256]{1,0:T(8,128)(2,1)S(1)}, bf16[64,256]{1,0:T(8,128)(2,1)S(1)}, u32[]{:S(2)}, u32[]{:S(2)}) collective-permute-start(bf16[64,256]{1,0:T(8,128)(2,1)S(1)} %pad_maximum_fusion.4), channel_id=1, source_target_pairs={{0,2},{2,0},{1,3},{3,1},{4,6},{6,4},{5,7},{7,5},{8,10},{10,8},{9,1... | collective-permute-start | bytes 98312 | tf_op jit(solution)/shard_map/ppermute | solution.py:19
  4.8 10.2 %collective-permute-start.4 = (bf16[128,256]{1,0:T(8,128)(2,1)S(1)}, bf16[128,256]{1,0:T(8,128)(2,1)S(1)}, u32[]{:S(2)}, u32[]{:S(2)}) collective-permute-start(bf16[128,256]{1,0:T(8,128)(2,1)S(1)} %pad_maximum_fusion.3), channel_id=1, source_target_pairs={{0,4},{4,0},{1,5},{5,1},{2,6},{6,2},{3,7},{7,3},{8,12},{12,8},{9,1... | collective-permute-start | bytes 196616 | tf_op jit(solution)/shard_map/ppermute | solution.py:19
  7.2 13.4 %collective-permute-start.6 = (bf16[32,512]{1,0:T(8,128)(2,1)S(1)}, bf16[32,512]{1,0:T(8,128)(2,1)S(1)}, u32[]{:S(2)}, u32[]{:S(2)}) collective-permute-start(bf16[32,512]{1,0:T(8,128)(2,1)S(1)} %select_bitcast_fusion), channel_id=1, source_target_pairs={{0,64},{64,0},{128,192},{192,128},{1,65},{65,1},{129,193},{193,129... | collective-permute-start | bytes 98312 | tf_op jit(solution)/shard_map/ppermute | solution.py:19
  10.5 13.2 %collective-permute-start.7 = (bf16[32,512]{1,0:T(8,128)(2,1)S(1)}, bf16[32,512]{1,0:T(8,128)(2,1)S(1)}, u32[]{:S(2)}, u32[]{:S(2)}) collective-permute-start(bf16[32,512]{1,0:T(8,128)(2,1)S(1)} %select_bitcast_fusion), channel_id=1, source_target_pairs={{0,128},{64,192},{128,0},{192,64},{1,129},{65,193},{129,1},{193,65... | collective-permute-start | bytes 98312 | tf_op jit(solution)/shard_map/ppermute | solution.py:19
  15.0 8.7 %collective-permute-start.8 = (bf16[32,512]{1,0:T(8,128)(2,1)S(1)}, bf16[32,512]{1,0:T(8,128)(2,1)S(1)}, u32[]{:S(2)}, u32[]{:S(2)}) collective-permute-start(bf16[32,512]{1,0:T(8,128)(2,1)S(1)} %select_bitcast_fusion), channel_id=1, source_target_pairs={{0,192},{64,128},{128,64},{192,0},{1,193},{65,129},{129,65},{193,1... | collective-permute-start | bytes 98312 | tf_op jit(solution)/shard_map/ppermute | solution.py:19
  15.1 10.2 %collective-permute-start.5 = (bf16[256,256]{1,0:T(8,128)(2,1)S(1)}, bf16[256,256]{1,0:T(8,128)(2,1)S(1)}, u32[]{:S(2)}, u32[]{:S(2)}) collective-permute-start(bf16[256,256]{1,0:T(8,128)(2,1)S(1)} %pad_maximum_fusion.1), channel_id=1, source_target_pairs={{0,12},{4,8},{8,4},{12,0},{1,13},{5,9},{9,5},{13,1},{2,14},{6,10},... | collective-permute-start | bytes 393224 | tf_op jit(solution)/shard_map/ppermute | solution.py:19
  17.3 11.5 %collective-permute-start.2 = (f32[2]{0:T(128)}, f32[2]{0:T(128)S(1)}, u32[]{:S(2)}, u32[]{:S(2)}) collective-permute-start(f32[2]{0:T(128)} %mine.1), channel_id=1, source_target_pairs={{0,1},{1,0},{2,3},{3,2},{4,5},{5,4},{6,7},{7,6},{8,9},{9,8},{10,11... | collective-permute-start | bytes 32 | tf_op jit(solution)/shard_map/ppermute | solution.py:228
  20.6 17.4 %collective-permute-start = (bf16[8,128,128]{2,1,0:T(8,128)(2,1)S(1)}, bf16[8,128,128]{2,1,0:T(8,128)(2,1)S(1)}, u32[]{:S(2)}, u32[]{:S(2)}) collective-permute-start(bf16[8,128,128]{2,1,0:T(8,128)(2,1)S(1)} %get-tuple-element.24), channel_id=1, source_target_pairs={{0,16},{16,0},{1,17},{17,1},{2,18},{18,2},{3,19},{19,3},{4,20},{20... | collective-permute-start | bytes 786440 | tf_op jit(solution)/shard_map/ppermute | solution.py:19
  23.7 12.8 %collective-permute-start.9 = (bf16[128,512]{1,0:T(8,128)(2,1)S(1)}, bf16[128,512]{1,0:T(8,128)(2,1)S(1)}, u32[]{:S(2)}, u32[]{:S(2)}) collective-permute-start(bf16[128,512]{1,0:T(8,128)(2,1)S(1)} %pad_maximum_fusion.2.refs_0_), channel_id=1, source_target_pairs={{0,16},{16,0},{32,48},{48,32},{1,17},{17,1},{33,49},{49,33},{2,18}... | collective-permute-start | bytes 393224 | tf_op jit(solution)/shard_map/ppermute | solution.py:19
  24.3 12.2 %collective-permute-start.10 = (bf16[128,512]{1,0:T(8,128)(2,1)S(1)}, bf16[128,512]{1,0:T(8,128)(2,1)S(1)}, u32[]{:S(2)}, u32[]{:S(2)}) collective-permute-start(bf16[128,512]{1,0:T(8,128)(2,1)S(1)} %pad_maximum_fusion.2.refs_0_), channel_id=1, source_target_pairs={{0,32},{16,48},{32,0},{48,16},{1,33},{17,49},{33,1},{49,17},{2,34}... | collective-permute-start | bytes 393224 | tf_op jit(solution)/shard_map/ppermute | solution.py:19
  25.3 11.7 %collective-permute-start.11 = (bf16[128,512]{1,0:T(8,128)(2,1)S(1)}, bf16[128,512]{1,0:T(8,128)(2,1)S(1)}, u32[]{:S(2)}, u32[]{:S(2)}) collective-permute-start(bf16[128,512]{1,0:T(8,128)(2,1)S(1)} %pad_maximum_fusion.2.refs_0_), channel_id=1, source_target_pairs={{0,48},{16,32},{32,16},{48,0},{1,49},{17,33},{33,17},{49,1},{2,50}... | collective-permute-start | bytes 393224 | tf_op jit(solution)/shard_map/ppermute | solution.py:19
  28.9 10.3 %collective-permute-start.12 = (bf16[128,512]{1,0:T(8,128)(2,1)S(1)}, bf16[128,512]{1,0:T(8,128)(2,1)S(1)}, u32[]{:S(2)}, u32[]{:S(2)}) collective-permute-start(bf16[128,512]{1,0:T(8,128)(2,1)S(1)} %pad_maximum_fusion.2.refs_0_), channel_id=1, source_target_pairs={{0,1},{1,0},{2,3},{3,2},{4,5},{5,4},{6,7},{7,6},{8,9},{9,8},{10,11... | collective-permute-start | bytes 393224 | tf_op jit(solution)/shard_map/ppermute | solution.py:221
  36.5 2.7 %collective-permute-start.13 = (bf16[128,512]{1,0:T(8,128)(2,1)S(1)}, bf16[128,512]{1,0:T(8,128)(2,1)S(1)}, u32[]{:S(2)}, u32[]{:S(2)}) collective-permute-start(bf16[128,512]{1,0:T(8,128)(2,1)S(1)} %collective-permute-done.9.refs_1_), channel_id=1, source_target_pairs={{0,1},{1,0},{2,3},{3,2},{4,5},{5,4},{6,7},{7,6},{8,9},{9,8},{10,11... | collective-permute-start | bytes 393224 | tf_op jit(solution)/shard_map/ppermute | solution.py:221
  36.5 2.7 %collective-permute-start.14 = (bf16[128,512]{1,0:T(8,128)(2,1)S(1)}, bf16[128,512]{1,0:T(8,128)(2,1)S(1)}, u32[]{:S(2)}, u32[]{:S(2)}) collective-permute-start(bf16[128,512]{1,0:T(8,128)(2,1)S(1)} %collective-permute-done.10.refs_2_), channel_id=1, source_target_pairs={{0,1},{1,0},{2,3},{3,2},{4,5},{5,4},{6,7},{7,6},{8,9},{9,8},{10,11... | collective-permute-start | bytes 393224 | tf_op jit(solution)/shard_map/ppermute | solution.py:221
  37.0 2.2 %collective-permute-start.15 = (bf16[128,512]{1,0:T(8,128)(2,1)S(1)}, bf16[128,512]{1,0:T(8,128)(2,1)S(1)}, u32[]{:S(2)}, u32[]{:S(2)}) collective-permute-start(bf16[128,512]{1,0:T(8,128)(2,1)S(1)} %collective-permute-done.11.refs_3_), channel_id=1, source_target_pairs={{0,1},{1,0},{2,3},{3,2},{4,5},{5,4},{6,7},{7,6},{8,9},{9,8},{10,11... | collective-permute-start | bytes 393224 | tf_op jit(solution)/shard_map/ppermute | solution.py:221
  38.1 29.1 %collective-permute-start.1 = (bf16[2,4,128,128]{3,2,1,0:T(8,128)(2,1)S(1)}, bf16[2,4,128,128]{3,2,1,0:T(8,128)(2,1)S(1)}, u32[]{:S(2)}, u32[]{:S(2)}) collective-permute-start(bf16[2,4,128,128]{3,2,1,0:T(8,128)(2,1)S(1)} %fusion.1), channel_id=1, source_target_pairs={{0,32},{32,0},{1,33},{33,1},{2,34},{34,2},{3,35},{35,3},{4,36},{36... | collective-permute-start | bytes 786440 | tf_op jit(solution)/shard_map/ppermute | solution.py:19
  41.1 26.1 %copy-start.5 = (f32[2]{0:T(128)S(1)}, f32[2]{0:T(128)}, u32[]{:S(2)}) copy-start(f32[2]{0:T(128)} %param.18) | copy-start | bytes 28
  41.4 39.2 %copy-start.6 = (f32[4]{0:T(128)S(1)}, f32[4]{0:T(128)}, u32[]{:S(2)}) copy-start(f32[4]{0:T(128)} %param.19) | copy-start | bytes 52
  41.4 8.3 %collective-permute-start.22 = (bf16[512,128]{1,0:T(8,128)(2,1)S(1)}, bf16[512,128]{1,0:T(8,128)(2,1)S(1)}, u32[]{:S(2)}, u32[]{:S(2)}) collective-permute-start(bf16[512,128]{1,0:T(8,128)(2,1)S(1)} %convolution_convert_fusion), channel_id=1, source_target_pairs={{0,10},{2,8},{4,14},{6,12},{8,2},{10,0},{12,6},{14,4},{1,11},{3,9}... | collective-permute-start | bytes 393224 | tf_op jit(solution)/shard_map/ppermute | solution.py:19
  43.4 11.1 %collective-permute-start.21 = (bf16[512,128]{1,0:T(8,128)(2,1)S(1)}, bf16[512,128]{1,0:T(8,128)(2,1)S(1)}, u32[]{:S(2)}, u32[]{:S(2)}) collective-permute-start(bf16[512,128]{1,0:T(8,128)(2,1)S(1)} %convolution_convert_fusion.1), channel_id=1, source_target_pairs={{0,8},{2,10},{4,12},{6,14},{8,0},{10,2},{12,4},{14,6},{1,9},{3,11}... | collective-permute-start | bytes 393224 | tf_op jit(solution)/shard_map/ppermute | solution.py:19
  46.2 10.1 %collective-permute-start.20 = (bf16[512,128]{1,0:T(8,128)(2,1)S(1)}, bf16[512,128]{1,0:T(8,128)(2,1)S(1)}, u32[]{:S(2)}, u32[]{:S(2)}) collective-permute-start(bf16[512,128]{1,0:T(8,128)(2,1)S(1)} %convolution_convert_fusion.2), channel_id=1, source_target_pairs={{0,14},{2,12},{4,10},{6,8},{8,6},{10,4},{12,2},{14,0},{1,15},{3,13... | collective-permute-start | bytes 393224 | tf_op jit(solution)/shard_map/ppermute | solution.py:19
  47.2 11.8 %collective-permute-start.19 = (bf16[512,128]{1,0:T(8,128)(2,1)S(1)}, bf16[512,128]{1,0:T(8,128)(2,1)S(1)}, u32[]{:S(2)}, u32[]{:S(2)}) collective-permute-start(bf16[512,128]{1,0:T(8,128)(2,1)S(1)} %convolution_convert_fusion.3), channel_id=1, source_target_pairs={{0,6},{2,4},{4,2},{6,0},{8,14},{10,12},{12,10},{14,8},{1,7},{3,5},... | collective-permute-start | bytes 393224 | tf_op jit(solution)/shard_map/ppermute | solution.py:19
  49.7 9.3 %collective-permute-start.18 = (bf16[512,128]{1,0:T(8,128)(2,1)S(1)}, bf16[512,128]{1,0:T(8,128)(2,1)S(1)}, u32[]{:S(2)}, u32[]{:S(2)}) collective-permute-start(bf16[512,128]{1,0:T(8,128)(2,1)S(1)} %convolution_convert_fusion.4), channel_id=1, source_target_pairs={{0,12},{2,14},{4,8},{6,10},{8,4},{10,6},{12,0},{14,2},{1,13},{3,15... | collective-permute-start | bytes 393224 | tf_op jit(solution)/shard_map/ppermute | solution.py:19
  54.6 5.0 %collective-permute-start.16 = (bf16[512,128]{1,0:T(8,128)(2,1)S(1)}, bf16[512,128]{1,0:T(8,128)(2,1)S(1)}, u32[]{:S(2)}, u32[]{:S(2)}) collective-permute-start(bf16[512,128]{1,0:T(8,128)(2,1)S(1)} %get-tuple-element.28), channel_id=1, source_target_pairs={{0,2},{2,0},{4,6},{6,4},{8,10},{10,8},{12,14},{14,12},{1,3},{3,1},... | collective-permute-start | bytes 393224 | tf_op jit(solution)/shard_map/ppermute | solution.py:19
  56.2 5.8 %collective-permute-start.17 = (bf16[512,128]{1,0:T(8,128)(2,1)S(1)}, bf16[512,128]{1,0:T(8,128)(2,1)S(1)}, u32[]{:S(2)}, u32[]{:S(2)}) collective-permute-start(bf16[512,128]{1,0:T(8,128)(2,1)S(1)} %get-tuple-element.29), channel_id=1, source_target_pairs={{0,4},{2,6},{4,0},{6,2},{8,12},{10,14},{12,8},{14,10},{1,5},{3,7},... | collective-permute-start | bytes 393224 | tf_op jit(solution)/shard_map/ppermute | solution.py:19
  62.1 6.7 %collective-permute-start.23 = (bf16[128,512]{1,0:T(8,128)(2,1)S(1)}, bf16[128,512]{1,0:T(8,128)(2,1)S(1)}, u32[]{:S(2)}, u32[]{:S(2)}) collective-permute-start(bf16[128,512]{1,0:T(8,128)(2,1)S(1)} %summed.1.refs_0_), channel_id=1, source_target_pairs={{0,16},{16,0},{32,48},{48,32},{1,17},{17,1},{33,49},{49,33},{2,18}... | collective-permute-start | bytes 393224 | tf_op jit(solution)/shard_map/ppermute | solution.py:19
  65.0 5.6 %collective-permute-start.24 = (bf16[128,512]{1,0:T(8,128)(2,1)S(1)}, bf16[128,512]{1,0:T(8,128)(2,1)S(1)}, u32[]{:S(2)}, u32[]{:S(2)}) collective-permute-start(bf16[128,512]{1,0:T(8,128)(2,1)S(1)} %summed.1.refs_0_), channel_id=1, source_target_pairs={{0,32},{16,48},{32,0},{48,16},{1,33},{17,49},{33,1},{49,17},{2,34}... | collective-permute-start | bytes 393224 | tf_op jit(solution)/shard_map/ppermute | solution.py:19
  66.0 7.4 %collective-permute-start.25 = (bf16[128,512]{1,0:T(8,128)(2,1)S(1)}, bf16[128,512]{1,0:T(8,128)(2,1)S(1)}, u32[]{:S(2)}, u32[]{:S(2)}) collective-permute-start(bf16[128,512]{1,0:T(8,128)(2,1)S(1)} %summed.1.refs_0_), channel_id=1, source_target_pairs={{0,48},{16,32},{32,16},{48,0},{1,49},{17,33},{33,17},{49,1},{2,50}... | collective-permute-start | bytes 393224 | tf_op jit(solution)/shard_map/ppermute | solution.py:19
  67.2 13.2 %collective-permute-start.26 = (f32[2]{0:T(128)S(1)}, f32[2]{0:T(128)S(1)}, u32[]{:S(2)}, u32[]{:S(2)}) collective-permute-start(f32[2]{0:T(128)S(1)} %copy-done.5), channel_id=1, source_target_pairs={{0,1},{1,0},{2,3},{3,2},{4,5},{5,4},{6,7},{7,6},{8,9},{9,8},{10,11... | collective-permute-start | bytes 32 | tf_op jit(solution)/shard_map/ppermute | solution.py:229
  73.8 11.6 %collective-permute-start.27 = (bf16[128,512]{1,0:T(8,128)(2,1)S(1)}, bf16[128,512]{1,0:T(8,128)(2,1)S(1)}, u32[]{:S(2)}, u32[]{:S(2)}) collective-permute-start(bf16[128,512]{1,0:T(8,128)(2,1)S(1)} %get-tuple-element.38), channel_id=1, source_target_pairs={{0,64},{64,0},{128,192},{192,128},{1,65},{65,1},{129,193},{193,129... | collective-permute-start | bytes 393224 | tf_op jit(solution)/shard_map/ppermute | solution.py:19
  75.9 13.8 %collective-permute-start.28 = (bf16[128,512]{1,0:T(8,128)(2,1)S(1)}, bf16[128,512]{1,0:T(8,128)(2,1)S(1)}, u32[]{:S(2)}, u32[]{:S(2)}) collective-permute-start(bf16[128,512]{1,0:T(8,128)(2,1)S(1)} %get-tuple-element.39), channel_id=1, source_target_pairs={{0,128},{64,192},{128,0},{192,64},{1,129},{65,193},{129,1},{193,65... | collective-permute-start | bytes 393224 | tf_op jit(solution)/shard_map/ppermute | solution.py:19
  80.4 10.5 %collective-permute-start.29 = (bf16[128,512]{1,0:T(8,128)(2,1)S(1)}, bf16[128,512]{1,0:T(8,128)(2,1)S(1)}, u32[]{:S(2)}, u32[]{:S(2)}) collective-permute-start(bf16[128,512]{1,0:T(8,128)(2,1)S(1)} %get-tuple-element.40), channel_id=1, source_target_pairs={{0,192},{64,128},{128,64},{192,0},{1,193},{65,129},{129,65},{193,1... | collective-permute-start | bytes 393224 | tf_op jit(solution)/shard_map/ppermute | solution.py:19
  (5 other events, 69.0 us)
